TPU v7x, 32 devices: a whole 2x2x4 slice. The times are simulated.
32 devices in a mesh: space: 16 (over z, x, core), bead: 2 (over y).
Axes of the slice: x: 2, y: 2, z: 4, core: 2. Of those that a mesh axis runs over, the one named last changes fastest.
Arguments:
- positions: float32 [32, 3, 65536], P('bead', None, 'space'), may hold values from -5 to 5
- momenta: float32 [32, 3, 65536], P('bead', None, 'space'), may hold values from -12 to 12
- masses: float32 [65536], P('space'), may hold values from 1 to 16
- strengths: float32 [65536], P('space'), may hold values from 0.5 to 2
- bond_ends: int32 [2, 65536], P(None, 'space'), may hold values from 0 to 127
- angle_ends: int32 [3, 32768], P(None, 'space'), may hold values from 0 to 127
- neighbour_tiles: int32 [3, 512], P(None, 'space'), may hold values from 0 to 511, as said below
Outputs:
- new_positions: float32 [32, 3, 65536], P('bead', None, 'space')
- new_momenta: float32 [32, 3, 65536], P('bead', None, 'space')
Inputs may be any that keep to these rules, and one draw needn't show every extreme that they name: `bond_ends`: entry [e, b] is the place within tile b // 128 of end e of bond b. `angle_ends`: entry [e, b] is the place within tile b // 64 of atom e of angle b. `neighbour_tiles`: column t names 3 different tiles, each within 2 tiles of t, counting around the ends (tile 512 - 1 lies next to tile 0).
All inputs are finite; a program needn't handle non-finite values.
Results may differ from a plain program's by a relative error of at most 0.0003.
Values sent between devices are 32-bit elements; how exact they have to be, the bound alone decides.
No kernel may reach another device: no remote copies, remote signals or barrier semaphores. Data moves between devices by JAX's collectives and lax.ppermute only.
A program may use at most 64 MiB of HBM per device.

v0:
```python
import functools
import math

import jax
import jax.numpy as jnp
import numpy as np
from jax import lax
from jax.experimental import pallas as pl
from jax.experimental.pallas import tpu as pltpu
from jax.sharding import PartitionSpec as P


BEADS = 32
KEPT = 4
SUBS = 3
TILE = 128
GT = 2
BPT = 128
APT = 64
ROWS = 4 * KEPT

time_step = 0.3
spring_freq = 80.0
bond_stiff = 0.2
bond_rest = 1.0
angle_stiff = 0.1
angle_rest = 0.5
range_sq = 4.0
HIGH = lax.Precision.HIGHEST
IN_VMEM = pl.BlockSpec(memory_space=pltpu.VMEM)
IN_SMEM = pl.BlockSpec(memory_space=pltpu.SMEM)
IN_SPACE = pltpu.MemorySpace.VMEM


def near(x):
    return pltpu.with_memory_space_constraint(x, IN_SPACE)


def vmem_out(shape, dtype):
    return IN_SPACE(shape, dtype)


COST = pl.CostEstimate(flops=10_000_000, bytes_accessed=100_000, transcendentals=0)
F32 = jnp.float32
BF16 = jnp.bfloat16


def mode_table(number):
    within = np.arange(number)
    result = np.zeros((number, number))
    for column in range(number):
        if column == 0:
            result[:, column] = 1.0 / math.sqrt(number)
        elif 2 * column < number:
            result[:, column] = math.sqrt(2.0 / number) * np.cos(
                2 * np.pi * within * column / number
            )
        elif 2 * column == number:
            result[:, column] = (-1.0) ** within / math.sqrt(number)
        else:
            result[:, column] = math.sqrt(2.0 / number) * np.sin(
                2 * np.pi * within * column / number
            )
    return result


def contract_table(number, kept):
    larger = mode_table(number)
    smaller = mode_table(kept)
    chosen = [column if 2 * column <= kept else number - kept + column for column in range(kept)]
    return math.sqrt(kept / number) * smaller @ larger[:, chosen].T


def motion_table(number, interval):
    freqs = 2.0 * spring_freq * np.sin(np.pi * np.arange(number) / number)
    modes = mode_table(number)
    safe = np.where(freqs > 0, freqs, 1.0)
    gains = np.where(freqs > 0, np.sin(freqs * interval) / safe, interval)
    drags = freqs * np.sin(freqs * interval)
    stay = modes @ np.diag(np.cos(freqs * interval)) @ modes.T
    gain = modes @ np.diag(gains) @ modes.T
    drag = modes @ np.diag(drags) @ modes.T
    return np.block([[stay, gain], [-drag, stay]])


def np_split(table, parts):
    out, rest = [], np.asarray(table, np.float64)
    for _ in range(parts):
        piece = rest.astype(np.float32).astype(jnp.bfloat16)
        out.append(piece)
        rest = rest - piece.astype(np.float64)
    return out


def stacked_left(table, parts=3):
    pieces = np_split(table, parts)
    zero = np.zeros_like(pieces[0])
    return np.concatenate(
        [
            np.concatenate([pieces[i]] * (parts - i) + [zero] * i, axis=1)
            for i in range(parts)
        ],
        axis=0,
    )


def split(x, parts):
    out = []
    for i in range(parts):
        piece = x.astype(BF16)
        out.append(piece)
        if i < parts - 1:
            x = x - piece.astype(F32)
    return out


def mm(left, right):
    return jnp.dot(left, right, preferred_element_type=F32)


def exact(left, x, parts=3):
    out = mm(left, jnp.concatenate(split(x, parts), axis=0))
    rows = out.shape[0] // parts
    total = out[:rows]
    for i in range(1, parts):
        total = total + out[i * rows : (i + 1) * rows]
    return total


def contract_rows(beads):
    table = contract_table(BEADS, KEPT)
    tables = []
    for turn in range(0, BEADS, beads):
        order = (np.arange(BEADS) + turn) % BEADS
        tables.append(table[:, order])
    return tables


def contract_left(table):
    out = np.zeros((ROWS, 3 * table.shape[1]))
    for c in range(KEPT):
        for k in range(3):
            out[4 * c + 1 + k, k * table.shape[1] : (k + 1) * table.shape[1]] = table[c]
    return out


def expand_left(table):
    return BEADS / KEPT * contract_left(table).T


def begin_kernel(pair, chunks, bead, left, strengths, pos, mom, *outs):
    comps, _, lanes = pos.shape
    step = pl.program_id(0)
    whole = outs[-1]
    x = jnp.concatenate([pos[c] for c in range(comps)], axis=0)
    c16 = exact(left[bead[0]], x)
    logs = math.log2(math.e) * jnp.log(strengths[...])
    logs = jnp.concatenate([logs[t : t + 1] for t in range(lanes // TILE)], axis=1)
    row = lax.broadcasted_iota(jnp.int32, (ROWS, lanes), 0)
    c16 = jnp.where(row == 0, logs, c16)
    whole[:, pl.ds(pl.multiple_of(step * lanes, TILE), lanes)] = c16
    if not pair:
        return
    mine, theirs, straight, across = outs[:4]
    targets = outs[4:-1]
    for i in range(2 * chunks):
        owner, chunk = divmod(i, chunks)

        def put(target):
            target[:3] = pos[...]
            target[3:] = mom[...]

        pl.when((step == i) & (bead[0] == owner))(functools.partial(put, targets[chunk]))
        pl.when((step == i) & (bead[0] != owner))(functools.partial(put, targets[chunks + chunk]))

    slab = whole.shape[1]
    block, rim = slab // 2, GT * TILE
    size = block + rim

    def sides(which):
        first, other = (0, block - rim) if which == 0 else (block - rim, 0)
        mine[...] = whole[:, first : first + size]
        theirs[...] = whole[:, other : other + size]
        head, tail = whole[:, :rim], whole[:, slab - rim :]
        straight[...] = tail if which == 0 else head
        across[...] = head if which == 0 else tail

    for which in range(2):
        pl.when((step == 2 * chunks - 1) & (bead[0] == which))(functools.partial(sides, which))


def begin(pair, chunks, bead, left, strengths, pos, mom):
    beads, slab = pos.shape[1:]
    if pair:
        block, rim = slab // 2, GT * TILE
        lanes = block // chunks
        shapes = [(ROWS, block + rim)] * 2 + [(ROWS, rim)] * 2
        shapes += [(6, beads, lanes)] * (2 * chunks)
        scratch = [pltpu.VMEM((ROWS, slab), F32)]
    else:
        lanes = math.gcd(slab, 1024)
        shapes, scratch = [(ROWS, slab)], []
    return pl.pallas_call(
        functools.partial(begin_kernel, pair, chunks),
        grid=(slab // lanes,),
        in_specs=[
            IN_SMEM,
            IN_VMEM,
            pl.BlockSpec((lanes // TILE, TILE), lambda i: (i, 0)),
            pl.BlockSpec((3, beads, lanes), lambda i: (0, 0, i)),
            pl.BlockSpec((3, beads, lanes), lambda i: (0, 0, i)),
        ],
        out_specs=[IN_VMEM] * len(shapes),
        scratch_shapes=scratch,
        out_shape=[vmem_out(s, F32) for s in shapes],
        cost_estimate=COST,
        name="begin",
    )(bead, left, strengths, pos, mom)


def prepare_kernel(group, bead, bonds, angles, ends, hot):
    lane = lax.broadcasted_iota(jnp.int32, (1, TILE), 1)
    atom = lax.broadcasted_iota(jnp.int32, (TILE, 2 * TILE), 0)
    low = lane < APT

    def merge(first, second, odd):
        a = pltpu.roll(first, APT, 1) if odd else first
        b = second if odd else pltpu.roll(second, APT, 1)
        return jnp.where(low, a, b)

    def tiles(i, carry):
        at = (bead[0] * (hot.shape[0] // group) + i) * group
        bond_rows = bonds[:, pl.ds(pl.multiple_of(at * BPT, BPT), group * BPT)]
        angle_rows = angles[:, pl.ds(pl.multiple_of(at * APT, TILE), group * APT)]
        for t in range(group):
            one = bond_rows[0:1, t * TILE : (t + 1) * TILE]
            other = bond_rows[1:2, t * TILE : (t + 1) * TILE]
            odd = t % 2
            window = slice((t // 2) * TILE, (t // 2 + 1) * TILE)
            first, middle, last = [angle_rows[e : e + 1, window] for e in range(3)]
            outer = merge(first, last, odd)
            opposite = merge(last, first, odd)
            centre = merge(middle, middle, odd)
            ends[i * group + t] = jnp.concatenate([one, other, outer, centre], axis=0)
            gains = jnp.concatenate([other, centre], axis=1)
            losses = jnp.concatenate([one, opposite], axis=1)
            table = (atom == gains).astype(F32) - (atom == losses).astype(F32)
            hot[i * group + t] = table.astype(BF16)
        return carry

    lax.fori_loop(0, hot.shape[0] // group, tiles, 0)


def prepare(bead, bond_ends, angle_ends, block_tiles):
    return pl.pallas_call(
        functools.partial(prepare_kernel, math.gcd(block_tiles, 4)),
        in_specs=[IN_SMEM, IN_VMEM, IN_VMEM],
        out_specs=[IN_VMEM] * 2,
        out_shape=[
            vmem_out((block_tiles, 4, TILE), jnp.int32),
            vmem_out((block_tiles, TILE, 2 * TILE), BF16),
        ],
        cost_estimate=COST,
        name="prepare",
    )(bead, bond_ends, angle_ends)


def pair_kernel(spots, seg_sizes, own_count, bead, space, nbr, *refs):
    total = sum(n for _, n in seg_sizes)
    count = sum(n for n, _ in seg_sizes)
    seg_refs = refs[:count]
    out, feat_i, feat_m, feat_p, base, weights_a, weights_b = refs[count:]
    column, own_spot, spot = spots((bead[0], space[0]))
    row = lax.broadcasted_iota(jnp.int32, (ROWS, TILE), 0)
    slot = row % 4
    scale = math.sqrt(2.0 * math.log2(math.e) / range_sq)
    same = (
        lax.broadcasted_iota(jnp.int32, (ROWS, ROWS), 0) // 4
        == lax.broadcasted_iota(jnp.int32, (ROWS, ROWS), 1) // 4
    ).astype(F32)

    def features(tile, c16):
        base[tile] = c16
        logs = c16[0:1]
        place = jnp.where(slot == 0, 0.0, c16)
        scaled = place * scale
        high, low = [piece.astype(F32) for piece in split(scaled, 2)]
        square = jnp.dot(same, scaled * scaled, precision=HIGH, preferred_element_type=F32)
        half = -0.5 * square

        def three(x):
            a, b, c = [piece.astype(F32) for piece in split(x, 3)]
            return jnp.where(slot == 0, a, jnp.where(slot == 1, b, jnp.where(slot == 2, c, 0.0)))

        ones = jnp.where(slot == 3, 0.0, 1.0)
        mine = jnp.concatenate([high, high, low, low, three(half), ones], axis=0)
        theirs = jnp.concatenate(
            [high, low, high, low, ones, three(half + logs), ones, ones], axis=0
        )
        feat_i[tile] = mine.astype(BF16)
        feat_m[tile] = jnp.transpose(theirs, (1, 0)).astype(BF16)
        one = jnp.ones((ROWS, TILE), F32)
        p_high, p_low = [piece.astype(F32) for piece in split(place, 2)]
        feat_p[tile] = jnp.concatenate([one, p_high, p_low], axis=0).astype(BF16)

    tile = 0
    at = 0
    for number, tiles in seg_sizes:
        group = seg_refs[at : at + number]
        at += number
        for i in range(tiles):
            lanes = slice(i * TILE, (i + 1) * TILE)
            c16 = group[0][:, lanes] if len(group[0].shape) == 2 else group[0][6, :, lanes]
            for other in group[1:]:
                more = other[:, i * TILE : (i + 1) * TILE]
                c16 = c16 + jnp.where(row == 0, 0.0, more)
            features(tile, c16)
            tile += 1
    assert tile == total

    groups = 6
    wide_row = lax.broadcasted_iota(jnp.int32, (groups * ROWS, TILE), 0)
    pick = [((wide_row % ROWS) // 4 == c).astype(BF16) for c in range(KEPT)]
    owner = row // 4

    def close(t, u):
        return spot(nbr[u, column + t])

    def weigh(t, weights):
        features_i = feat_i[own_spot(t)]
        right = jnp.concatenate([features_i * pick[c] for c in range(KEPT)], axis=1)
        right = jnp.concatenate([right, jnp.zeros((2 * ROWS, KEPT * TILE), BF16)], axis=0)
        left = jnp.concatenate([feat_m[close(t, u)] for u in range(3)], axis=0)
        power = mm(left, right)
        for u in range(3):
            high, low = split(jnp.exp2(power[u * TILE : (u + 1) * TILE]), 2)
            weights[2 * u * TILE : (2 * u + 1) * TILE] = high
            weights[(2 * u + 1) * TILE : (2 * u + 2) * TILE] = low

    def pull(t, weights):
        left = []
        for u in range(3):
            piece = feat_p[close(t, u)]
            left += [piece, piece]
        total_p = mm(jnp.concatenate(left, axis=1), weights[...])
        sums = total_p[:ROWS]
        pulls = total_p[ROWS : 2 * ROWS] + total_p[2 * ROWS :]
        c16 = base[own_spot(t)]
        factor = (2.0 / range_sq) * jnp.exp2(c16[0:1])
        result = jnp.zeros((ROWS, TILE), F32)
        for c in range(KEPT):
            lanes = slice(c * TILE, (c + 1) * TILE)
            force = factor * (c16 * sums[:, lanes] - pulls[:, lanes])
            result = jnp.where((owner == c) & (slot > 0), force, result)
        out[:, pl.ds(pl.multiple_of(t * TILE, TILE), TILE)] = result

    weigh(0, weights_a)

    def two_tiles(i, carry):
        t = 2 * i
        weigh(t + 1, weights_b)
        pull(t, weights_a)
        weigh(jnp.minimum(t + 2, own_count - 1), weights_a)
        pull(t + 1, weights_b)
        return carry

    lax.fori_loop(0, own_count // 2, two_tiles, 0)


def pair_forces(spots, segments, own_count, bead, space, neighbour_tiles):
    sizes = tuple((len(group), group[0].shape[-1] // TILE) for group in segments)
    total = sum(n for _, n in sizes)
    assert own_count % 2 == 0
    flat = [array for group in segments for array in group]
    return pl.pallas_call(
        functools.partial(pair_kernel, spots, sizes, own_count),
        in_specs=[IN_SMEM] * 3 + [IN_VMEM] * len(flat),
        out_specs=IN_VMEM,
        out_shape=vmem_out((ROWS, own_count * TILE), F32),
        scratch_shapes=[
            pltpu.VMEM((total, 6 * ROWS, TILE), BF16),
            pltpu.VMEM((total, TILE, 8 * ROWS), BF16),
            pltpu.VMEM((total, 3 * ROWS, TILE), BF16),
            pltpu.VMEM((total, ROWS, TILE), F32),
            pltpu.VMEM((6 * TILE, KEPT * TILE), BF16),
            pltpu.VMEM((6 * TILE, KEPT * TILE), BF16),
        ],
        cost_estimate=COST,
        name="pair_forces",
    )(bead, space, neighbour_tiles, *[near(x) for x in flat])


def step_kernel(parts, chunk, chunks, group, edge, bead, *refs):
    pieces = refs[:parts]
    force, mass_rows, strength_rows, ends, hot, motion, expand, contract = refs[parts : parts + 8]
    before = refs[parts + 8] if edge and chunk else None
    outs = refs[len(refs) - parts - 1 - edge :]
    c_out = outs[parts]
    interval = time_step / SUBS
    width = group * TILE
    first = chunk * group
    motion_l = motion[...]

    def per_atom(rows):
        at = (bead[0] * chunks + chunk) * group
        return jnp.concatenate([rows[pl.ds(at + t, 1), :] for t in range(group)], axis=1)

    masses = per_atom(mass_rows)
    inverse = 1.0 / masses

    def gathered(plane):
        if parts == 1:
            return pieces[0][plane]
        return jnp.concatenate([piece[plane] for piece in pieces], axis=0)

    q = [gathered(c) for c in range(3)]
    p = [gathered(3 + c) for c in range(3)]
    kick = exact(expand[bead[0]], force[:, first * TILE : first * TILE + width])
    v = [
        (p[c] + 0.5 * time_step * kick[c * BEADS : (c + 1) * BEADS]) * inverse for c in range(3)
    ]
    places = []
    for t in range(group):
        places.append([jnp.broadcast_to(ends[first + t, e : e + 1], (3 * BEADS, TILE)) for e in range(4)])

    def take(x, index):
        return jnp.take_along_axis(x, index, axis=1, mode="promise_in_bounds")

    def bonded(q):
        forces = []
        for t in range(group):
            lanes = slice(t * TILE, (t + 1) * TILE)
            rows = jnp.concatenate([q[c][:, lanes] for c in range(3)], axis=0)
            one, other, outer, centre = places[t]
            stretch = take(rows, one) - take(rows, other)
            arms = take(rows, outer) - take(rows, centre)
            s = [stretch[c * BEADS : (c + 1) * BEADS] for c in range(3)]
            a = [arms[c * BEADS : (c + 1) * BEADS] for c in range(3)]
            length = s[0] * s[0] + s[1] * s[1] + s[2] * s[2]
            g = bond_stiff * (length - bond_rest)
            turned = [pltpu.roll(x, APT, 1) for x in a]
            inner = a[0] * turned[0] + a[1] * turned[1] + a[2] * turned[2]
            h = angle_stiff * (inner - angle_rest)
            bonds = jnp.concatenate([g * x for x in s], axis=0)
            angles = jnp.concatenate([h * x for x in a], axis=0)
            both = jnp.concatenate([bonds, angles], axis=1)
            out = lax.dot_general(
                jnp.concatenate(split(both, 2), axis=0),
                hot[first + t],
                (((1,), (1,)), ((), ())),
                preferred_element_type=F32,
            )
            forces.append(out[: 3 * BEADS] + out[3 * BEADS :])
        return [
            jnp.concatenate([f[c * BEADS : (c + 1) * BEADS] for f in forces], axis=1)
            for c in range(3)
        ]

    for sub in range(SUBS):
        pushed = bonded(q)
        factor = (0.5 if sub == 0 else 1.0) * interval * inverse
        v = [v[c] + factor * pushed[c] for c in range(3)]
        for c in range(3):
            moved = exact(motion_l, jnp.concatenate([q[c], v[c]], axis=0))
            q[c], v[c] = moved[:BEADS], moved[BEADS:]
    pushed = bonded(q)
    p = [masses * v[c] + (0.5 * interval) * pushed[c] for c in range(3)]
    beads = BEADS // parts
    for i in range(parts):
        for c in range(3):
            outs[i][c] = q[c][i * beads : (i + 1) * beads]
            outs[i][3 + c] = p[c][i * beads : (i + 1) * beads]
    rows = jnp.concatenate(q, axis=0)
    c16 = exact(contract[bead[0]], rows, 2)
    row = lax.broadcasted_iota(jnp.int32, (ROWS, width), 0)
    logs = math.log2(math.e) * jnp.log(per_atom(strength_rows))
    c16 = jnp.where(row == 0, logs, c16)
    c_out[...] = c16
    for out in outs[1:parts]:
        if out.shape[0] == 7:
            out[6] = c16
    if edge:
        rim = GT * TILE
        head = c16[:, :rim] if before is None else before[:, :rim]
        outs[-1][...] = jnp.where(bead[0] == 0, head, c16[:, width - rim :])


def substeps(chunk, chunks, bead, pieces, force, mass, strength, ends, hot, motion, expand, contract, edge, before):
    parts = len(pieces)
    lanes = pieces[0].shape[2]
    beads = BEADS // parts
    extra = [before] if edge and chunk else []
    shapes = [(6, beads, lanes)] + [(7, beads, lanes)] * (parts - 1) + [(ROWS, lanes)]
    if edge:
        shapes.append((ROWS, GT * TILE))
    return pl.pallas_call(
        functools.partial(step_kernel, parts, chunk, chunks, lanes // TILE, int(edge)),
        in_specs=[IN_SMEM] + [IN_VMEM] * (parts + 8 + len(extra)),
        out_specs=[IN_VMEM] * len(shapes),
        out_shape=[vmem_out(s, F32) for s in shapes],
        cost_estimate=COST,
        name="substeps",
    )(
        bead,
        *[near(x) for x in pieces + [force]],
        mass,
        strength,
        near(ends),
        near(hot),
        motion,
        expand,
        contract,
        *[near(x) for x in extra],
    )


def finish_kernel(chunks, bead, expand, force, *refs):
    pos, mom = refs[-2:]
    parts = refs[:-2]
    bead_count = len(parts) // chunks
    lanes = parts[0].shape[2]
    comp = pl.program_id(0)
    table = expand[bead[0], comp]
    for i, part in enumerate(parts):
        chunk, distance = divmod(i, bead_count)
        block = lax.rem(bead[0] + bead_count - distance, bead_count)
        start = pl.multiple_of(block * (chunks * lanes) + chunk * lanes, TILE)
        where = pl.ds(start, lanes)
        pos[0, :, where] = part[comp]
        mom[0, :, where] = part[3 + comp] + 0.5 * time_step * exact(table, force[:, where])


def finish(chunks, bead, parts, expand, force):
    slab = force.shape[1]
    beads = parts[0].shape[1]
    return pl.pallas_call(
        functools.partial(finish_kernel, chunks),
        grid=(3,),
        in_specs=[IN_SMEM] + [IN_VMEM] * (2 + len(parts)),
        out_specs=[pl.BlockSpec((1, beads, slab), lambda i: (i, 0, 0))] * 2,
        out_shape=[jax.ShapeDtypeStruct((3, beads, slab), F32)] * 2,
        cost_estimate=COST,
        name="finish",
    )(bead, expand, near(force), *[near(x) for x in parts])


def body(positions, momenta, masses, strengths, bond_ends, angle_ends, neighbour_tiles):
    beads, _, slab = positions.shape
    bead_count = lax.axis_size("bead")
    bead = lax.axis_index("bead")
    space_count = lax.axis_size("space")
    space = lax.axis_index("space")
    block = slab // bead_count
    slab_tiles = slab // TILE
    block_tiles = block // TILE
    all_tiles = slab_tiles * space_count
    rim = GT * TILE
    chunks = 2 if block_tiles % 4 == 0 else 1
    lanes = block // chunks
    interval = time_step / SUBS
    pair = bead_count == 2

    pos = positions.transpose(1, 0, 2)
    mom = momenta.transpose(1, 0, 2)
    bead_at = jnp.reshape(bead, (1,)).astype(jnp.int32)
    space_at = jnp.reshape(space, (1,)).astype(jnp.int32)
    mass = masses.reshape(slab_tiles, TILE)
    strength = strengths.reshape(slab_tiles, TILE)
    turned = contract_rows(beads)
    table = contract_table(BEADS, KEPT)
    own_tables = [table[:, i * beads : (i + 1) * beads] for i in range(bead_count)]

    def stack(tables):
        return jnp.asarray(np.stack(tables))

    begin_left = stack([stacked_left(contract_left(t)) for t in own_tables])
    finish_left = stack(
        [
            np.stack(
                [stacked_left(expand_left(t)[c * beads : (c + 1) * beads]) for c in range(3)]
            )
            for t in own_tables
        ]
    )
    contract_l = stack([stacked_left(contract_left(t), 2) for t in turned])
    expand_l = stack([stacked_left(expand_left(t)) for t in turned])
    motion = jnp.asarray(stacked_left(motion_table(BEADS, interval)))

    def lanes_of(x, start, size):
        return lax.dynamic_slice_in_dim(x, start, size, x.ndim - 1)

    def permutation(step, flip):
        return [
            (s * 2 + b, ((s + step(b)) % space_count) * 2 + (b ^ flip))
            for s in range(space_count)
            for b in range(2)
        ]

    def rims(x):
        up = [(i, (i + 1) % space_count) for i in range(space_count)]
        down = [((i + 1) % space_count, i) for i in range(space_count)]
        return (
            lax.ppermute(x[:, slab - rim :], "space", up),
            lax.ppermute(x[:, :rim], "space", down),
        )

    def relative(tile, info):
        x = tile - info[1] * slab_tiles
        x = jnp.where(x >= all_tiles - GT, x - all_tiles, x)
        return jnp.where(x < -GT, x + all_tiles, x)

    def spots_first(info):
        first = info[0] * (block_tiles - GT)
        outside = block_tiles + GT

        def spot(tile):
            x = relative(tile, info)
            right = jnp.where(x >= slab_tiles, x - slab_tiles + outside, x - first)
            return jnp.where(x < 0, x + GT + outside, right)

        return info[0] * block_tiles, lambda t: t + info[0] * GT, spot

    def spots_last(info):
        left_at = slab_tiles + jnp.where(info[0] == 0, GT, 0)
        right_at = slab_tiles + jnp.where(info[0] == 0, 0, GT)

        def turn(x):
            x = x - info[0] * block_tiles
            return jnp.where(x < 0, x + slab_tiles, x)

        def spot(tile):
            x = relative(tile, info)
            right = jnp.where(x >= slab_tiles, x - slab_tiles + right_at, turn(x))
            return jnp.where(x < 0, x + GT + left_at, right)

        return 0, turn, spot

    def spots_slab(first):
        def spots(info):
            start = info[0] * block_tiles if first else 0

            def spot(tile):
                x = relative(tile, info)
                return jnp.where(x < 0, x + GT + slab_tiles, jnp.where(x >= slab_tiles, x + GT, x))

            return start, lambda t: t + start, spot

        return spots

    pieces = [[] for _ in range(chunks)]
    if pair:
        mine, theirs, straight, across, *blocks = begin(
            True, chunks, bead_at, begin_left, strength, pos, mom
        )
        theirs = lax.ppermute(theirs, "bead", SWAP)
        straight = lax.ppermute(
            straight, ("space", "bead"), permutation(lambda b: -1 if b else 1, 0)
        )
        across = lax.ppermute(across, ("space", "bead"), permutation(lambda b: 1 if b else -1, 1))
        segments = [[mine, theirs], [straight, across]]
        for chunk in range(chunks):
            other = lax.ppermute(blocks[chunks + chunk], "bead", SWAP)
            pieces[chunk] = [blocks[chunk], other]
        spots = spots_first
    else:
        (part,) = begin(False, chunks, bead_at, begin_left, strength, pos, mom)
        summed = lax.psum(part, "bead")
        first_row = lax.broadcasted_iota(jnp.int32, summed.shape, 0) == 0
        summed = jnp.where(first_row, jnp.log2(strengths)[None, :], summed)
        segments = [[summed], *[[x] for x in rims(summed)]]
        spots = spots_slab(True)
        for chunk in range(chunks):
            parts = []
            for d in range(bead_count):
                start = jnp.mod(bead - d, bead_count) * block + chunk * lanes
                piece = jnp.concatenate(
                    [lanes_of(pos, start, lanes), lanes_of(mom, start, lanes)], 0
                )
                back = [(i, (i - d) % bead_count) for i in range(bead_count)]
                parts.append(lax.ppermute(piece, "bead", back) if d else piece)
            pieces[chunk] = [jnp.concatenate(parts, 1)]

    ends, hot = prepare(bead_at, bond_ends, angle_ends, block_tiles)
    force = pair_forces(spots, segments, block_tiles, bead_at, space_at, neighbour_tiles)

    own_out, returned, contracted = [], [], []
    edge = None
    for chunk in range(chunks):
        last = pair and chunk == chunks - 1
        outs = substeps(
            chunk, chunks, bead_at, pieces[chunk], force, mass, strength, ends, hot, motion,
            expand_l, contract_l, last, contracted[0] if contracted else None,
        )
        if last:
            *outs, edge = outs
        *outs, c16 = outs
        if not pair:
            outs = [outs[0][:, d * beads : (d + 1) * beads] for d in range(bead_count)]
        own_out.append(outs[0])
        contracted.append(c16)
        back = []
        for d in range(1, bead_count):
            on = [(i, (i + d) % bead_count) for i in range(bead_count)]
            back.append(lax.ppermute(outs[d], "bead", on))
        returned.append(back)

    if pair:
        theirs = lax.ppermute(contracted[-1], "bead", SWAP)
        straight = lax.ppermute(edge, ("space", "bead"), permutation(lambda b: 1 if b else -1, 0))
        across = lax.ppermute(
            edge, ("space", "bead"), permutation(lambda b: 1 if b else -1, 1)
        )
        early = [x[0] for x in returned[:-1]]
        segments = [[x] for x in contracted + early + [theirs, straight, across]]
        spots = spots_last
    else:
        c16 = jnp.concatenate(contracted, 1) if chunks > 1 else contracted[0]
        everyone = lax.all_gather(c16, "bead", axis=1, tiled=True)
        segments = [[everyone], *[[x] for x in rims(everyone)]]
        spots = spots_slab(False)
    force = pair_forces(spots, segments, slab_tiles, bead_at, space_at, neighbour_tiles)

    parts = [x for chunk in range(chunks) for x in [own_out[chunk]] + returned[chunk]]
    new_pos, new_mom = finish(chunks, bead_at, parts, finish_left, force)
    return new_pos.transpose(1, 0, 2), new_mom.transpose(1, 0, 2)


SWAP = [(0, 1), (1, 0)]


def solution(mesh):
    placed = (
        P("bead", None, "space"),
        P("bead", None, "space"),
        P("space"),
        P("space"),
        P(None, "space"),
        P(None, "space"),
        P(None, "space"),
    )

    return jax.shard_map(
        body,
        mesh=mesh,
        in_specs=placed,
        out_specs=(P("bead", None, "space"), P("bead", None, "space")),
        check_vma=False,
    )
```

profile of v0, /device:TPU:0, one launch (start us, length us, event | category | flops | bytes accessed | tf_op | source)
XLA Modules:
  0.0 80.9 jit_solution(11131245746312233232)
XLA Ops:
  0.6 3.7 %begin.1 = (f32[16,2304]{1,0:T(8,128)S(1)}, f32[16,2304]{1,0:T(8,128)S(1)}, f32[16,256]{1,0:T(8,128)S(1)}, f32[16,256]{1,0:T(8,128)S(1)}, f32[6,16,1024]{2,1,0:T...) custom-call(s32[1]{0:T(128)} %bitcast.bead, ...), custom_call_target="tpu_custom_call" | custom-call | flops 10000000 | bytes 100000 | tf_op jit(solution)/shard_map/begin/pallas_call | solution.py:203
  4.4 0.0 copy-start.2
  4.4 0.7 copy-done.2
  5.1 3.0 %collective-permute-start = (f32[6,16,1024]{2,1,0:T(8,128)S(1)}, f32[6,16,1024]{2,1,0:T(8,128)S(1)}, u32[]{:S(2)}, u32[]{:S(2)}) collective-permute-start(f32[6,16,1024]{2,1,0:T(8,128)S(1)} %get-tuple-element.22), channel_id=1, source_target_pairs={{0,1},{1,0},{2,3},{3,2},{4,5},{5,4},{6,7},{7,6},{8,9},{9,8},{10,11... | collective-permute-start | bytes 1179656 | tf_op jit(solution)/shard_map/ppermute | solution.py:662
  8.2 0.0 collective-permute-start.4
  8.2 2.0 %collective-permute-start.1 = (f32[16,2304]{1,0:T(8,128)S(1)}, f32[16,2304]{1,0:T(8,128)S(1)}, u32[]{:S(2)}, u32[]{:S(2)}) collective-permute-start(f32[16,2304]{1,0:T(8,128)S(1)} %get-tuple-element.24), channel_id=1, source_target_pairs={{0,1},{1,0},{2,3},{3,2},{4,5},{5,4},{6,7},{7,6},{8,9},{9,8},{10,11... | collective-permute-start | bytes 442376 | tf_op jit(solution)/shard_map/ppermute | solution.py:655
  10.2 0.0 collective-permute-start.2
  10.2 4.6 %collective-permute-start.3 = (f32[16,256]{1,0:T(8,128)S(1)}, f32[16,256]{1,0:T(8,128)S(1)}, u32[]{:S(2)}, u32[]{:S(2)}) collective-permute-start(f32[16,256]{1,0:T(8,128)S(1)} %get-tuple-element.26), channel_id=1, source_target_pairs={{0,31},{1,2},{2,1},{3,4},{4,3},{5,6},{6,5},{7,8},{8,7},{9,10},{10,... | collective-permute-start | bytes 49160 | tf_op jit(solution)/shard_map/ppermute | solution.py:659
  14.7 1.4 %prepare.1 = (s32[16,4,128]{2,1,0:T(4,128)S(1)}, bf16[16,128,256]{2,1,0:T(8,128)(2,1)S(1)}) custom-call(s32[1]{0:T(128)} %bitcast.bead, s32[2,4096]{1,0:T(2,128)} %bonds.1, s32[3,2048]{1,0:T(4,128)} %angles.1), custom_call_target="tpu_custom_call" | custom-call | flops 10000000 | bytes 100000 | tf_op jit(solution)/shard_map/prepare/pallas_call | solution.py:255
  16.2 0.0 collective-permute-done.2.refs_2_
  16.2 0.9 %collective-permute-done.3.refs_3_ = f32[16,256]{1,0:T(8,128)S(1)} collective-permute-done((f32[16,256]{1,0:T(8,128)S(1)}, f32[16,256]{1,0:T(8,128)S(1)}, u32[]{:S(2)}, u32[]{:S(2)}) %collective-permute-start.3) | collective-permute-done | bytes 16416 | tf_op jit(solution)/shard_map/ppermute | solution.py:659
  17.0 12.0 %collective-permute-done.1.refs_1_ = f32[16,2304]{1,0:T(8,128)S(1)} collective-permute-done((f32[16,2304]{1,0:T(8,128)S(1)}, f32[16,2304]{1,0:T(8,128)S(1)}, u32[]{:S(2)}, u32[]{:S(2)}) %collective-permute-start.1) | collective-permute-done | bytes 147488 | tf_op jit(solution)/shard_map/ppermute | solution.py:655
  29.0 6.0 %pair_forces.2.refs_2_ = f32[16,2048]{1,0:T(8,128)S(1)} custom-call(s32[1]{0:T(128)} %bitcast.bead, s32[1]{0:T(128)} %bitcast.1.space, s32[3,32]{1,0:T(4,128)} %nbr.3, f32[16,2304]{1,0:T(8,128)S(1)} %get-tuple-element.23.refs_0_, f32[16,2304]{1,0:T(8,128)S(1)} %collective-permute-done.1.refs_1_, f32[16,256]{1,0:T(8,128)S(1)} %collective-permute-done.2.refs_2_, ...), custom_call_target="tpu_custom_call" | custom-call | flops 10000000 | bytes 100000 | tf_op jit(solution)/shard_map/pair_forces/pallas_call | solution.py:375
  35.0 0.0 collective-permute-done.refs_1_
  35.0 0.0 copy-start.3
  35.0 7.2 %substeps.2 = (f32[6,16,1024]{2,1,0:T(8,128)S(1)}, f32[7,16,1024]{2,1,0:T(8,128)}, f32[16,1024]{1,0:T(8,128)S(1)}) custom-call(s32[1]{0:T(128)} %bitcast.bead, f32[6,16,1024]{2,1,0:T(8,128)S(1)} %get-tuple-element.21.refs_0_, f32[6,16,1024]{2,1,0:T(8,128)S(1)} %collective-permute-done.refs_1_, f32[16,2048]{1,0:T(8,128)S(1)} %pair_forces.2.refs_2_, ...), custom_call_target="tpu_custom_call" | custom-call | flops 10000000 | bytes 100000 | tf_op jit(solution)/shard_map/substeps/pallas_call | solution.py:496
  42.2 0.0 copy-start
  42.2 0.8 copy-done
  43.0 1.9 %collective-permute-start.5 = (f32[7,16,1024]{2,1,0:T(8,128)}, f32[7,16,1024]{2,1,0:T(8,128)S(1)}, u32[]{:S(2)}, u32[]{:S(2)}) collective-permute-start(f32[7,16,1024]{2,1,0:T(8,128)} %get-tuple-element.33), channel_id=1, source_target_pairs={{0,1},{1,0},{2,3},{3,2},{4,5},{5,4},{6,7},{7,6},{8,9},{9,8},{10,11... | collective-permute-start | bytes 1376264 | tf_op jit(solution)/shard_map/ppermute | solution.py:704
  44.9 0.0 collective-permute-done.4.refs_1_
  44.9 0.0 copy-done.3
  44.9 6.5 %substeps.3 = (f32[6,16,1024]{2,1,0:T(8,128)S(1)}, f32[7,16,1024]{2,1,0:T(8,128)S(1)}, f32[16,1024]{1,0:T(8,128)S(1)}, f32[16,256]{1,0:T(8,128)S(1)}) custom-call(s32[1]{0:T(128)} %bitcast.bead, f32[6,16,1024]{2,1,0:T(8,128)S(1)} %copy-done.3, f32[6,16,1024]{2,1,0:T(8,128)} %collective-permute-done.4.refs_1_, f32[16,2048]{1,0:T(8,128)S(1)} %pair_forces.2.refs_2_, ...), custom_call_target="tpu_custom_call" | custom-call | flops 10000000 | bytes 100000 | tf_op jit(solution)/shard_map/substeps/pallas_call | solution.py:496
  51.4 0.2 collective-permute-start.9
  51.5 1.9 %collective-permute-start.6 = (f32[16,1024]{1,0:T(8,128)S(1)}, f32[16,1024]{1,0:T(8,128)S(1)}, u32[]{:S(2)}, u32[]{:S(2)}) collective-permute-start(f32[16,1024]{1,0:T(8,128)S(1)} %get-tuple-element.32.refs_1_), channel_id=1, source_target_pairs={{0,1},{1,0},{2,3},{3,2},{4,5},{5,4},{6,7},{7,6},{8,9},{9,8},{10,11... | collective-permute-start | bytes 196616 | tf_op jit(solution)/shard_map/ppermute | solution.py:708
  53.5 0.0 copy-start.1
  53.5 3.2 %collective-permute-start.8 = (f32[16,256]{1,0:T(8,128)S(1)}, f32[16,256]{1,0:T(8,128)S(1)}, u32[]{:S(2)}, u32[]{:S(2)}) collective-permute-start(f32[16,256]{1,0:T(8,128)S(1)} %get-tuple-element.34), channel_id=1, source_target_pairs={{0,31},{1,2},{2,1},{3,4},{4,3},{5,6},{6,5},{7,8},{8,7},{9,10},{10,... | collective-permute-start | bytes 49160 | tf_op jit(solution)/shard_map/ppermute | solution.py:710
  56.6 1.4 %collective-permute-start.7 = (f32[16,256]{1,0:T(8,128)S(1)}, f32[16,256]{1,0:T(8,128)S(1)}, u32[]{:S(2)}, u32[]{:S(2)}) collective-permute-start(f32[16,256]{1,0:T(8,128)S(1)} %get-tuple-element.34), channel_id=1, source_target_pairs={{0,30},{1,3},{2,0},{3,5},{4,2},{5,7},{6,4},{7,9},{8,6},{9,11},{10,... | collective-permute-start | bytes 49160 | tf_op jit(solution)/shard_map/ppermute | solution.py:709
  58.0 2.3 %collective-permute-done.8.refs_5_ = f32[16,256]{1,0:T(8,128)S(1)} collective-permute-done((f32[16,256]{1,0:T(8,128)S(1)}, f32[16,256]{1,0:T(8,128)S(1)}, u32[]{:S(2)}, u32[]{:S(2)}) %collective-permute-start.8) | collective-permute-done | bytes 16416 | tf_op jit(solution)/shard_map/ppermute | solution.py:710
  60.3 0.0 collective-permute-done.7.refs_4_
  60.3 6.8 %collective-permute-done.6.refs_3_ = f32[16,1024]{1,0:T(8,128)S(1)} collective-permute-done((f32[16,1024]{1,0:T(8,128)S(1)}, f32[16,1024]{1,0:T(8,128)S(1)}, u32[]{:S(2)}, u32[]{:S(2)}) %collective-permute-start.6) | collective-permute-done | bytes 65568 | tf_op jit(solution)/shard_map/ppermute | solution.py:708
  67.1 0.0 collective-permute-done.5.refs_2_.refs_1_
  67.1 10.8 %pair_forces.3.force = f32[16,4096]{1,0:T(8,128)S(1)} custom-call(s32[1]{0:T(128)} %bitcast.bead, s32[1]{0:T(128)} %bitcast.1.space, s32[3,32]{1,0:T(4,128)} %nbr.3, f32[16,1024]{1,0:T(8,128)S(1)} %get-tuple-element.29.refs_10_.refs_0_, f32[16,1024]{1,0:T(8,128)S(1)} %get-tuple-element.32.refs_1_, f32[7,16,1024]{2,1,0:T(8,128)S(1)} %collective-permute-done.5.refs_2_.refs_1_, ...), custom_call_target="tpu_custom_call" | custom-call | flops 10000000 | bytes 100000 | tf_op jit(solution)/shard_map/pair_forces/pallas_call | solution.py:375
  77.9 0.0 collective-permute-done.9.refs_3_
  77.9 0.0 copy-done.1
  78.0 2.9 %finish.1 = (f32[3,16,4096]{2,1,0:T(8,128)}, f32[3,16,4096]{2,1,0:T(8,128)}) custom-call(s32[1]{0:T(128)} %bitcast.bead, bf16[2,3,48,48]{3,2,1,0:T(8,128)(2,1)} %constant.19.clone.expand, f32[16,4096]{1,0:T(8,128)S(1)} %pair_forces.3.force, f32[6,16,1024]{2,1,0:T(8,128)S(1)} %copy-done.1, f32[7,16,1024]{2,1,0:T(8,128)S(1)} %collective-permute-done.5.refs_2_.refs_1_, ...), custom_call_target="tpu_custom_call" | custom-call | flops 10000000 | bytes 100000 | tf_op jit(solution)/shard_map/finish/pallas_call | solution.py:536
Async XLA Ops:
  4.4 0.8 copy-start.2
  5.1 29.9 %collective-permute-start = (f32[6,16,1024]{2,1,0:T(8,128)S(1)}, f32[6,16,1024]{2,1,0:T(8,128)S(1)}, u32[]{:S(2)}, u32[]{:S(2)}) collective-permute-start(f32[6,16,1024]{2,1,0:T(8,128)S(1)} %get-tuple-element.22), channel_id=1, source_target_pairs={{0,1},{1,0},{2,3},{3,2},{4,5},{5,4},{6,7},{7,6},{8,9},{9,8},{10,11... | collective-permute-start | bytes 1179656 | tf_op jit(solution)/shard_map/ppermute | solution.py:662
  8.2 36.7 %collective-permute-start.4 = (f32[6,16,1024]{2,1,0:T(8,128)}, f32[6,16,1024]{2,1,0:T(8,128)}, u32[]{:S(2)}, u32[]{:S(2)}) collective-permute-start(f32[6,16,1024]{2,1,0:T(8,128)} %get-tuple-element.31), channel_id=1, source_target_pairs={{0,1},{1,0},{2,3},{3,2},{4,5},{5,4},{6,7},{7,6},{8,9},{9,8},{10,11... | collective-permute-start | bytes 1179656 | tf_op jit(solution)/shard_map/ppermute | solution.py:662
  8.2 20.8 %collective-permute-start.1 = (f32[16,2304]{1,0:T(8,128)S(1)}, f32[16,2304]{1,0:T(8,128)S(1)}, u32[]{:S(2)}, u32[]{:S(2)}) collective-permute-start(f32[16,2304]{1,0:T(8,128)S(1)} %get-tuple-element.24), channel_id=1, source_target_pairs={{0,1},{1,0},{2,3},{3,2},{4,5},{5,4},{6,7},{7,6},{8,9},{9,8},{10,11... | collective-permute-start | bytes 442376 | tf_op jit(solution)/shard_map/ppermute | solution.py:655
  10.2 6.0 %collective-permute-start.2 = (f32[16,256]{1,0:T(8,128)S(1)}, f32[16,256]{1,0:T(8,128)S(1)}, u32[]{:S(2)}, u32[]{:S(2)}) collective-permute-start(f32[16,256]{1,0:T(8,128)S(1)} %get-tuple-element.25), channel_id=1, source_target_pairs={{0,2},{1,31},{2,4},{3,1},{4,6},{5,3},{6,8},{7,5},{8,10},{9,7},{10,... | collective-permute-start | bytes 49160 | tf_op jit(solution)/shard_map/ppermute | solution.py:656
  10.2 6.9 %collective-permute-start.3 = (f32[16,256]{1,0:T(8,128)S(1)}, f32[16,256]{1,0:T(8,128)S(1)}, u32[]{:S(2)}, u32[]{:S(2)}) collective-permute-start(f32[16,256]{1,0:T(8,128)S(1)} %get-tuple-element.26), channel_id=1, source_target_pairs={{0,31},{1,2},{2,1},{3,4},{4,3},{5,6},{6,5},{7,8},{8,7},{9,10},{10,... | collective-permute-start | bytes 49160 | tf_op jit(solution)/shard_map/ppermute | solution.py:659
  35.0 9.9 %copy-start.3 = (f32[6,16,1024]{2,1,0:T(8,128)S(1)}, f32[6,16,1024]{2,1,0:T(8,128)}, u32[]{:S(2)}) copy-start(f32[6,16,1024]{2,1,0:T(8,128)} %copy-done.2) | copy-start | bytes 1179652
  42.2 0.8 copy-start
  43.0 24.2 %collective-permute-start.5 = (f32[7,16,1024]{2,1,0:T(8,128)}, f32[7,16,1024]{2,1,0:T(8,128)S(1)}, u32[]{:S(2)}, u32[]{:S(2)}) collective-permute-start(f32[7,16,1024]{2,1,0:T(8,128)} %get-tuple-element.33), channel_id=1, source_target_pairs={{0,1},{1,0},{2,3},{3,2},{4,5},{5,4},{6,7},{7,6},{8,9},{9,8},{10,11... | collective-permute-start | bytes 1376264 | tf_op jit(solution)/shard_map/ppermute | solution.py:704
  51.4 26.6 %collective-permute-start.9 = (f32[7,16,1024]{2,1,0:T(8,128)S(1)}, f32[7,16,1024]{2,1,0:T(8,128)S(1)}, u32[]{:S(2)}, u32[]{:S(2)}) collective-permute-start(f32[7,16,1024]{2,1,0:T(8,128)S(1)} %get-tuple-element.37), channel_id=1, source_target_pairs={{0,1},{1,0},{2,3},{3,2},{4,5},{5,4},{6,7},{7,6},{8,9},{9,8},{10,11... | collective-permute-start | bytes 1376264 | tf_op jit(solution)/shard_map/ppermute | solution.py:704
  51.5 15.6 %collective-permute-start.6 = (f32[16,1024]{1,0:T(8,128)S(1)}, f32[16,1024]{1,0:T(8,128)S(1)}, u32[]{:S(2)}, u32[]{:S(2)}) collective-permute-start(f32[16,1024]{1,0:T(8,128)S(1)} %get-tuple-element.32.refs_1_), channel_id=1, source_target_pairs={{0,1},{1,0},{2,3},{3,2},{4,5},{5,4},{6,7},{7,6},{8,9},{9,8},{10,11... | collective-permute-start | bytes 196616 | tf_op jit(solution)/shard_map/ppermute | solution.py:708
  53.5 24.5 %copy-start.1 = (f32[6,16,1024]{2,1,0:T(8,128)S(1)}, f32[6,16,1024]{2,1,0:T(8,128)}, u32[]{:S(2)}) copy-start(f32[6,16,1024]{2,1,0:T(8,128)} %copy-done) | copy-start | bytes 1179652
  53.5 6.9 %collective-permute-start.8 = (f32[16,256]{1,0:T(8,128)S(1)}, f32[16,256]{1,0:T(8,128)S(1)}, u32[]{:S(2)}, u32[]{:S(2)}) collective-permute-start(f32[16,256]{1,0:T(8,128)S(1)} %get-tuple-element.34), channel_id=1, source_target_pairs={{0,31},{1,2},{2,1},{3,4},{4,3},{5,6},{6,5},{7,8},{8,7},{9,10},{10,... | collective-permute-start | bytes 49160 | tf_op jit(solution)/shard_map/ppermute | solution.py:710
  56.6 3.7 %collective-permute-start.7 = (f32[16,256]{1,0:T(8,128)S(1)}, f32[16,256]{1,0:T(8,128)S(1)}, u32[]{:S(2)}, u32[]{:S(2)}) collective-permute-start(f32[16,256]{1,0:T(8,128)S(1)} %get-tuple-element.34), channel_id=1, source_target_pairs={{0,30},{1,3},{2,0},{3,5},{4,2},{5,7},{6,4},{7,9},{8,6},{9,11},{10,... | collective-permute-start | bytes 49160 | tf_op jit(solution)/shard_map/ppermute | solution.py:709
where the time goes:
time: 81.2 us; the launch traced here: 80.9 us
  Pallas kernels  38.5 us (47%)
  waiting for transfers between devices  22 us (27%)
  starting transfers between devices  18.2 us (22%)
  local copies, waits for them, and re-layouts  1.52 us (2%)
    pallas_call x2, Pallas kernels, pair_forces(): pl.pallas_call(functools.partial(pair_kernel, spots, sizes, own_count), i...  16.8 us
    pallas_call x2, Pallas kernels, substeps(): pl.pallas_call(functools.partial(step_kernel, parts, chunk, chunks, lanes...  13.6 us
    ppermute x1, waiting for transfers between devices, body(): theirs = lax.ppermute(theirs, 'bead', SWAP)  12 us
    ppermute x1, waiting for transfers between devices, body(): theirs = lax.ppermute(contracted[-1], 'bead', SWAP)  6.82 us
    ppermute x1, starting transfers between devices, body(): lax.ppermute(across, ('space', 'bead'), permutation(lambda b: 1 if b else...  4.56 us
    ppermute x2, starting transfers between devices, body(): lax.ppermute(edge, ('space', 'bead'), permutation(lambda b: 1 if b else -...  4.55 us
    pallas_call x1, Pallas kernels, begin(): pl.pallas_call(functools.partial(begin_kernel, pair, chunks), grid=(slab...  3.75 us
    ppermute x2, starting transfers between devices, body(): other = lax.ppermute(blocks[chunks + chunk], 'bead', SWAP)  3.04 us
  transfers between devices with their start and end apart: 10, of which 4 were waited for; matrix products, arithmetic and copies ran while one was open for 0% of the time, Pallas kernels for 39%

commit v1 on v0

--- a/solution.py
+++ b/solution.py
@@ -36,10 +36,15 @@
     return pltpu.with_memory_space_constraint(x, IN_SPACE)
 
 
+def far(x):
+    return pltpu.with_memory_space_constraint(x, pltpu.MemorySpace.HBM)
+
+
 def vmem_out(shape, dtype):
     return IN_SPACE(shape, dtype)
 
 
+PARAMS = pltpu.CompilerParams(vmem_limit_bytes=20 * 1024 * 1024)
 COST = pl.CostEstimate(flops=10_000_000, bytes_accessed=100_000, transcendentals=0)
 F32 = jnp.float32
 BF16 = jnp.bfloat16
@@ -148,32 +153,36 @@
     return BEADS / KEPT * contract_left(table).T
 
 
-def begin_kernel(pair, chunks, bead, left, strengths, pos, mom, *outs):
-    comps, _, lanes = pos.shape
-    step = pl.program_id(0)
-    whole = outs[-1]
-    x = jnp.concatenate([pos[c] for c in range(comps)], axis=0)
-    c16 = exact(left[bead[0]], x)
+def begin_kernel(chunks, bead, left, strengths, pos, mom, *refs):
+    mine, theirs, straight, across = refs[:4]
+    blocks = refs[4:-2]
+    whole, sems = refs[-2:]
+    lanes = blocks[0].shape[2]
+    slab = whole.shape[1]
+    starts, copies = [], []
+    for i in range(2 * chunks):
+        owner = bead[0] if i < chunks else 1 - bead[0]
+        starts.append(pl.multiple_of((owner * chunks + i % chunks) * lanes, TILE))
+    for half, source in enumerate((pos, mom)):
+        for i, block in enumerate(blocks):
+            copy = pltpu.make_async_copy(
+                source.at[:, :, pl.ds(starts[i], lanes)],
+                block.at[pl.ds(3 * half, 3)],
+                sems.at[half * len(blocks) + i],
+            )
+            copy.start()
+            copies.append(copy)
+    table = left[bead[0]]
     logs = math.log2(math.e) * jnp.log(strengths[...])
-    logs = jnp.concatenate([logs[t : t + 1] for t in range(lanes // TILE)], axis=1)
-    row = lax.broadcasted_iota(jnp.int32, (ROWS, lanes), 0)
-    c16 = jnp.where(row == 0, logs, c16)
-    whole[:, pl.ds(pl.multiple_of(step * lanes, TILE), lanes)] = c16
-    if not pair:
-        return
-    mine, theirs, straight, across = outs[:4]
-    targets = outs[4:-1]
-    for i in range(2 * chunks):
-        owner, chunk = divmod(i, chunks)
-
-        def put(target):
-            target[:3] = pos[...]
-            target[3:] = mom[...]
-
-        pl.when((step == i) & (bead[0] == owner))(functools.partial(put, targets[chunk]))
-        pl.when((step == i) & (bead[0] != owner))(functools.partial(put, targets[chunks + chunk]))
-
-    slab = whole.shape[1]
+    for t in range(slab // TILE):
+        whole[0:1, t * TILE : (t + 1) * TILE] = logs[t : t + 1]
+    for i, block in enumerate(blocks):
+        copies[i].wait()
+        x = jnp.concatenate([block[c] for c in range(3)], axis=0)
+        where = pl.ds(starts[i], lanes)
+        row = lax.broadcasted_iota(jnp.int32, (ROWS, lanes), 0)
+        whole[:, where] = jnp.where(row == 0, whole[:, where], exact(table, x))
+
     block, rim = slab // 2, GT * TILE
     size = block + rim
 
@@ -186,36 +195,57 @@
         across[...] = head if which == 0 else tail
 
     for which in range(2):
-        pl.when((step == 2 * chunks - 1) & (bead[0] == which))(functools.partial(sides, which))
-
-
-def begin(pair, chunks, bead, left, strengths, pos, mom):
+        pl.when(bead[0] == which)(functools.partial(sides, which))
+    for copy in copies[len(blocks) :]:
+        copy.wait()
+
+
+def begin(chunks, bead, left, strengths, pos, mom):
     beads, slab = pos.shape[1:]
-    if pair:
-        block, rim = slab // 2, GT * TILE
-        lanes = block // chunks
-        shapes = [(ROWS, block + rim)] * 2 + [(ROWS, rim)] * 2
-        shapes += [(6, beads, lanes)] * (2 * chunks)
-        scratch = [pltpu.VMEM((ROWS, slab), F32)]
-    else:
-        lanes = math.gcd(slab, 1024)
-        shapes, scratch = [(ROWS, slab)], []
+    block, rim = slab // 2, GT * TILE
+    lanes = block // chunks
+    shapes = [(ROWS, block + rim)] * 2 + [(ROWS, rim)] * 2
+    shapes += [(6, beads, lanes)] * (2 * chunks)
     return pl.pallas_call(
-        functools.partial(begin_kernel, pair, chunks),
+        functools.partial(begin_kernel, chunks),
+        in_specs=[IN_SMEM, IN_VMEM, IN_VMEM] + [pl.BlockSpec(memory_space=pl.ANY)] * 2,
+        out_specs=[IN_VMEM] * len(shapes),
+        out_shape=[vmem_out(s, F32) for s in shapes],
+        scratch_shapes=[
+            pltpu.VMEM((ROWS, slab), F32),
+            pltpu.SemaphoreType.DMA((4 * chunks,)),
+        ],
+        compiler_params=PARAMS,
+        cost_estimate=COST,
+        name="begin",
+    )(bead, left, strengths, far(pos), far(mom))
+
+
+def partial_kernel(bead, left, strengths, pos, out):
+    comps, _, lanes = pos.shape
+    logs = math.log2(math.e) * jnp.log(strengths[...])
+    logs = jnp.concatenate([logs[t : t + 1] for t in range(lanes // TILE)], axis=1)
+    row = lax.broadcasted_iota(jnp.int32, (ROWS, lanes), 0)
+    x = jnp.concatenate([pos[c] for c in range(comps)], axis=0)
+    out[...] = jnp.where(row == 0, logs, exact(left[bead[0]], x))
+
+
+def partial_rows(bead, left, strengths, pos):
+    beads, slab = pos.shape[1:]
+    lanes = math.gcd(slab, 1024)
+    return pl.pallas_call(
+        partial_kernel,
         grid=(slab // lanes,),
         in_specs=[
             IN_SMEM,
             IN_VMEM,
             pl.BlockSpec((lanes // TILE, TILE), lambda i: (i, 0)),
             pl.BlockSpec((3, beads, lanes), lambda i: (0, 0, i)),
-            pl.BlockSpec((3, beads, lanes), lambda i: (0, 0, i)),
         ],
-        out_specs=[IN_VMEM] * len(shapes),
-        scratch_shapes=scratch,
-        out_shape=[vmem_out(s, F32) for s in shapes],
-        cost_estimate=COST,
-        name="begin",
-    )(bead, left, strengths, pos, mom)
+        out_specs=pl.BlockSpec((ROWS, lanes), lambda i: (0, i)),
+        out_shape=jax.ShapeDtypeStruct((ROWS, slab), F32),
+        name="partial_rows",
+    )(bead, left, strengths, pos)
 
 
 def prepare_kernel(group, bead, bonds, angles, ends, hot):
@@ -260,14 +290,15 @@
             vmem_out((block_tiles, 4, TILE), jnp.int32),
             vmem_out((block_tiles, TILE, 2 * TILE), BF16),
         ],
+        compiler_params=PARAMS,
         cost_estimate=COST,
         name="prepare",
     )(bead, bond_ends, angle_ends)
 
 
 def pair_kernel(spots, seg_sizes, own_count, bead, space, nbr, *refs):
-    total = sum(n for _, n in seg_sizes)
-    count = sum(n for n, _ in seg_sizes)
+    total = sum(n for *_, n in seg_sizes)
+    count = sum(n for n, *_ in seg_sizes)
     seg_refs = refs[:count]
     out, feat_i, feat_m, feat_p, base, weights_a, weights_b = refs[count:]
     column, own_spot, spot = spots((bead[0], space[0]))
@@ -305,12 +336,11 @@
 
     tile = 0
     at = 0
-    for number, tiles in seg_sizes:
+    for number, begins, tiles in seg_sizes:
         group = seg_refs[at : at + number]
         at += number
-        for i in range(tiles):
-            lanes = slice(i * TILE, (i + 1) * TILE)
-            c16 = group[0][:, lanes] if len(group[0].shape) == 2 else group[0][6, :, lanes]
+        for i in range(begins, begins + tiles):
+            c16 = group[0][:, i * TILE : (i + 1) * TILE]
             for other in group[1:]:
                 more = other[:, i * TILE : (i + 1) * TILE]
                 c16 = c16 + jnp.where(row == 0, 0.0, more)
@@ -324,7 +354,7 @@
     owner = row // 4
 
     def close(t, u):
-        return spot(nbr[u, column + t])
+        return spot(nbr[u, column(t)])
 
     def weigh(t, weights):
         features_i = feat_i[own_spot(t)]
@@ -368,10 +398,10 @@
 
 
 def pair_forces(spots, segments, own_count, bead, space, neighbour_tiles):
-    sizes = tuple((len(group), group[0].shape[-1] // TILE) for group in segments)
-    total = sum(n for _, n in sizes)
+    sizes = tuple((len(group), start, tiles) for group, start, tiles in segments)
+    total = sum(n for *_, n in sizes)
     assert own_count % 2 == 0
-    flat = [array for group in segments for array in group]
+    flat = [array for group, *_ in segments for array in group]
     return pl.pallas_call(
         functools.partial(pair_kernel, spots, sizes, own_count),
         in_specs=[IN_SMEM] * 3 + [IN_VMEM] * len(flat),
@@ -385,6 +415,7 @@
             pltpu.VMEM((6 * TILE, KEPT * TILE), BF16),
             pltpu.VMEM((6 * TILE, KEPT * TILE), BF16),
         ],
+        compiler_params=PARAMS,
         cost_estimate=COST,
         name="pair_forces",
     )(bead, space, neighbour_tiles, *[near(x) for x in flat])
@@ -394,7 +425,7 @@
     pieces = refs[:parts]
     force, mass_rows, strength_rows, ends, hot, motion, expand, contract = refs[parts : parts + 8]
     before = refs[parts + 8] if edge and chunk else None
-    outs = refs[len(refs) - parts - 1 - edge :]
+    outs = refs[len(refs) - parts - 1 - 2 * edge :]
     c_out = outs[parts]
     interval = time_step / SUBS
     width = group * TILE
@@ -476,13 +507,12 @@
     logs = math.log2(math.e) * jnp.log(per_atom(strength_rows))
     c16 = jnp.where(row == 0, logs, c16)
     c_out[...] = c16
-    for out in outs[1:parts]:
-        if out.shape[0] == 7:
-            out[6] = c16
     if edge:
         rim = GT * TILE
         head = c16[:, :rim] if before is None else before[:, :rim]
-        outs[-1][...] = jnp.where(bead[0] == 0, head, c16[:, width - rim :])
+        tail = c16[:, width - rim :]
+        outs[-2][...] = jnp.where(bead[0] == 0, tail, head)
+        outs[-1][...] = jnp.where(bead[0] == 0, head, tail)
 
 
 def substeps(chunk, chunks, bead, pieces, force, mass, strength, ends, hot, motion, expand, contract, edge, before):
@@ -490,14 +520,15 @@
     lanes = pieces[0].shape[2]
     beads = BEADS // parts
     extra = [before] if edge and chunk else []
-    shapes = [(6, beads, lanes)] + [(7, beads, lanes)] * (parts - 1) + [(ROWS, lanes)]
+    shapes = [(6, beads, lanes)] * parts + [(ROWS, lanes)]
     if edge:
-        shapes.append((ROWS, GT * TILE))
+        shapes += [(ROWS, GT * TILE)] * 2
     return pl.pallas_call(
         functools.partial(step_kernel, parts, chunk, chunks, lanes // TILE, int(edge)),
         in_specs=[IN_SMEM] + [IN_VMEM] * (parts + 8 + len(extra)),
         out_specs=[IN_VMEM] * len(shapes),
         out_shape=[vmem_out(s, F32) for s in shapes],
+        compiler_params=PARAMS,
         cost_estimate=COST,
         name="substeps",
     )(
@@ -539,9 +570,50 @@
         in_specs=[IN_SMEM] + [IN_VMEM] * (2 + len(parts)),
         out_specs=[pl.BlockSpec((1, beads, slab), lambda i: (i, 0, 0))] * 2,
         out_shape=[jax.ShapeDtypeStruct((3, beads, slab), F32)] * 2,
+        compiler_params=PARAMS,
         cost_estimate=COST,
         name="finish",
     )(bead, expand, near(force), *[near(x) for x in parts])
+
+
+def finish_block_kernel(chunks, bead, expand, inner, outer, *refs):
+    parts = refs[:chunks]
+    pos, mom = refs[-2:]
+    lanes = parts[0].shape[2]
+    rim = GT * TILE
+    comp = pl.program_id(0)
+    force = jnp.concatenate([outer[:, :rim], inner[...], outer[:, rim:]], axis=1)
+    kick = 0.5 * time_step * exact(expand[bead[0], comp], force)
+    for chunk, part in enumerate(parts):
+        where = slice(chunk * lanes, (chunk + 1) * lanes)
+        pos[0, :, where] = part[comp]
+        mom[0, :, where] = part[3 + comp] + kick[:, where]
+
+
+def finish_block(bead, distance, parts, expand, inner, outer, before):
+    beads, lanes = parts[0].shape[1:]
+    block = lanes * len(parts)
+    anywhere = [pl.BlockSpec(memory_space=pl.ANY)] * len(before)
+    whole = pl.BlockSpec(memory_space=pltpu.VMEM)
+    grid_spec = pltpu.PrefetchScalarGridSpec(
+        num_scalar_prefetch=1,
+        grid=(3,),
+        in_specs=[whole] * (3 + len(parts)) + anywhere,
+        out_specs=[
+            pl.BlockSpec((1, beads, block), lambda i, b: (i, 0, lax.rem(b[0] + distance, 2)))
+        ]
+        * 2,
+    )
+    at = 4 + len(parts)
+    return pl.pallas_call(
+        functools.partial(finish_block_kernel, len(parts)),
+        grid_spec=grid_spec,
+        out_shape=[jax.ShapeDtypeStruct((3, beads, 2 * block), F32)] * 2,
+        input_output_aliases={at + i: i for i in range(len(before))},
+        compiler_params=PARAMS,
+        cost_estimate=COST,
+        name="finish_block",
+    )(bead, expand, near(inner), near(outer), *[near(x) for x in parts], *before)
 
 
 def body(positions, momenta, masses, strengths, bond_ends, angle_ends, neighbour_tiles):
@@ -618,22 +690,32 @@
             right = jnp.where(x >= slab_tiles, x - slab_tiles + outside, x - first)
             return jnp.where(x < 0, x + GT + outside, right)
 
-        return info[0] * block_tiles, lambda t: t + info[0] * GT, spot
-
-    def spots_last(info):
-        left_at = slab_tiles + jnp.where(info[0] == 0, GT, 0)
-        right_at = slab_tiles + jnp.where(info[0] == 0, 0, GT)
-
-        def turn(x):
-            x = x - info[0] * block_tiles
-            return jnp.where(x < 0, x + slab_tiles, x)
-
+        return lambda t: t + info[0] * block_tiles, lambda t: t + info[0] * GT, spot
+
+    def spots_inner(info):
         def spot(tile):
-            x = relative(tile, info)
-            right = jnp.where(x >= slab_tiles, x - slab_tiles + right_at, turn(x))
+            return relative(tile, info) - info[0] * block_tiles
+
+        return lambda t: t + GT + info[0] * block_tiles, lambda t: t + GT, spot
+
+    def spots_outer(info):
+        bead_at = 4 * GT
+        far_at = bead_at + GT
+        left_at = jnp.where(info[0] == 0, far_at, bead_at)
+        right_at = jnp.where(info[0] == 0, bead_at, far_at)
+
+        def own(t):
+            return jnp.where(t < GT, t, t + block_tiles - 2 * GT)
+
+        def place(x):
+            return jnp.where(x < 2 * GT, x, x - (block_tiles - 4 * GT))
+
+        def spot(tile):
+            x = relative(tile, info) - info[0] * block_tiles
+            right = jnp.where(x >= block_tiles, x - block_tiles + right_at, place(x))
             return jnp.where(x < 0, x + GT + left_at, right)
 
-        return 0, turn, spot
+        return lambda t: own(t) + info[0] * block_tiles, lambda t: place(own(t)), spot
 
     def spots_slab(first):
         def spots(info):
@@ -643,31 +725,31 @@
                 x = relative(tile, info)
                 return jnp.where(x < 0, x + GT + slab_tiles, jnp.where(x >= slab_tiles, x + GT, x))
 
-            return start, lambda t: t + start, spot
+            return lambda t: t + start, lambda t: t + start, spot
 
         return spots
 
     pieces = [[] for _ in range(chunks)]
     if pair:
         mine, theirs, straight, across, *blocks = begin(
-            True, chunks, bead_at, begin_left, strength, pos, mom
+            chunks, bead_at, begin_left, strength, pos, mom
         )
         theirs = lax.ppermute(theirs, "bead", SWAP)
         straight = lax.ppermute(
             straight, ("space", "bead"), permutation(lambda b: -1 if b else 1, 0)
         )
         across = lax.ppermute(across, ("space", "bead"), permutation(lambda b: 1 if b else -1, 1))
-        segments = [[mine, theirs], [straight, across]]
+        segments = [([mine, theirs], 0, block_tiles + GT), ([straight, across], 0, GT)]
         for chunk in range(chunks):
             other = lax.ppermute(blocks[chunks + chunk], "bead", SWAP)
             pieces[chunk] = [blocks[chunk], other]
         spots = spots_first
     else:
-        (part,) = begin(False, chunks, bead_at, begin_left, strength, pos, mom)
+        part = partial_rows(bead_at, begin_left, strength, pos)
         summed = lax.psum(part, "bead")
         first_row = lax.broadcasted_iota(jnp.int32, summed.shape, 0) == 0
         summed = jnp.where(first_row, jnp.log2(strengths)[None, :], summed)
-        segments = [[summed], *[[x] for x in rims(summed)]]
+        segments = [([summed], 0, slab_tiles), *[([x], 0, GT) for x in rims(summed)]]
         spots = spots_slab(True)
         for chunk in range(chunks):
             parts = []
@@ -684,7 +766,6 @@
     force = pair_forces(spots, segments, block_tiles, bead_at, space_at, neighbour_tiles)
 
     own_out, returned, contracted = [], [], []
-    edge = None
     for chunk in range(chunks):
         last = pair and chunk == chunks - 1
         outs = substeps(
@@ -692,7 +773,7 @@
             expand_l, contract_l, last, contracted[0] if contracted else None,
         )
         if last:
-            *outs, edge = outs
+            *outs, bead_edge, far_edge = outs
         *outs, c16 = outs
         if not pair:
             outs = [outs[0][:, d * beads : (d + 1) * beads] for d in range(bead_count)]
@@ -704,24 +785,38 @@
             back.append(lax.ppermute(outs[d], "bead", on))
         returned.append(back)
 
-    if pair:
-        theirs = lax.ppermute(contracted[-1], "bead", SWAP)
-        straight = lax.ppermute(edge, ("space", "bead"), permutation(lambda b: 1 if b else -1, 0))
-        across = lax.ppermute(
-            edge, ("space", "bead"), permutation(lambda b: 1 if b else -1, 1)
-        )
-        early = [x[0] for x in returned[:-1]]
-        segments = [[x] for x in contracted + early + [theirs, straight, across]]
-        spots = spots_last
-    else:
+    if not pair:
         c16 = jnp.concatenate(contracted, 1) if chunks > 1 else contracted[0]
         everyone = lax.all_gather(c16, "bead", axis=1, tiled=True)
-        segments = [[everyone], *[[x] for x in rims(everyone)]]
-        spots = spots_slab(False)
-    force = pair_forces(spots, segments, slab_tiles, bead_at, space_at, neighbour_tiles)
-
-    parts = [x for chunk in range(chunks) for x in [own_out[chunk]] + returned[chunk]]
-    new_pos, new_mom = finish(chunks, bead_at, parts, finish_left, force)
+        segments = [([everyone], 0, slab_tiles), *[([x], 0, GT) for x in rims(everyone)]]
+        force = pair_forces(
+            spots_slab(False), segments, slab_tiles, bead_at, space_at, neighbour_tiles
+        )
+        parts = [x for chunk in range(chunks) for x in [own_out[chunk]] + returned[chunk]]
+        new_pos, new_mom = finish(chunks, bead_at, parts, finish_left, force)
+        return new_pos.transpose(1, 0, 2), new_mom.transpose(1, 0, 2)
+
+    beside = lax.ppermute(bead_edge, "bead", SWAP)
+    across = lax.ppermute(
+        far_edge, ("space", "bead"), permutation(lambda b: 1 if b else -1, 1)
+    )
+    chunk_tiles = lanes // TILE
+    segments = [([x], 0, chunk_tiles) for x in contracted]
+    inner = pair_forces(
+        spots_inner, segments, block_tiles - 2 * GT, bead_at, space_at, neighbour_tiles
+    )
+    segments = [
+        ([contracted[0]], 0, 2 * GT),
+        ([contracted[-1]], chunk_tiles - 2 * GT, 2 * GT),
+        ([beside], 0, GT),
+        ([across], 0, GT),
+    ]
+    outer = pair_forces(spots_outer, segments, 2 * GT, bead_at, space_at, neighbour_tiles)
+    result = finish_block(bead_at, 0, own_out, finish_left, inner, outer, [])
+    inner = lax.ppermute(inner, "bead", SWAP)
+    outer = lax.ppermute(outer, "bead", SWAP)
+    others = [x[0] for x in returned]
+    new_pos, new_mom = finish_block(bead_at, 1, others, finish_left, inner, outer, result)
     return new_pos.transpose(1, 0, 2), new_mom.transpose(1, 0, 2)
 
 

time: 81.2 us -> 69.9 us (0.86)
  Pallas kernels: 38.5 us -> 29.6 us
  waiting for transfers between devices: 22 us -> 19.8 us
    pallas_call x2 -> x3, Pallas kernels: 16.8 us -> 12.9 us  [pair_forces(): pl.pallas_call(functools.partial(pair_kernel, spots, sizes, own_count), i...]
    ppermute x3 -> x4, waiting for transfers between devices: 9.12 us -> 6.25 us  [the longest x1 4.81 us: body(): beside = lax.ppermute(bead_edge, 'bead', SWAP)]
    pallas_call x2, Pallas kernels: 13.6 us -> 10.8 us  [substeps(): pl.pallas_call(functools.partial(step_kernel, parts, chunk, chunks, lanes...]
    pallas_call x2 -> x3, Pallas kernels: 6.65 us -> 5.24 us  [the longest x2 3.48 us: finish_block(): pl.pallas_call(functools.partial(finish_block_kernel, len(parts)), grid_s...]
    ppermute x3 -> x4, starting transfers between devices: 6.48 us -> 6.08 us  [the longest x1 3.2 us: body(): lax.ppermute(far_edge, ('space', 'bead'), permutation(lambda b: 1 if b el...]
  transfers between devices with their start and end apart: 10 -> 11, of which waited for: 4 -> 5; matrix products, arithmetic and copies ran while one was open for 0% -> 0% of each run, Pallas kernels for 39% -> 37%
where the time goes in v1:
time: 69.9 us; the launch traced here: 69.6 us
  Pallas kernels  29.6 us (42%)
  waiting for transfers between devices  19.8 us (28%)
  starting transfers between devices  17.9 us (26%)
  local copies, waits for them, and re-layouts  1.55 us (2%)
  between operations  0.75 us (1%)
    pallas_call x3, Pallas kernels, pair_forces(): pl.pallas_call(functools.partial(pair_kernel, spots, sizes, own_count), i...  12.9 us
    ppermute x1, waiting for transfers between devices, body(): theirs = lax.ppermute(theirs, 'bead', SWAP)  12 us
    pallas_call x2, Pallas kernels, substeps(): pl.pallas_call(functools.partial(step_kernel, parts, chunk, chunks, lanes...  10.8 us
    ppermute x1, waiting for transfers between devices, body(): beside = lax.ppermute(bead_edge, 'bead', SWAP)  4.81 us
    ppermute x1, starting transfers between devices, body(): lax.ppermute(across, ('space', 'bead'), permutation(lambda b: 1 if b else...  4.58 us
    pallas_call x2, Pallas kernels, finish_block(): pl.pallas_call(functools.partial(finish_block_kernel, len(parts)), grid_s...  3.48 us
    ppermute x1, starting transfers between devices, body(): lax.ppermute(far_edge, ('space', 'bead'), permutation(lambda b: 1 if b el...  3.2 us
    ppermute x2, starting transfers between devices, body(): other = lax.ppermute(blocks[chunks + chunk], 'bead', SWAP)  3.14 us
  transfers between devices with their start and end apart: 11, of which 5 were waited for; matrix products, arithmetic and copies ran while one was open for 0% of the time, Pallas kernels for 37%

profile of v1, /device:TPU:0, one launch (start us, length us, event | category | flops | bytes accessed | tf_op | source)
XLA Modules:
  0.0 69.6 jit_solution(7614222258601489295)
XLA Ops:
  0.6 0.0 copy-start.3
  0.6 0.7 %copy-done.3 = f32[4096]{0:T(1024)S(1)} copy-done((f32[4096]{0:T(1024)S(1)}, f32[4096]{0:T(1024)}, u32[]{:S(2)}) %copy-start.3) | copy-done | bytes 16408
  1.4 0.0 copy-start.7
  1.4 0.8 %copy-done.7 = bf16[2,48,144]{2,1,0:T(8,128)(2,1)S(1)} copy-done((bf16[2,48,144]{2,1,0:T(8,128)(2,1)S(1)}, bf16[2,48,144]{2,1,0:T(8,128)(2,1)}, u32[]{:S(2)}) %copy-start.7) | copy-done | bytes 27672
  2.2 0.0 copy-start.8
  2.2 1.8 %begin.1 = (f32[16,2304]{1,0:T(8,128)S(1)}, f32[16,2304]{1,0:T(8,128)S(1)}, f32[16,256]{1,0:T(8,128)S(1)}, f32[16,256]{1,0:T(8,128)S(1)}, f32[6,16,1024]{2,1,0:T...) custom-call(s32[1]{0:T(128)} %bitcast.bead, ...), custom_call_target="tpu_custom_call" | custom-call | flops 10000000 | bytes 100000 | tf_op jit(solution)/shard_map/begin/pallas_call | solution.py:209
  3.9 3.1 %collective-permute-start = (f32[6,16,1024]{2,1,0:T(8,128)S(1)}, f32[6,16,1024]{2,1,0:T(8,128)S(1)}, u32[]{:S(2)}, u32[]{:S(2)}) collective-permute-start(f32[6,16,1024]{2,1,0:T(8,128)S(1)} %get-tuple-element.25), channel_id=1, source_target_pairs={{0,1},{1,0},{2,3},{3,2},{4,5},{5,4},{6,7},{7,6},{8,9},{9,8},{10,11... | collective-permute-start | bytes 1179656 | tf_op jit(solution)/shard_map/ppermute | solution.py:744
  7.0 0.1 collective-permute-start.4
  7.1 1.9 %collective-permute-start.1 = (f32[16,2304]{1,0:T(8,128)S(1)}, f32[16,2304]{1,0:T(8,128)S(1)}, u32[]{:S(2)}, u32[]{:S(2)}) collective-permute-start(f32[16,2304]{1,0:T(8,128)S(1)} %get-tuple-element.27), channel_id=1, source_target_pairs={{0,1},{1,0},{2,3},{3,2},{4,5},{5,4},{6,7},{7,6},{8,9},{9,8},{10,11... | collective-permute-start | bytes 442376 | tf_op jit(solution)/shard_map/ppermute | solution.py:737
  9.0 0.0 collective-permute-start.2
  9.0 4.6 %collective-permute-start.3 = (f32[16,256]{1,0:T(8,128)S(1)}, f32[16,256]{1,0:T(8,128)S(1)}, u32[]{:S(2)}, u32[]{:S(2)}) collective-permute-start(f32[16,256]{1,0:T(8,128)S(1)} %get-tuple-element.29), channel_id=1, source_target_pairs={{0,31},{1,2},{2,1},{3,4},{4,3},{5,6},{6,5},{7,8},{8,7},{9,10},{10,... | collective-permute-start | bytes 49160 | tf_op jit(solution)/shard_map/ppermute | solution.py:741
  13.6 0.0 copy-done.8
  13.6 0.0 copy-done.9
  13.6 0.7 prepare.1
  14.3 0.0 copy-start.10
  14.3 0.6 collective-permute-done.2.refs_2_
  14.9 1.0 %collective-permute-done.3.refs_3_ = f32[16,256]{1,0:T(8,128)S(1)} collective-permute-done((f32[16,256]{1,0:T(8,128)S(1)}, f32[16,256]{1,0:T(8,128)S(1)}, u32[]{:S(2)}, u32[]{:S(2)}) %collective-permute-start.3) | collective-permute-done | bytes 16416 | tf_op jit(solution)/shard_map/ppermute | solution.py:741
  15.9 12.0 %collective-permute-done.1.refs_1_ = f32[16,2304]{1,0:T(8,128)S(1)} collective-permute-done((f32[16,2304]{1,0:T(8,128)S(1)}, f32[16,2304]{1,0:T(8,128)S(1)}, u32[]{:S(2)}, u32[]{:S(2)}) %collective-permute-start.1) | collective-permute-done | bytes 147488 | tf_op jit(solution)/shard_map/ppermute | solution.py:737
  27.9 0.0 copy-done.10
  27.9 0.0 copy-start.5
  27.9 0.0 copy-start.6
  27.9 5.9 %pair_forces.3.refs_2_ = f32[16,2048]{1,0:T(8,128)S(1)} custom-call(s32[1]{0:T(128)} %bitcast.bead, s32[1]{0:T(128)} %bitcast.1.space, s32[3,32]{1,0:T(4,128)S(1)} %copy-done.10, f32[16,2304]{1,0:T(8,128)S(1)} %get-tuple-element.26.refs_0_, f32[16,2304]{1,0:T(8,128)S(1)} %collective-permute-done.1.refs_1_, f32[16,256]{1,0:T(8,128)S(1)} %collective-permute-done.2.refs_2_, ...), custom_call_target="tpu_custom_call" | custom-call | flops 10000000 | bytes 100000 | tf_op jit(solution)/shard_map/pair_forces/pallas_call | solution.py:405
  33.8 0.0 collective-permute-done.refs_1_
  33.8 0.0 copy-done
  33.8 0.0 copy-done.1
  33.8 0.0 copy-done.4
  33.8 0.0 copy-done.5
  33.8 0.0 copy-done.6
  33.8 5.4 %substeps.2 = (f32[6,16,1024]{2,1,0:T(8,128)S(1)}, f32[6,16,1024]{2,1,0:T(8,128)S(1)}, f32[16,1024]{1,0:T(8,128)S(1)}) custom-call(s32[1]{0:T(128)} %bitcast.bead, f32[6,16,1024]{2,1,0:T(8,128)S(1)} %get-tuple-element.24.refs_0_, f32[6,16,1024]{2,1,0:T(8,128)S(1)} %collective-permute-done.refs_1_, f32[16,2048]{1,0:T(8,128)S(1)} %pair_forces.3.refs_2_, ...), custom_call_target="tpu_custom_call" | custom-call | flops 10000000 | bytes 100000 | tf_op jit(solution)/shard_map/substeps/pallas_call | solution.py:526
  39.2 2.0 %collective-permute-start.9 = (f32[6,16,1024]{2,1,0:T(8,128)S(1)}, f32[6,16,1024]{2,1,0:T(8,128)S(1)}, u32[]{:S(2)}, u32[]{:S(2)}) collective-permute-start(f32[6,16,1024]{2,1,0:T(8,128)S(1)} %get-tuple-element.38), channel_id=1, source_target_pairs={{0,1},{1,0},{2,3},{3,2},{4,5},{5,4},{6,7},{7,6},{8,9},{9,8},{10,11... | collective-permute-start | bytes 1179656 | tf_op jit(solution)/shard_map/ppermute | solution.py:785
  41.2 0.0 collective-permute-done.4.refs_1_
  41.2 5.4 %substeps.3 = (f32[6,16,1024]{2,1,0:T(8,128)S(1)}, f32[6,16,1024]{2,1,0:T(8,128)S(1)}, f32[16,1024]{1,0:T(8,128)S(1)}, f32[16,256]{1,0:T(8,128)S(1)}, f32[16,256]{1,0:T(8,128)S(1)}) custom-call(s32[1]{0:T(128)} %bitcast.bead, f32[6,16,1024]{2,1,0:T(8,128)S(1)} %get-tuple-element.33.refs_0_, f32[6,16,1024]{2,1,0:T(8,128)S(1)} %collective-permute-done.4.refs_1_, ...), custom_call_target="tpu_custom_call" | custom-call | flops 10000000 | bytes 100000 | tf_op jit(solution)/shard_map/substeps/pallas_call | solution.py:526
  46.6 0.1 collective-permute-start.10
  46.7 4.7 %pair_forces.4.inner = f32[16,1536]{1,0:T(8,128)S(1)} custom-call(s32[1]{0:T(128)} %bitcast.bead, s32[1]{0:T(128)} %bitcast.1.space, s32[3,32]{1,0:T(4,128)S(1)} %copy-done.10, f32[16,1024]{1,0:T(8,128)S(1)} %get-tuple-element.32.refs_10_.refs_0_, f32[16,1024]{1,0:T(8,128)S(1)} %get-tuple-element.35.refs_1_), custom_call_target="tpu_custom_call" | custom-call | flops 10000000 | bytes 100000 | tf_op jit(solution)/shard_map/pair_forces/pallas_call | solution.py:405
  51.4 2.0 %collective-permute-start.5 = (f32[16,1536]{1,0:T(8,128)S(1)}, f32[16,1536]{1,0:T(8,128)S(1)}, u32[]{:S(2)}, u32[]{:S(2)}) collective-permute-start(f32[16,1536]{1,0:T(8,128)S(1)} %pair_forces.4.inner), channel_id=1, source_target_pairs={{0,1},{1,0},{2,3},{3,2},{4,5},{5,4},{6,7},{7,6},{8,9},{9,8},{10,11... | collective-permute-start | bytes 294920 | tf_op jit(solution)/shard_map/ppermute | solution.py:816
  53.4 0.1 collective-permute-start.6
  53.5 3.2 %collective-permute-start.7 = (f32[16,256]{1,0:T(8,128)S(1)}, f32[16,256]{1,0:T(8,128)S(1)}, u32[]{:S(2)}, u32[]{:S(2)}) collective-permute-start(f32[16,256]{1,0:T(8,128)S(1)} %get-tuple-element.37), channel_id=1, source_target_pairs={{0,31},{1,2},{2,1},{3,4},{4,3},{5,6},{6,5},{7,8},{8,7},{9,10},{10,... | collective-permute-start | bytes 49160 | tf_op jit(solution)/shard_map/ppermute | solution.py:800
  56.7 4.8 %collective-permute-done.6.refs_2_ = f32[16,256]{1,0:T(8,128)S(1)} collective-permute-done((f32[16,256]{1,0:T(8,128)S(1)}, f32[16,256]{1,0:T(8,128)S(1)}, u32[]{:S(2)}, u32[]{:S(2)}) %collective-permute-start.6) | collective-permute-done | bytes 16416 | tf_op jit(solution)/shard_map/ppermute | solution.py:799
  61.5 0.0 collective-permute-done.7.refs_3_
  61.5 2.4 %pair_forces.5.outer = f32[16,512]{1,0:T(8,128)S(1)} custom-call(s32[1]{0:T(128)} %bitcast.bead, s32[1]{0:T(128)} %bitcast.1.space, s32[3,32]{1,0:T(4,128)S(1)} %copy-done.10, f32[16,1024]{1,0:T(8,128)S(1)} %get-tuple-element.32.refs_10_.refs_0_, f32[16,1024]{1,0:T(8,128)S(1)} %get-tuple-element.35.refs_1_, f32[16,256]{1,0:T(8,128)S(1)} %collective-permute-done.6.refs_2_, ...), custom_call_target="tpu_custom_call" | custom-call | flops 10000000 | bytes 100000 | tf_op jit(solution)/shard_map/pair_forces/pallas_call | solution.py:405
  63.9 0.8 %collective-permute-start.8 = (f32[16,512]{1,0:T(8,128)S(1)}, f32[16,512]{1,0:T(8,128)S(1)}, u32[]{:S(2)}, u32[]{:S(2)}) collective-permute-start(f32[16,512]{1,0:T(8,128)S(1)} %pair_forces.5.outer), channel_id=1, source_target_pairs={{0,1},{1,0},{2,3},{3,2},{4,5},{5,4},{6,7},{7,6},{8,9},{9,8},{10,11... | collective-permute-start | bytes 98312 | tf_op jit(solution)/shard_map/ppermute | solution.py:817
  64.7 0.0 copy-done.2
  64.7 1.7 %finish_block.2 = (f32[3,16,4096]{2,1,0:T(8,128)}, f32[3,16,4096]{2,1,0:T(8,128)}) custom-call(s32[1]{0:T(128)} %bitcast.bead, bf16[2,3,48,48]{3,2,1,0:T(8,128)(2,1)S(1)} %copy-done.2, f32[16,1536]{1,0:T(8,128)S(1)} %pair_forces.4.inner, f32[16,512]{1,0:T(8,128)S(1)} %pair_forces.5.outer, f32[6,16,1024]{2,1,0:T(8,128)S(1)} %get-tuple-element.40.refs_0_, ...), custom_call_target="tpu_custom_call" | custom-call | flops 10000000 | bytes 100000 | tf_op jit(solution)/shard_map/finish_block/pallas_call | solution.py:608
  66.4 1.4 %collective-permute-done.8.outer = f32[16,512]{1,0:T(8,128)S(1)} collective-permute-done((f32[16,512]{1,0:T(8,128)S(1)}, f32[16,512]{1,0:T(8,128)S(1)}, u32[]{:S(2)}, u32[]{:S(2)}) %collective-permute-start.8) | collective-permute-done | bytes 32800 | tf_op jit(solution)/shard_map/ppermute | solution.py:817
  67.9 0.0 collective-permute-done.5.inner
  67.9 0.0 collective-permute-done.9.refs_0_
  67.9 0.0 collective-permute-done.10.refs_1_
  67.9 1.8 %finish_block.3 = (f32[3,16,4096]{2,1,0:T(8,128)}, f32[3,16,4096]{2,1,0:T(8,128)}) custom-call(s32[1]{0:T(128)} %bitcast.bead, bf16[2,3,48,48]{3,2,1,0:T(8,128)(2,1)S(1)} %copy-done.2, f32[16,1536]{1,0:T(8,128)S(1)} %collective-permute-done.5.inner, f32[16,512]{1,0:T(8,128)S(1)} %collective-permute-done.8.outer, ...), custom_call_target="tpu_custom_call", output_to_operand_aliasing={{0}: (6, {}), {1}: (7, {})} | custom-call | flops 10000000 | bytes 100000 | tf_op jit(solution)/shard_map/finish_block/pallas_call | solution.py:608
  (5 shorter events, 0.0 us)
Async XLA Ops:
  0.6 0.7 %copy-start.3 = (f32[4096]{0:T(1024)S(1)}, f32[4096]{0:T(1024)}, u32[]{:S(2)}) copy-start(f32[4096]{0:T(1024)} %param.15) | copy-start | bytes 49156
  1.4 0.8 %copy-start.7 = (bf16[2,48,144]{2,1,0:T(8,128)(2,1)S(1)}, bf16[2,48,144]{2,1,0:T(8,128)(2,1)}, u32[]{:S(2)}) copy-start(bf16[2,48,144]{2,1,0:T(8,128)(2,1)} %constant.18.clone.left) | copy-start | bytes 82948
  2.2 11.4 %copy-start.8 = (s32[2,4096]{1,0:T(2,128)S(1)}, s32[2,4096]{1,0:T(2,128)}, u32[]{:S(2)}) copy-start(s32[2,4096]{1,0:T(2,128)} %bonds.1) | copy-start | bytes 98308
  2.2 11.4 %copy-start.9 = (s32[3,2048]{1,0:T(4,128)S(1)}, s32[3,2048]{1,0:T(4,128)}, u32[]{:S(2)}) copy-start(s32[3,2048]{1,0:T(4,128)} %angles.1) | copy-start | bytes 73732
  3.9 29.9 %collective-permute-start = (f32[6,16,1024]{2,1,0:T(8,128)S(1)}, f32[6,16,1024]{2,1,0:T(8,128)S(1)}, u32[]{:S(2)}, u32[]{:S(2)}) collective-permute-start(f32[6,16,1024]{2,1,0:T(8,128)S(1)} %get-tuple-element.25), channel_id=1, source_target_pairs={{0,1},{1,0},{2,3},{3,2},{4,5},{5,4},{6,7},{7,6},{8,9},{9,8},{10,11... | collective-permute-start | bytes 1179656 | tf_op jit(solution)/shard_map/ppermute | solution.py:744
  7.0 34.2 %collective-permute-start.4 = (f32[6,16,1024]{2,1,0:T(8,128)S(1)}, f32[6,16,1024]{2,1,0:T(8,128)S(1)}, u32[]{:S(2)}, u32[]{:S(2)}) collective-permute-start(f32[6,16,1024]{2,1,0:T(8,128)S(1)} %get-tuple-element.34), channel_id=1, source_target_pairs={{0,1},{1,0},{2,3},{3,2},{4,5},{5,4},{6,7},{7,6},{8,9},{9,8},{10,11... | collective-permute-start | bytes 1179656 | tf_op jit(solution)/shard_map/ppermute | solution.py:744
  7.1 20.8 %collective-permute-start.1 = (f32[16,2304]{1,0:T(8,128)S(1)}, f32[16,2304]{1,0:T(8,128)S(1)}, u32[]{:S(2)}, u32[]{:S(2)}) collective-permute-start(f32[16,2304]{1,0:T(8,128)S(1)} %get-tuple-element.27), channel_id=1, source_target_pairs={{0,1},{1,0},{2,3},{3,2},{4,5},{5,4},{6,7},{7,6},{8,9},{9,8},{10,11... | collective-permute-start | bytes 442376 | tf_op jit(solution)/shard_map/ppermute | solution.py:737
  9.0 5.9 %collective-permute-start.2 = (f32[16,256]{1,0:T(8,128)S(1)}, f32[16,256]{1,0:T(8,128)S(1)}, u32[]{:S(2)}, u32[]{:S(2)}) collective-permute-start(f32[16,256]{1,0:T(8,128)S(1)} %get-tuple-element.28), channel_id=1, source_target_pairs={{0,2},{1,31},{2,4},{3,1},{4,6},{5,3},{6,8},{7,5},{8,10},{9,7},{10,... | collective-permute-start | bytes 49160 | tf_op jit(solution)/shard_map/ppermute | solution.py:738
  9.0 6.9 %collective-permute-start.3 = (f32[16,256]{1,0:T(8,128)S(1)}, f32[16,256]{1,0:T(8,128)S(1)}, u32[]{:S(2)}, u32[]{:S(2)}) collective-permute-start(f32[16,256]{1,0:T(8,128)S(1)} %get-tuple-element.29), channel_id=1, source_target_pairs={{0,31},{1,2},{2,1},{3,4},{4,3},{5,6},{6,5},{7,8},{8,7},{9,10},{10,... | collective-permute-start | bytes 49160 | tf_op jit(solution)/shard_map/ppermute | solution.py:741
  14.3 13.6 %copy-start.10 = (s32[3,32]{1,0:T(4,128)S(1)}, s32[3,32]{1,0:T(4,128)}, u32[]{:S(2)}) copy-start(s32[3,32]{1,0:T(4,128)} %nbr.5) | copy-start | bytes 1156
  27.9 5.9 %copy-start = (bf16[2,288,48]{2,1,0:T(8,128)(2,1)S(1)}, bf16[2,288,48]{2,1,0:T(8,128)(2,1)}, u32[]{:S(2)}) copy-start(bf16[2,288,48]{2,1,0:T(8,128)(2,1)} %constant.21.clone.refs_8_) | copy-start | bytes 165892
  27.9 5.9 %copy-start.1 = (bf16[192,192]{1,0:T(8,128)(2,1)S(1)}, bf16[192,192]{1,0:T(8,128)(2,1)}, u32[]{:S(2)}) copy-start(bf16[192,192]{1,0:T(8,128)(2,1)} %constant.22.clone.refs_7_) | copy-start | bytes 221188
  27.9 5.9 %copy-start.4 = (f32[4096]{0:T(1024)S(1)}, f32[4096]{0:T(1024)}, u32[]{:S(2)}) copy-start(f32[4096]{0:T(1024)} %param.15) | copy-start | bytes 49156
  27.9 5.9 %copy-start.5 = (bf16[2,32,192]{2,1,0:T(8,128)(2,1)S(1)}, bf16[2,32,192]{2,1,0:T(8,128)(2,1)}, u32[]{:S(2)}) copy-start(bf16[2,32,192]{2,1,0:T(8,128)(2,1)} %constant.20.clone.refs_9_) | copy-start | bytes 73732
  27.9 5.9 %copy-start.6 = (f32[4096]{0:T(1024)S(1)}, f32[4096]{0:T(1024)}, u32[]{:S(2)}) copy-start(f32[4096]{0:T(1024)} %param.14) | copy-start | bytes 49156
  39.2 28.6 %collective-permute-start.9 = (f32[6,16,1024]{2,1,0:T(8,128)S(1)}, f32[6,16,1024]{2,1,0:T(8,128)S(1)}, u32[]{:S(2)}, u32[]{:S(2)}) collective-permute-start(f32[6,16,1024]{2,1,0:T(8,128)S(1)} %get-tuple-element.38), channel_id=1, source_target_pairs={{0,1},{1,0},{2,3},{3,2},{4,5},{5,4},{6,7},{7,6},{8,9},{9,8},{10,11... | collective-permute-start | bytes 1179656 | tf_op jit(solution)/shard_map/ppermute | solution.py:785
  46.6 21.3 %collective-permute-start.10 = (f32[6,16,1024]{2,1,0:T(8,128)S(1)}, f32[6,16,1024]{2,1,0:T(8,128)S(1)}, u32[]{:S(2)}, u32[]{:S(2)}) collective-permute-start(f32[6,16,1024]{2,1,0:T(8,128)S(1)} %get-tuple-element.39), channel_id=1, source_target_pairs={{0,1},{1,0},{2,3},{3,2},{4,5},{5,4},{6,7},{7,6},{8,9},{9,8},{10,11... | collective-permute-start | bytes 1179656 | tf_op jit(solution)/shard_map/ppermute | solution.py:785
  51.4 16.4 %collective-permute-start.5 = (f32[16,1536]{1,0:T(8,128)S(1)}, f32[16,1536]{1,0:T(8,128)S(1)}, u32[]{:S(2)}, u32[]{:S(2)}) collective-permute-start(f32[16,1536]{1,0:T(8,128)S(1)} %pair_forces.4.inner), channel_id=1, source_target_pairs={{0,1},{1,0},{2,3},{3,2},{4,5},{5,4},{6,7},{7,6},{8,9},{9,8},{10,11... | collective-permute-start | bytes 294920 | tf_op jit(solution)/shard_map/ppermute | solution.py:816
  53.4 8.1 %collective-permute-start.6 = (f32[16,256]{1,0:T(8,128)S(1)}, f32[16,256]{1,0:T(8,128)S(1)}, u32[]{:S(2)}, u32[]{:S(2)}) collective-permute-start(f32[16,256]{1,0:T(8,128)S(1)} %get-tuple-element.36), channel_id=1, source_target_pairs={{0,1},{1,0},{2,3},{3,2},{4,5},{5,4},{6,7},{7,6},{8,9},{9,8},{10,11... | collective-permute-start | bytes 49160 | tf_op jit(solution)/shard_map/ppermute | solution.py:799
  53.5 11.2 %copy-start.2 = (bf16[2,3,48,48]{3,2,1,0:T(8,128)(2,1)S(1)}, bf16[2,3,48,48]{3,2,1,0:T(8,128)(2,1)}, u32[]{:S(2)}) copy-start(bf16[2,3,48,48]{3,2,1,0:T(8,128)(2,1)} %constant.19.clone.expand) | copy-start | bytes 82948
  53.5 8.0 %collective-permute-start.7 = (f32[16,256]{1,0:T(8,128)S(1)}, f32[16,256]{1,0:T(8,128)S(1)}, u32[]{:S(2)}, u32[]{:S(2)}) collective-permute-start(f32[16,256]{1,0:T(8,128)S(1)} %get-tuple-element.37), channel_id=1, source_target_pairs={{0,31},{1,2},{2,1},{3,4},{4,3},{5,6},{6,5},{7,8},{8,7},{9,10},{10,... | collective-permute-start | bytes 49160 | tf_op jit(solution)/shard_map/ppermute | solution.py:800
  63.9 4.0 %collective-permute-start.8 = (f32[16,512]{1,0:T(8,128)S(1)}, f32[16,512]{1,0:T(8,128)S(1)}, u32[]{:S(2)}, u32[]{:S(2)}) collective-permute-start(f32[16,512]{1,0:T(8,128)S(1)} %pair_forces.5.outer), channel_id=1, source_target_pairs={{0,1},{1,0},{2,3},{3,2},{4,5},{5,4},{6,7},{7,6},{8,9},{9,8},{10,11... | collective-permute-start | bytes 98312 | tf_op jit(solution)/shard_map/ppermute | solution.py:817

commit v2 on v1

--- a/solution.py
+++ b/solution.py
@@ -154,9 +154,9 @@
 
 
 def begin_kernel(chunks, bead, left, strengths, pos, mom, *refs):
-    mine, theirs, straight, across = refs[:4]
-    blocks = refs[4:-2]
-    whole, sems = refs[-2:]
+    mine, theirs, straight = refs[:3]
+    blocks = refs[3:-4]
+    whole, table, rows, sems = refs[-4:]
     lanes = blocks[0].shape[2]
     slab = whole.shape[1]
     starts, copies = [], []
@@ -172,8 +172,15 @@
             )
             copy.start()
             copies.append(copy)
-    table = left[bead[0]]
-    logs = math.log2(math.e) * jnp.log(strengths[...])
+    small = [
+        pltpu.make_async_copy(left.at[bead[0]], table, sems.at[len(copies)]),
+        pltpu.make_async_copy(strengths, rows, sems.at[len(copies) + 1]),
+    ]
+    for copy in small:
+        copy.start()
+    for copy in small:
+        copy.wait()
+    logs = math.log2(math.e) * jnp.log(rows[...])
     for t in range(slab // TILE):
         whole[0:1, t * TILE : (t + 1) * TILE] = logs[t : t + 1]
     for i, block in enumerate(blocks):
@@ -181,7 +188,7 @@
         x = jnp.concatenate([block[c] for c in range(3)], axis=0)
         where = pl.ds(starts[i], lanes)
         row = lax.broadcasted_iota(jnp.int32, (ROWS, lanes), 0)
-        whole[:, where] = jnp.where(row == 0, whole[:, where], exact(table, x))
+        whole[:, where] = jnp.where(row == 0, whole[:, where], exact(table[...], x))
 
     block, rim = slab // 2, GT * TILE
     size = block + rim
@@ -189,10 +196,10 @@
     def sides(which):
         first, other = (0, block - rim) if which == 0 else (block - rim, 0)
         mine[...] = whole[:, first : first + size]
-        theirs[...] = whole[:, other : other + size]
+        theirs[:, :size] = whole[:, other : other + size]
         head, tail = whole[:, :rim], whole[:, slab - rim :]
         straight[...] = tail if which == 0 else head
-        across[...] = head if which == 0 else tail
+        theirs[:, size:] = head if which == 0 else tail
 
     for which in range(2):
         pl.when(bead[0] == which)(functools.partial(sides, which))
@@ -204,21 +211,23 @@
     beads, slab = pos.shape[1:]
     block, rim = slab // 2, GT * TILE
     lanes = block // chunks
-    shapes = [(ROWS, block + rim)] * 2 + [(ROWS, rim)] * 2
+    shapes = [(ROWS, block + rim), (ROWS, block + 2 * rim), (ROWS, rim)]
     shapes += [(6, beads, lanes)] * (2 * chunks)
     return pl.pallas_call(
         functools.partial(begin_kernel, chunks),
-        in_specs=[IN_SMEM, IN_VMEM, IN_VMEM] + [pl.BlockSpec(memory_space=pl.ANY)] * 2,
+        in_specs=[IN_SMEM] + [pl.BlockSpec(memory_space=pl.ANY)] * 4,
         out_specs=[IN_VMEM] * len(shapes),
         out_shape=[vmem_out(s, F32) for s in shapes],
         scratch_shapes=[
             pltpu.VMEM((ROWS, slab), F32),
-            pltpu.SemaphoreType.DMA((4 * chunks,)),
+            pltpu.VMEM(left.shape[1:], left.dtype),
+            pltpu.VMEM(strengths.shape, F32),
+            pltpu.SemaphoreType.DMA((4 * chunks + 2,)),
         ],
         compiler_params=PARAMS,
         cost_estimate=COST,
         name="begin",
-    )(bead, left, strengths, far(pos), far(mom))
+    )(bead, far(left), far(strengths), far(pos), far(mom))
 
 
 def partial_kernel(bead, left, strengths, pos, out):
@@ -418,7 +427,7 @@
         compiler_params=PARAMS,
         cost_estimate=COST,
         name="pair_forces",
-    )(bead, space, neighbour_tiles, *[near(x) for x in flat])
+    )(bead, space, far(neighbour_tiles), *[near(x) for x in flat])
 
 
 def step_kernel(parts, chunk, chunks, group, edge, bead, *refs):
@@ -576,44 +585,61 @@
     )(bead, expand, near(force), *[near(x) for x in parts])
 
 
-def finish_block_kernel(chunks, bead, expand, inner, outer, *refs):
-    parts = refs[:chunks]
-    pos, mom = refs[-2:]
+def finish_block_kernel(chunks, owner, moves, count, bead, expand, inner, outer, *refs):
+    parts = refs[:count]
+    pos, mom, held, sems = refs[-4:]
     lanes = parts[0].shape[2]
     rim = GT * TILE
-    comp = pl.program_id(0)
+    blocks = [bead[0], 1 - bead[0]]
+
+    def where(owner, chunk):
+        return pl.ds(pl.multiple_of((blocks[owner] * chunks + chunk) * lanes, TILE), lanes)
+
+    copies = []
+
+    def copy(source, target):
+        copies.append(pltpu.make_async_copy(source, target, sems.at[len(copies)]))
+        copies[-1].start()
+
+    for part, move_owner, chunk in moves:
+        copy(parts[part].at[pl.ds(0, 3)], pos.at[:, :, where(move_owner, chunk)])
     force = jnp.concatenate([outer[:, :rim], inner[...], outer[:, rim:]], axis=1)
-    kick = 0.5 * time_step * exact(expand[bead[0], comp], force)
-    for chunk, part in enumerate(parts):
-        where = slice(chunk * lanes, (chunk + 1) * lanes)
-        pos[0, :, where] = part[comp]
-        mom[0, :, where] = part[3 + comp] + kick[:, where]
-
-
-def finish_block(bead, distance, parts, expand, inner, outer, before):
+    for chunk in range(chunks):
+        lane = slice(chunk * lanes, (chunk + 1) * lanes)
+        for c in range(3):
+            kick = 0.5 * time_step * exact(expand[bead[0], c], force[:, lane])
+            held[c, :, lane] = parts[chunk][3 + c] + kick
+        copy(held.at[:, :, pl.ds(chunk * lanes, lanes)], mom.at[:, :, where(owner, chunk)])
+    for waiting in copies:
+        waiting.wait()
+
+
+def finish_block(chunks, owner, moves, bead, parts, expand, inner, outer, before):
     beads, lanes = parts[0].shape[1:]
-    block = lanes * len(parts)
-    anywhere = [pl.BlockSpec(memory_space=pl.ANY)] * len(before)
-    whole = pl.BlockSpec(memory_space=pltpu.VMEM)
-    grid_spec = pltpu.PrefetchScalarGridSpec(
-        num_scalar_prefetch=1,
-        grid=(3,),
-        in_specs=[whole] * (3 + len(parts)) + anywhere,
-        out_specs=[
-            pl.BlockSpec((1, beads, block), lambda i, b: (i, 0, lax.rem(b[0] + distance, 2)))
-        ]
-        * 2,
-    )
+    block = lanes * chunks
+    anywhere = pl.BlockSpec(memory_space=pl.ANY)
     at = 4 + len(parts)
     return pl.pallas_call(
-        functools.partial(finish_block_kernel, len(parts)),
-        grid_spec=grid_spec,
-        out_shape=[jax.ShapeDtypeStruct((3, beads, 2 * block), F32)] * 2,
+        functools.partial(finish_block_kernel, chunks, owner, moves, len(parts)),
+        in_specs=[IN_SMEM] + [IN_VMEM] * (3 + len(parts)) + [anywhere] * len(before),
+        out_specs=[anywhere] * 2,
+        out_shape=[pltpu.MemorySpace.HBM((3, beads, 2 * block), F32)] * 2,
+        scratch_shapes=[
+            pltpu.VMEM((3, beads, block), F32),
+            pltpu.SemaphoreType.DMA((len(moves) + chunks,)),
+        ],
         input_output_aliases={at + i: i for i in range(len(before))},
         compiler_params=PARAMS,
         cost_estimate=COST,
         name="finish_block",
-    )(bead, expand, near(inner), near(outer), *[near(x) for x in parts], *before)
+    )(
+        bead,
+        expand,
+        near(inner),
+        near(outer),
+        *[near(x) for x in parts],
+        *[far(x) for x in before],
+    )
 
 
 def body(positions, momenta, masses, strengths, bond_ends, angle_ends, neighbour_tiles):
@@ -731,18 +757,20 @@
 
     pieces = [[] for _ in range(chunks)]
     if pair:
-        mine, theirs, straight, across, *blocks = begin(
+        mine, theirs, straight, *blocks = begin(
             chunks, bead_at, begin_left, strength, pos, mom
         )
         theirs = lax.ppermute(theirs, "bead", SWAP)
+        for chunk in range(chunks):
+            other = lax.ppermute(blocks[chunks + chunk], "bead", SWAP)
+            pieces[chunk] = [blocks[chunk], other]
+        more = theirs[:, block + rim :]
+        row = lax.broadcasted_iota(jnp.int32, more.shape, 0)
+        straight = straight + jnp.where(row == 0, 0.0, more)
         straight = lax.ppermute(
             straight, ("space", "bead"), permutation(lambda b: -1 if b else 1, 0)
         )
-        across = lax.ppermute(across, ("space", "bead"), permutation(lambda b: 1 if b else -1, 1))
-        segments = [([mine, theirs], 0, block_tiles + GT), ([straight, across], 0, GT)]
-        for chunk in range(chunks):
-            other = lax.ppermute(blocks[chunks + chunk], "bead", SWAP)
-            pieces[chunk] = [blocks[chunk], other]
+        segments = [([mine, theirs], 0, block_tiles + GT), ([straight], 0, GT)]
         spots = spots_first
     else:
         part = partial_rows(bead_at, begin_left, strength, pos)
@@ -812,11 +840,18 @@
         ([across], 0, GT),
     ]
     outer = pair_forces(spots_outer, segments, 2 * GT, bead_at, space_at, neighbour_tiles)
-    result = finish_block(bead_at, 0, own_out, finish_left, inner, outer, [])
+    others = [x[0] for x in returned]
+    moves = [(i, 0, i) for i in range(chunks)]
+    moves += [(chunks + i, 1, i) for i in range(chunks - 1)]
+    result = finish_block(
+        chunks, 0, moves, bead_at, own_out + others[:-1], finish_left, inner, outer, []
+    )
     inner = lax.ppermute(inner, "bead", SWAP)
     outer = lax.ppermute(outer, "bead", SWAP)
-    others = [x[0] for x in returned]
-    new_pos, new_mom = finish_block(bead_at, 1, others, finish_left, inner, outer, result)
+    moves = [(chunks - 1, 1, chunks - 1)]
+    new_pos, new_mom = finish_block(
+        chunks, 1, moves, bead_at, others, finish_left, inner, outer, result
+    )
     return new_pos.transpose(1, 0, 2), new_mom.transpose(1, 0, 2)
 
 

time: 69.9 us -> 57.5 us (0.82)
  starting transfers between devices: 17.9 us -> 12.3 us
  waiting for transfers between devices: 19.8 us -> 14.8 us
  local copies, waits for them, and re-layouts: 1.55 us -> 0.04 us
    ppermute x1, waiting for transfers between devices: 12 us -> 3.02 us  [body(): theirs = lax.ppermute(theirs, 'bead', SWAP)]
    ppermute x1 -> x0, starting transfers between devices: 4.58 us -> none  [body(): lax.ppermute(across, ('space', 'bead'), permutation(lambda b: 1 if b else...]
    ppermute x1, waiting for transfers between devices: 0.6 us -> 5.17 us  [body(): lax.ppermute(straight, ('space', 'bead'), permutation(lambda b: -1 if b e...]
    ppermute x1, starting transfers between devices: 0.09 us -> 1.99 us  [body(): beside = lax.ppermute(bead_edge, 'bead', SWAP)]
    ppermute x1, starting transfers between devices: 2 us -> 0.1 us  [body(): inner = lax.ppermute(inner, 'bead', SWAP)]
    ppermute x1, waiting for transfers between devices: 4.81 us -> 2.98 us  [body(): beside = lax.ppermute(bead_edge, 'bead', SWAP)]
    unnamed x22 -> x16, local copies, waits for them, and re-layouts: 1.55 us -> 0.04 us
    ppermute x1, waiting for transfers between devices: 0.01 us -> 1.45 us  [body(): lax.ppermute(far_edge, ('space', 'bead'), permutation(lambda b: 1 if b el...]
  transfers between devices with their start and end apart: 11 -> 10, of which waited for: 5 -> 5; matrix products, arithmetic and copies ran while one was open for 0% -> 0% of each run, Pallas kernels for 37% -> 45%
where the time goes in v2:
time: 57.5 us; the launch traced here: 57.2 us
  Pallas kernels  29.2 us (51%)
  waiting for transfers between devices  14.8 us (26%)
  starting transfers between devices  12.3 us (21%)
  between operations  0.77 us (1%)
    pallas_call x3, Pallas kernels, pair_forces(): pl.pallas_call(functools.partial(pair_kernel, spots, sizes, own_count), i...  13.4 us
    pallas_call x2, Pallas kernels, substeps(): pl.pallas_call(functools.partial(step_kernel, parts, chunk, chunks, lanes...  10.8 us
    ppermute x1, waiting for transfers between devices, body(): lax.ppermute(straight, ('space', 'bead'), permutation(lambda b: -1 if b e...  5.17 us
    ppermute x1, starting transfers between devices, body(): theirs = lax.ppermute(theirs, 'bead', SWAP)  3.07 us
    ppermute x1, waiting for transfers between devices, body(): theirs = lax.ppermute(theirs, 'bead', SWAP)  3.02 us
    ppermute x1, waiting for transfers between devices, body(): beside = lax.ppermute(bead_edge, 'bead', SWAP)  2.98 us
    ppermute x1, starting transfers between devices, body(): lax.ppermute(far_edge, ('space', 'bead'), permutation(lambda b: 1 if b el...  2.32 us
    pallas_call x1, Pallas kernels, begin(): pl.pallas_call(functools.partial(begin_kernel, chunks), in_specs=[IN_SMEM...  2.2 us
  transfers between devices with their start and end apart: 10, of which 5 were waited for; matrix products, arithmetic and copies ran while one was open for 0% of the time, Pallas kernels for 45%

profile of v2, /device:TPU:0, one launch (start us, length us, event | category | flops | bytes accessed | tf_op | source)
XLA Modules:
  0.0 57.2 jit_solution(15253226025198552374)
XLA Ops:
  0.6 0.0 copy-start.7
  0.6 2.2 %begin.1 = (f32[16,2304]{1,0:T(8,128)S(1)}, f32[16,2560]{1,0:T(8,128)S(1)}, f32[16,256]{1,0:T(8,128)S(1)}, f32[6,16,1024]{2,1,0:T(8,128)S(1)}, f32[6,16,1024]{2,...) custom-call(s32[1]{0:T(128)} %bitcast.bead, bf16[2,48,144]{2,1,0:T(8,128)(2,1)} %constant.22.clone.left, ...), custom_call_target="tpu_custom_call" | custom-call | flops 10000000 | bytes 100000 | tf_op jit(solution)/shard_map/begin/pallas_call | solution.py:216
  2.9 0.0 copy-start.6
  2.9 3.1 %collective-permute-start.1 = (f32[16,2560]{1,0:T(8,128)S(1)}, f32[16,2560]{1,0:T(8,128)S(1)}, u32[]{:S(2)}, u32[]{:S(2)}) collective-permute-start(f32[16,2560]{1,0:T(8,128)S(1)} %get-tuple-element.26), channel_id=1, source_target_pairs={{0,1},{1,0},{2,3},{3,2},{4,5},{5,4},{6,7},{7,6},{8,9},{9,8},{10,11... | collective-permute-start | bytes 491528 | tf_op jit(solution)/shard_map/ppermute | solution.py:763
  5.9 0.1 collective-permute-start
  6.0 1.9 %collective-permute-start.3 = (f32[6,16,1024]{2,1,0:T(8,128)S(1)}, f32[6,16,1024]{2,1,0:T(8,128)S(1)}, u32[]{:S(2)}, u32[]{:S(2)}) collective-permute-start(f32[6,16,1024]{2,1,0:T(8,128)S(1)} %get-tuple-element.32), channel_id=1, source_target_pairs={{0,1},{1,0},{2,3},{3,2},{4,5},{5,4},{6,7},{7,6},{8,9},{9,8},{10,11... | collective-permute-start | bytes 1179656 | tf_op jit(solution)/shard_map/ppermute | solution.py:765
  8.0 3.0 %collective-permute-done.1.refs_1_ = f32[16,2560]{1,0:T(8,128)S(1)} collective-permute-done((f32[16,2560]{1,0:T(8,128)S(1)}, f32[16,2560]{1,0:T(8,128)S(1)}, u32[]{:S(2)}, u32[]{:S(2)}) %collective-permute-start.1) | collective-permute-done | bytes 163872 | tf_op jit(solution)/shard_map/ppermute | solution.py:763
  11.0 0.1 fusion
  11.1 0.0 collective-permute-start.2
  11.1 0.0 copy-done.7
  11.1 0.0 copy-done.6
  11.1 0.7 %prepare.1 = (s32[16,4,128]{2,1,0:T(4,128)S(1)}, bf16[16,128,256]{2,1,0:T(8,128)(2,1)S(1)}) custom-call(s32[1]{0:T(128)} %bitcast.bead, s32[2,4096]{1,0:T(2,128)S(1)} %copy-done.6, s32[3,2048]{1,0:T(4,128)S(1)} %copy-done.7), custom_call_target="tpu_custom_call" | custom-call | flops 10000000 | bytes 100000 | tf_op jit(solution)/shard_map/prepare/pallas_call | solution.py:294
  11.8 5.2 %collective-permute-done.2.refs_2_ = f32[16,256]{1,0:T(8,128)S(1)} collective-permute-done((f32[16,256]{1,0:T(8,128)S(1)}, f32[16,256]{1,0:T(8,128)S(1)}, u32[]{:S(2)}, u32[]{:S(2)}) %collective-permute-start.2) | collective-permute-done | bytes 16416 | tf_op jit(solution)/shard_map/ppermute | solution.py:770
  16.9 0.0 copy-start
  16.9 0.0 copy-start.1
  16.9 0.0 copy-start.3
  16.9 0.0 copy-start.4
  16.9 0.0 copy-start.5
  16.9 6.1 %pair_forces.3.refs_2_ = f32[16,2048]{1,0:T(8,128)S(1)} custom-call(s32[1]{0:T(128)} %bitcast.bead, s32[1]{0:T(128)} %bitcast.1.space, s32[3,32]{1,0:T(4,128)} %nbr.5, f32[16,2304]{1,0:T(8,128)S(1)} %get-tuple-element.25.refs_0_, f32[16,2560]{1,0:T(8,128)S(1)} %collective-permute-done.1.refs_1_, f32[16,256]{1,0:T(8,128)S(1)} %collective-permute-done.2.refs_2_), custom_call_target="tpu_custom_call" | custom-call | flops 10000000 | bytes 100000 | tf_op jit(solution)/shard_map/pair_forces/pallas_call | solution.py:414
  23.1 0.0 collective-permute-done.refs_1_
  23.1 0.0 copy-done
  23.1 0.0 copy-done.1
  23.1 0.0 copy-done.3
  23.1 0.0 copy-done.4
  23.1 0.0 copy-done.5
  23.1 5.4 %substeps.2 = (f32[6,16,1024]{2,1,0:T(8,128)S(1)}, f32[6,16,1024]{2,1,0:T(8,128)S(1)}, f32[16,1024]{1,0:T(8,128)S(1)}) custom-call(s32[1]{0:T(128)} %bitcast.bead, f32[6,16,1024]{2,1,0:T(8,128)S(1)} %get-tuple-element.23.refs_0_, f32[6,16,1024]{2,1,0:T(8,128)S(1)} %collective-permute-done.refs_1_, f32[16,2048]{1,0:T(8,128)S(1)} %pair_forces.3.refs_2_, ...), custom_call_target="tpu_custom_call" | custom-call | flops 10000000 | bytes 100000 | tf_op jit(solution)/shard_map/substeps/pallas_call | solution.py:535
  28.5 0.1 collective-permute-start.8
  28.6 0.0 collective-permute-done.3.refs_1_
  28.6 5.4 %substeps.3 = (f32[6,16,1024]{2,1,0:T(8,128)S(1)}, f32[6,16,1024]{2,1,0:T(8,128)S(1)}, f32[16,1024]{1,0:T(8,128)S(1)}, f32[16,256]{1,0:T(8,128)S(1)}, f32[16,256]{1,0:T(8,128)S(1)}) custom-call(s32[1]{0:T(128)} %bitcast.bead, f32[6,16,1024]{2,1,0:T(8,128)S(1)} %get-tuple-element.31.refs_0_, f32[6,16,1024]{2,1,0:T(8,128)S(1)} %collective-permute-done.3.refs_1_, ...), custom_call_target="tpu_custom_call" | custom-call | flops 10000000 | bytes 100000 | tf_op jit(solution)/shard_map/substeps/pallas_call | solution.py:535
  34.0 2.0 %collective-permute-start.9 = (f32[6,16,1024]{2,1,0:T(8,128)S(1)}, f32[6,16,1024]{2,1,0:T(8,128)S(1)}, u32[]{:S(2)}, u32[]{:S(2)}) collective-permute-start(f32[6,16,1024]{2,1,0:T(8,128)S(1)} %get-tuple-element.37), channel_id=1, source_target_pairs={{0,1},{1,0},{2,3},{3,2},{4,5},{5,4},{6,7},{7,6},{8,9},{9,8},{10,11... | collective-permute-start | bytes 1179656 | tf_op jit(solution)/shard_map/ppermute | solution.py:813
  36.1 4.8 %pair_forces.4.inner = f32[16,1536]{1,0:T(8,128)S(1)} custom-call(s32[1]{0:T(128)} %bitcast.bead, s32[1]{0:T(128)} %bitcast.1.space, s32[3,32]{1,0:T(4,128)} %nbr.5, f32[16,1024]{1,0:T(8,128)S(1)} %get-tuple-element.30.refs_10_.refs_0_, f32[16,1024]{1,0:T(8,128)S(1)} %get-tuple-element.33.refs_1_), custom_call_target="tpu_custom_call" | custom-call | flops 10000000 | bytes 100000 | tf_op jit(solution)/shard_map/pair_forces/pallas_call | solution.py:414
  40.8 0.1 collective-permute-start.4
  40.9 2.0 %collective-permute-start.5 = (f32[16,256]{1,0:T(8,128)S(1)}, f32[16,256]{1,0:T(8,128)S(1)}, u32[]{:S(2)}, u32[]{:S(2)}) collective-permute-start(f32[16,256]{1,0:T(8,128)S(1)} %get-tuple-element.34), channel_id=1, source_target_pairs={{0,1},{1,0},{2,3},{3,2},{4,5},{5,4},{6,7},{7,6},{8,9},{9,8},{10,11... | collective-permute-start | bytes 49160 | tf_op jit(solution)/shard_map/ppermute | solution.py:827
  42.9 0.0 copy-start.2
  42.9 2.3 %collective-permute-start.6 = (f32[16,256]{1,0:T(8,128)S(1)}, f32[16,256]{1,0:T(8,128)S(1)}, u32[]{:S(2)}, u32[]{:S(2)}) collective-permute-start(f32[16,256]{1,0:T(8,128)S(1)} %get-tuple-element.35), channel_id=1, source_target_pairs={{0,31},{1,2},{2,1},{3,4},{4,3},{5,6},{6,5},{7,8},{8,7},{9,10},{10,... | collective-permute-start | bytes 49160 | tf_op jit(solution)/shard_map/ppermute | solution.py:828
  45.3 3.0 %collective-permute-done.5.refs_2_ = f32[16,256]{1,0:T(8,128)S(1)} collective-permute-done((f32[16,256]{1,0:T(8,128)S(1)}, f32[16,256]{1,0:T(8,128)S(1)}, u32[]{:S(2)}, u32[]{:S(2)}) %collective-permute-start.5) | collective-permute-done | bytes 16416 | tf_op jit(solution)/shard_map/ppermute | solution.py:827
  48.2 1.5 %collective-permute-done.6.refs_3_ = f32[16,256]{1,0:T(8,128)S(1)} collective-permute-done((f32[16,256]{1,0:T(8,128)S(1)}, f32[16,256]{1,0:T(8,128)S(1)}, u32[]{:S(2)}, u32[]{:S(2)}) %collective-permute-start.6) | collective-permute-done | bytes 16416 | tf_op jit(solution)/shard_map/ppermute | solution.py:828
  49.7 2.5 %pair_forces.5.outer = f32[16,512]{1,0:T(8,128)S(1)} custom-call(s32[1]{0:T(128)} %bitcast.bead, s32[1]{0:T(128)} %bitcast.1.space, s32[3,32]{1,0:T(4,128)} %nbr.5, f32[16,1024]{1,0:T(8,128)S(1)} %get-tuple-element.30.refs_10_.refs_0_, f32[16,1024]{1,0:T(8,128)S(1)} %get-tuple-element.33.refs_1_, f32[16,256]{1,0:T(8,128)S(1)} %collective-permute-done.5.refs_2_, ...), custom_call_target="tpu_custom_call" | custom-call | flops 10000000 | bytes 100000 | tf_op jit(solution)/shard_map/pair_forces/pallas_call | solution.py:414
  52.2 0.7 %collective-permute-start.7 = (f32[16,512]{1,0:T(8,128)S(1)}, f32[16,512]{1,0:T(8,128)S(1)}, u32[]{:S(2)}, u32[]{:S(2)}) collective-permute-start(f32[16,512]{1,0:T(8,128)S(1)} %pair_forces.5.outer), channel_id=1, source_target_pairs={{0,1},{1,0},{2,3},{3,2},{4,5},{5,4},{6,7},{7,6},{8,9},{9,8},{10,11... | collective-permute-start | bytes 98312 | tf_op jit(solution)/shard_map/ppermute | solution.py:850
  52.9 0.0 collective-permute-done.8.refs_2_.refs_0_
  52.9 0.0 copy-done.2
  52.9 1.1 %finish_block.2 = (f32[3,16,4096]{2,1,0:T(8,128)}, f32[3,16,4096]{2,1,0:T(8,128)}) custom-call(s32[1]{0:T(128)} %bitcast.bead, bf16[2,3,48,48]{3,2,1,0:T(8,128)(2,1)S(1)} %copy-done.2, f32[16,1536]{1,0:T(8,128)S(1)} %pair_forces.4.inner, f32[16,512]{1,0:T(8,128)S(1)} %pair_forces.5.outer, f32[6,16,1024]{2,1,0:T(8,128)S(1)} %get-tuple-element.38.refs_0_, ...), custom_call_target="tpu_custom_call" | custom-call | flops 10000000 | bytes 100000 | tf_op jit(solution)/shard_map/finish_block/pallas_call | solution.py:622
  54.0 2.2 %collective-permute-done.7.outer = f32[16,512]{1,0:T(8,128)S(1)} collective-permute-done((f32[16,512]{1,0:T(8,128)S(1)}, f32[16,512]{1,0:T(8,128)S(1)}, u32[]{:S(2)}, u32[]{:S(2)}) %collective-permute-start.7) | collective-permute-done | bytes 32800 | tf_op jit(solution)/shard_map/ppermute | solution.py:850
  56.2 0.0 collective-permute-done.4.inner
  56.2 0.0 collective-permute-done.9.refs_1_
  56.2 1.1 %finish_block.3 = (f32[3,16,4096]{2,1,0:T(8,128)}, f32[3,16,4096]{2,1,0:T(8,128)}) custom-call(s32[1]{0:T(128)} %bitcast.bead, bf16[2,3,48,48]{3,2,1,0:T(8,128)(2,1)S(1)} %copy-done.2, f32[16,1536]{1,0:T(8,128)S(1)} %collective-permute-done.4.inner, f32[16,512]{1,0:T(8,128)S(1)} %collective-permute-done.7.outer, ...), custom_call_target="tpu_custom_call", output_to_operand_aliasing={{0}: (6, {}), {1}: (7, {})} | custom-call | flops 10000000 | bytes 100000 | tf_op jit(solution)/shard_map/finish_block/pallas_call | solution.py:622
  (1 shorter events, 0.0 us)
Async XLA Ops:
  0.6 10.4 %copy-start.7 = (s32[3,2048]{1,0:T(4,128)S(1)}, s32[3,2048]{1,0:T(4,128)}, u32[]{:S(2)}) copy-start(s32[3,2048]{1,0:T(4,128)} %angles.1) | copy-start | bytes 73732
  2.9 8.2 %copy-start.6 = (s32[2,4096]{1,0:T(2,128)S(1)}, s32[2,4096]{1,0:T(2,128)}, u32[]{:S(2)}) copy-start(s32[2,4096]{1,0:T(2,128)} %bonds.1) | copy-start | bytes 98308
  2.9 8.1 %collective-permute-start.1 = (f32[16,2560]{1,0:T(8,128)S(1)}, f32[16,2560]{1,0:T(8,128)S(1)}, u32[]{:S(2)}, u32[]{:S(2)}) collective-permute-start(f32[16,2560]{1,0:T(8,128)S(1)} %get-tuple-element.26), channel_id=1, source_target_pairs={{0,1},{1,0},{2,3},{3,2},{4,5},{5,4},{6,7},{7,6},{8,9},{9,8},{10,11... | collective-permute-start | bytes 491528 | tf_op jit(solution)/shard_map/ppermute | solution.py:763
  5.9 17.2 %collective-permute-start = (f32[6,16,1024]{2,1,0:T(8,128)S(1)}, f32[6,16,1024]{2,1,0:T(8,128)S(1)}, u32[]{:S(2)}, u32[]{:S(2)}) collective-permute-start(f32[6,16,1024]{2,1,0:T(8,128)S(1)} %get-tuple-element.24), channel_id=1, source_target_pairs={{0,1},{1,0},{2,3},{3,2},{4,5},{5,4},{6,7},{7,6},{8,9},{9,8},{10,11... | collective-permute-start | bytes 1179656 | tf_op jit(solution)/shard_map/ppermute | solution.py:765
  6.0 22.6 %collective-permute-start.3 = (f32[6,16,1024]{2,1,0:T(8,128)S(1)}, f32[6,16,1024]{2,1,0:T(8,128)S(1)}, u32[]{:S(2)}, u32[]{:S(2)}) collective-permute-start(f32[6,16,1024]{2,1,0:T(8,128)S(1)} %get-tuple-element.32), channel_id=1, source_target_pairs={{0,1},{1,0},{2,3},{3,2},{4,5},{5,4},{6,7},{7,6},{8,9},{9,8},{10,11... | collective-permute-start | bytes 1179656 | tf_op jit(solution)/shard_map/ppermute | solution.py:765
  11.1 5.9 %collective-permute-start.2 = (f32[16,256]{1,0:T(8,128)S(1)}, f32[16,256]{1,0:T(8,128)S(1)}, u32[]{:S(2)}, u32[]{:S(2)}) collective-permute-start(f32[16,256]{1,0:T(8,128)S(1)} %fusion), channel_id=1, source_target_pairs={{0,2},{1,31},{2,4},{3,1},{4,6},{5,3},{6,8},{7,5},{8,10},{9,7},{10,... | collective-permute-start | bytes 49160 | tf_op jit(solution)/shard_map/ppermute | solution.py:770
  16.9 6.2 %copy-start = (bf16[2,288,48]{2,1,0:T(8,128)(2,1)S(1)}, bf16[2,288,48]{2,1,0:T(8,128)(2,1)}, u32[]{:S(2)}) copy-start(bf16[2,288,48]{2,1,0:T(8,128)(2,1)} %constant.25.clone.refs_8_) | copy-start | bytes 165892
  16.9 6.2 %copy-start.1 = (bf16[192,192]{1,0:T(8,128)(2,1)S(1)}, bf16[192,192]{1,0:T(8,128)(2,1)}, u32[]{:S(2)}) copy-start(bf16[192,192]{1,0:T(8,128)(2,1)} %constant.26.clone.refs_7_) | copy-start | bytes 221188
  16.9 6.2 %copy-start.3 = (f32[4096]{0:T(1024)S(1)}, f32[4096]{0:T(1024)}, u32[]{:S(2)}) copy-start(f32[4096]{0:T(1024)} %param.15) | copy-start | bytes 49156
  16.9 6.2 %copy-start.4 = (bf16[2,32,192]{2,1,0:T(8,128)(2,1)S(1)}, bf16[2,32,192]{2,1,0:T(8,128)(2,1)}, u32[]{:S(2)}) copy-start(bf16[2,32,192]{2,1,0:T(8,128)(2,1)} %constant.24.clone.refs_9_) | copy-start | bytes 73732
  16.9 6.2 %copy-start.5 = (f32[4096]{0:T(1024)S(1)}, f32[4096]{0:T(1024)}, u32[]{:S(2)}) copy-start(f32[4096]{0:T(1024)} %param.14) | copy-start | bytes 49156
  28.5 24.4 %collective-permute-start.8 = (f32[6,16,1024]{2,1,0:T(8,128)S(1)}, f32[6,16,1024]{2,1,0:T(8,128)S(1)}, u32[]{:S(2)}, u32[]{:S(2)}) collective-permute-start(f32[6,16,1024]{2,1,0:T(8,128)S(1)} %get-tuple-element.36), channel_id=1, source_target_pairs={{0,1},{1,0},{2,3},{3,2},{4,5},{5,4},{6,7},{7,6},{8,9},{9,8},{10,11... | collective-permute-start | bytes 1179656 | tf_op jit(solution)/shard_map/ppermute | solution.py:813
  34.0 22.2 %collective-permute-start.9 = (f32[6,16,1024]{2,1,0:T(8,128)S(1)}, f32[6,16,1024]{2,1,0:T(8,128)S(1)}, u32[]{:S(2)}, u32[]{:S(2)}) collective-permute-start(f32[6,16,1024]{2,1,0:T(8,128)S(1)} %get-tuple-element.37), channel_id=1, source_target_pairs={{0,1},{1,0},{2,3},{3,2},{4,5},{5,4},{6,7},{7,6},{8,9},{9,8},{10,11... | collective-permute-start | bytes 1179656 | tf_op jit(solution)/shard_map/ppermute | solution.py:813
  40.8 15.3 %collective-permute-start.4 = (f32[16,1536]{1,0:T(8,128)S(1)}, f32[16,1536]{1,0:T(8,128)S(1)}, u32[]{:S(2)}, u32[]{:S(2)}) collective-permute-start(f32[16,1536]{1,0:T(8,128)S(1)} %pair_forces.4.inner), channel_id=1, source_target_pairs={{0,1},{1,0},{2,3},{3,2},{4,5},{5,4},{6,7},{7,6},{8,9},{9,8},{10,11... | collective-permute-start | bytes 294920 | tf_op jit(solution)/shard_map/ppermute | solution.py:849
  40.9 7.3 %collective-permute-start.5 = (f32[16,256]{1,0:T(8,128)S(1)}, f32[16,256]{1,0:T(8,128)S(1)}, u32[]{:S(2)}, u32[]{:S(2)}) collective-permute-start(f32[16,256]{1,0:T(8,128)S(1)} %get-tuple-element.34), channel_id=1, source_target_pairs={{0,1},{1,0},{2,3},{3,2},{4,5},{5,4},{6,7},{7,6},{8,9},{9,8},{10,11... | collective-permute-start | bytes 49160 | tf_op jit(solution)/shard_map/ppermute | solution.py:827
  42.9 10.0 %copy-start.2 = (bf16[2,3,48,48]{3,2,1,0:T(8,128)(2,1)S(1)}, bf16[2,3,48,48]{3,2,1,0:T(8,128)(2,1)}, u32[]{:S(2)}) copy-start(bf16[2,3,48,48]{3,2,1,0:T(8,128)(2,1)} %constant.23.clone.expand) | copy-start | bytes 82948
  42.9 6.8 %collective-permute-start.6 = (f32[16,256]{1,0:T(8,128)S(1)}, f32[16,256]{1,0:T(8,128)S(1)}, u32[]{:S(2)}, u32[]{:S(2)}) collective-permute-start(f32[16,256]{1,0:T(8,128)S(1)} %get-tuple-element.35), channel_id=1, source_target_pairs={{0,31},{1,2},{2,1},{3,4},{4,3},{5,6},{6,5},{7,8},{8,7},{9,10},{10,... | collective-permute-start | bytes 49160 | tf_op jit(solution)/shard_map/ppermute | solution.py:828
  52.2 4.0 %collective-permute-start.7 = (f32[16,512]{1,0:T(8,128)S(1)}, f32[16,512]{1,0:T(8,128)S(1)}, u32[]{:S(2)}, u32[]{:S(2)}) collective-permute-start(f32[16,512]{1,0:T(8,128)S(1)} %pair_forces.5.outer), channel_id=1, source_target_pairs={{0,1},{1,0},{2,3},{3,2},{4,5},{5,4},{6,7},{7,6},{8,9},{9,8},{10,11... | collective-permute-start | bytes 98312 | tf_op jit(solution)/shard_map/ppermute | solution.py:850

commit v3 on v2

--- a/solution.py
+++ b/solution.py
@@ -153,7 +153,7 @@
     return BEADS / KEPT * contract_left(table).T
 
 
-def begin_kernel(chunks, bead, left, strengths, pos, mom, *refs):
+def begin_kernel(chunks, bead, left, strengths, pos, *refs):
     mine, theirs, straight = refs[:3]
     blocks = refs[3:-4]
     whole, table, rows, sems = refs[-4:]
@@ -163,15 +163,12 @@
     for i in range(2 * chunks):
         owner = bead[0] if i < chunks else 1 - bead[0]
         starts.append(pl.multiple_of((owner * chunks + i % chunks) * lanes, TILE))
-    for half, source in enumerate((pos, mom)):
-        for i, block in enumerate(blocks):
-            copy = pltpu.make_async_copy(
-                source.at[:, :, pl.ds(starts[i], lanes)],
-                block.at[pl.ds(3 * half, 3)],
-                sems.at[half * len(blocks) + i],
-            )
-            copy.start()
-            copies.append(copy)
+    for i, block in enumerate(blocks):
+        copy = pltpu.make_async_copy(
+            pos.at[:, :, pl.ds(starts[i], lanes)], block.at[pl.ds(0, 3)], sems.at[i]
+        )
+        copy.start()
+        copies.append(copy)
     small = [
         pltpu.make_async_copy(left.at[bead[0]], table, sems.at[len(copies)]),
         pltpu.make_async_copy(strengths, rows, sems.at[len(copies) + 1]),
@@ -203,11 +200,40 @@
 
     for which in range(2):
         pl.when(bead[0] == which)(functools.partial(sides, which))
-    for copy in copies[len(blocks) :]:
+
+
+def fetch_kernel(chunks, bead, mom, *refs):
+    blocks = refs[2 * chunks : 4 * chunks]
+    sems = refs[-1]
+    lanes = blocks[0].shape[2]
+    copies = []
+    for i, block in reversed(list(enumerate(blocks))):
+        owner = bead[0] if i < chunks else 1 - bead[0]
+        start = pl.multiple_of((owner * chunks + i % chunks) * lanes, TILE)
+        copy = pltpu.make_async_copy(
+            mom.at[:, :, pl.ds(start, lanes)], block.at[pl.ds(3, 3)], sems.at[i]
+        )
+        copy.start()
+        copies.append(copy)
+    for copy in copies:
         copy.wait()
 
 
-def begin(chunks, bead, left, strengths, pos, mom):
+def fetch(chunks, bead, mom, blocks):
+    return pl.pallas_call(
+        functools.partial(fetch_kernel, chunks),
+        in_specs=[IN_SMEM] + [pl.BlockSpec(memory_space=pl.ANY)] + [IN_VMEM] * len(blocks),
+        out_specs=[IN_VMEM] * len(blocks),
+        out_shape=[vmem_out(x.shape, F32) for x in blocks],
+        scratch_shapes=[pltpu.SemaphoreType.DMA((len(blocks),))],
+        input_output_aliases={2 + i: i for i in range(len(blocks))},
+        compiler_params=PARAMS,
+        cost_estimate=COST,
+        name="fetch",
+    )(bead, far(mom), *[near(x) for x in blocks])
+
+
+def begin(chunks, bead, left, strengths, pos):
     beads, slab = pos.shape[1:]
     block, rim = slab // 2, GT * TILE
     lanes = block // chunks
@@ -215,19 +241,19 @@
     shapes += [(6, beads, lanes)] * (2 * chunks)
     return pl.pallas_call(
         functools.partial(begin_kernel, chunks),
-        in_specs=[IN_SMEM] + [pl.BlockSpec(memory_space=pl.ANY)] * 4,
+        in_specs=[IN_SMEM] + [pl.BlockSpec(memory_space=pl.ANY)] * 3,
         out_specs=[IN_VMEM] * len(shapes),
         out_shape=[vmem_out(s, F32) for s in shapes],
         scratch_shapes=[
             pltpu.VMEM((ROWS, slab), F32),
             pltpu.VMEM(left.shape[1:], left.dtype),
             pltpu.VMEM(strengths.shape, F32),
-            pltpu.SemaphoreType.DMA((4 * chunks + 2,)),
+            pltpu.SemaphoreType.DMA((2 * chunks + 2,)),
         ],
         compiler_params=PARAMS,
         cost_estimate=COST,
         name="begin",
-    )(bead, far(left), far(strengths), far(pos), far(mom))
+    )(bead, far(left), far(strengths), far(pos))
 
 
 def partial_kernel(bead, left, strengths, pos, out):
@@ -430,10 +456,17 @@
     )(bead, space, far(neighbour_tiles), *[near(x) for x in flat])
 
 
-def step_kernel(parts, chunk, chunks, group, edge, bead, *refs):
+def whole_force(inner, outer):
+    rim = GT * TILE
+    return jnp.concatenate([outer[:, :rim], inner[...], outer[:, rim:]], axis=1)
+
+
+def step_kernel(parts, forces, chunk, chunks, group, edge, bead, *refs):
     pieces = refs[:parts]
-    force, mass_rows, strength_rows, ends, hot, motion, expand, contract = refs[parts : parts + 8]
-    before = refs[parts + 8] if edge and chunk else None
+    force = refs[parts] if forces == 1 else whole_force(*refs[parts : parts + 2])
+    at = parts + forces
+    mass_rows, strength_rows, ends, hot, motion, expand, contract = refs[at : at + 7]
+    before = refs[at + 7] if edge and chunk else None
     outs = refs[len(refs) - parts - 1 - 2 * edge :]
     c_out = outs[parts]
     interval = time_step / SUBS
@@ -533,8 +566,10 @@
     if edge:
         shapes += [(ROWS, GT * TILE)] * 2
     return pl.pallas_call(
-        functools.partial(step_kernel, parts, chunk, chunks, lanes // TILE, int(edge)),
-        in_specs=[IN_SMEM] + [IN_VMEM] * (parts + 8 + len(extra)),
+        functools.partial(
+            step_kernel, parts, len(force), chunk, chunks, lanes // TILE, int(edge)
+        ),
+        in_specs=[IN_SMEM] + [IN_VMEM] * (parts + len(force) + 7 + len(extra)),
         out_specs=[IN_VMEM] * len(shapes),
         out_shape=[vmem_out(s, F32) for s in shapes],
         compiler_params=PARAMS,
@@ -542,7 +577,7 @@
         name="substeps",
     )(
         bead,
-        *[near(x) for x in pieces + [force]],
+        *[near(x) for x in pieces + force],
         mass,
         strength,
         near(ends),
@@ -589,7 +624,6 @@
     parts = refs[:count]
     pos, mom, held, sems = refs[-4:]
     lanes = parts[0].shape[2]
-    rim = GT * TILE
     blocks = [bead[0], 1 - bead[0]]
 
     def where(owner, chunk):
@@ -603,7 +637,7 @@
 
     for part, move_owner, chunk in moves:
         copy(parts[part].at[pl.ds(0, 3)], pos.at[:, :, where(move_owner, chunk)])
-    force = jnp.concatenate([outer[:, :rim], inner[...], outer[:, rim:]], axis=1)
+    force = whole_force(inner, outer)
     for chunk in range(chunks):
         lane = slice(chunk * lanes, (chunk + 1) * lanes)
         for c in range(3):
@@ -707,16 +741,22 @@
         x = jnp.where(x >= all_tiles - GT, x - all_tiles, x)
         return jnp.where(x < -GT, x + all_tiles, x)
 
-    def spots_first(info):
-        first = info[0] * (block_tiles - GT)
-        outside = block_tiles + GT
-
-        def spot(tile):
-            x = relative(tile, info)
-            right = jnp.where(x >= slab_tiles, x - slab_tiles + outside, x - first)
-            return jnp.where(x < 0, x + GT + outside, right)
-
-        return lambda t: t + info[0] * block_tiles, lambda t: t + info[0] * GT, spot
+    def spots_first(inner):
+        def spots(info):
+            first = info[0] * (block_tiles - GT)
+            outside = block_tiles + GT
+
+            def own(t):
+                return t + GT if inner else jnp.where(t < GT, t, t + block_tiles - 2 * GT)
+
+            def spot(tile):
+                x = relative(tile, info)
+                right = jnp.where(x >= slab_tiles, x - slab_tiles + outside, x - first)
+                return jnp.where(x < 0, x + GT + outside, right)
+
+            return lambda t: own(t) + info[0] * block_tiles, lambda t: own(t) + info[0] * GT, spot
+
+        return spots
 
     def spots_inner(info):
         def spot(tile):
@@ -758,9 +798,10 @@
     pieces = [[] for _ in range(chunks)]
     if pair:
         mine, theirs, straight, *blocks = begin(
-            chunks, bead_at, begin_left, strength, pos, mom
+            chunks, bead_at, begin_left, strength, pos
         )
         theirs = lax.ppermute(theirs, "bead", SWAP)
+        blocks = fetch(chunks, bead_at, mom, blocks)
         for chunk in range(chunks):
             other = lax.ppermute(blocks[chunks + chunk], "bead", SWAP)
             pieces[chunk] = [blocks[chunk], other]
@@ -770,8 +811,8 @@
         straight = lax.ppermute(
             straight, ("space", "bead"), permutation(lambda b: -1 if b else 1, 0)
         )
-        segments = [([mine, theirs], 0, block_tiles + GT), ([straight], 0, GT)]
-        spots = spots_first
+        inside = [([mine, theirs], 0, block_tiles + GT)]
+        rim_tiles = [([straight], 0, GT)]
     else:
         part = partial_rows(bead_at, begin_left, strength, pos)
         summed = lax.psum(part, "bead")
@@ -791,7 +832,13 @@
             pieces[chunk] = [jnp.concatenate(parts, 1)]
 
     ends, hot = prepare(bead_at, bond_ends, angle_ends, block_tiles)
-    force = pair_forces(spots, segments, block_tiles, bead_at, space_at, neighbour_tiles)
+    if pair:
+        ids = bead_at, space_at, neighbour_tiles
+        inner = pair_forces(spots_first(True), inside, block_tiles - 2 * GT, *ids)
+        outer = pair_forces(spots_first(False), inside + rim_tiles, 2 * GT, *ids)
+        force = [inner, outer]
+    else:
+        force = [pair_forces(spots, segments, block_tiles, bead_at, space_at, neighbour_tiles)]
 
     own_out, returned, contracted = [], [], []
     for chunk in range(chunks):

time: 57.5 us -> 56.4 us (0.981)
  waiting for transfers between devices: 14.8 us -> 8.43 us
  starting transfers between devices: 12.3 us -> 15.1 us
  Pallas kernels: 29.2 us -> 31.7 us
    ppermute x1, waiting for transfers between devices: 5.17 us -> 0.27 us  [body(): lax.ppermute(straight, ('space', 'bead'), permutation(lambda b: -1 if b e...]
    ppermute x1, starting transfers between devices: 0.1 us -> 2.07 us  [body(): inner = lax.ppermute(inner, 'bead', SWAP)]
    ppermute x1, starting transfers between devices: 1.99 us -> 0.08 us  [body(): beside = lax.ppermute(bead_edge, 'bead', SWAP)]
    ppermute x2, starting transfers between devices: 2.1 us -> 4 us  [body(): back.append(lax.ppermute(outs[d], 'bead', on))]
    ppermute x1, waiting for transfers between devices: 2.98 us -> 4.64 us  [body(): beside = lax.ppermute(bead_edge, 'bead', SWAP)]
    pallas_call x3 -> x4, Pallas kernels: 13.4 us -> 15 us  [pair_forces(): pl.pallas_call(functools.partial(pair_kernel, spots, sizes, own_count), i...]
    ppermute x1, waiting for transfers between devices: 3.02 us -> 1.52 us  [body(): theirs = lax.ppermute(theirs, 'bead', SWAP)]
    ppermute x1, waiting for transfers between devices: 1.45 us -> 0.01 us  [body(): lax.ppermute(far_edge, ('space', 'bead'), permutation(lambda b: 1 if b el...]
  transfers between devices with their start and end apart: 10 -> 10, of which waited for: 5 -> 4; matrix products, arithmetic and copies ran while one was open for 0% -> 0% of each run, Pallas kernels for 45% -> 51%
where the time goes in v3:
time: 56.4 us; the launch traced here: 56.2 us
  Pallas kernels  31.7 us (56%)
  starting transfers between devices  15.1 us (27%)
  waiting for transfers between devices  8.43 us (15%)
  between operations  0.77 us (1%)
    pallas_call x4, Pallas kernels, pair_forces(): pl.pallas_call(functools.partial(pair_kernel, spots, sizes, own_count), i...  15 us
    pallas_call x2, Pallas kernels, substeps(): pl.pallas_call(functools.partial(step_kernel, parts, len(force), chunk, c...  10.8 us
    ppermute x1, waiting for transfers between devices, body(): beside = lax.ppermute(bead_edge, 'bead', SWAP)  4.64 us
    ppermute x2, starting transfers between devices, body(): back.append(lax.ppermute(outs[d], 'bead', on))  4 us
    ppermute x1, starting transfers between devices, body(): theirs = lax.ppermute(theirs, 'bead', SWAP)  3.06 us
    ppermute x1, starting transfers between devices, body(): lax.ppermute(far_edge, ('space', 'bead'), permutation(lambda b: 1 if b el...  2.93 us
    pallas_call x2, Pallas kernels, finish_block(): pl.pallas_call(functools.partial(finish_block_kernel, chunks, owner, move...  2.15 us
    ppermute x2, starting transfers between devices, body(): other = lax.ppermute(blocks[chunks + chunk], 'bead', SWAP)  2.09 us
  transfers between devices with their start and end apart: 10, of which 4 were waited for; matrix products, arithmetic and copies ran while one was open for 0% of the time, Pallas kernels for 51%

profile of v3, /device:TPU:0, one launch (start us, length us, event | category | flops | bytes accessed | tf_op | source)
XLA Modules:
  0.0 56.2 jit_solution(10609715441825550057)
XLA Ops:
  0.6 1.9 %begin.1 = (f32[16,2304]{1,0:T(8,128)S(1)}, f32[16,2560]{1,0:T(8,128)S(1)}, f32[16,256]{1,0:T(8,128)S(1)}, f32[6,16,1024]{2,1,0:T(8,128)S(1)}, f32[6,16,1024]{2,...) custom-call(s32[1]{0:T(128)} %bitcast.bead, bf16[2,48,144]{2,1,0:T(8,128)(2,1)} %constant.22.clone.left, ...), custom_call_target="tpu_custom_call" | custom-call | flops 10000000 | bytes 100000 | tf_op jit(solution)/shard_map/begin/pallas_call | solution.py:242
  2.5 3.1 %collective-permute-start.1 = (f32[16,2560]{1,0:T(8,128)S(1)}, f32[16,2560]{1,0:T(8,128)S(1)}, u32[]{:S(2)}, u32[]{:S(2)}) collective-permute-start(f32[16,2560]{1,0:T(8,128)S(1)} %get-tuple-element.34), channel_id=1, source_target_pairs={{0,1},{1,0},{2,3},{3,2},{4,5},{5,4},{6,7},{7,6},{8,9},{9,8},{10,11... | collective-permute-start | bytes 491528 | tf_op jit(solution)/shard_map/ppermute | solution.py:803
  5.6 0.0 copy-start.7
  5.6 1.3 %fetch.1 = (f32[6,16,1024]{2,1,0:T(8,128)S(1)}, f32[6,16,1024]{2,1,0:T(8,128)S(1)}, f32[6,16,1024]{2,1,0:T(8,128)S(1)}, f32[6,16,1024]{2,1,0:T(8,128)S(1)}) custom-call(s32[1]{0:T(128)} %bitcast.bead, f32[3,16,4096]{2,1,0:T(8,128)} %bitcast.13, ...), custom_call_target="tpu_custom_call", output_to_operand_aliasing={{0}: (2, {}), {1}: (3, {}), {2}: (4, {}), {3}: (5, {})} | custom-call | flops 10000000 | bytes 100000 | tf_op jit(solution)/shard_map/fetch/pallas_call | solution.py:223
  6.9 0.0 copy-start.6
  6.9 0.1 collective-permute-start
  7.0 2.0 %collective-permute-start.3 = (f32[6,16,1024]{2,1,0:T(8,128)S(1)}, f32[6,16,1024]{2,1,0:T(8,128)S(1)}, u32[]{:S(2)}, u32[]{:S(2)}) collective-permute-start(f32[6,16,1024]{2,1,0:T(8,128)S(1)} %get-tuple-element.40), channel_id=1, source_target_pairs={{0,1},{1,0},{2,3},{3,2},{4,5},{5,4},{6,7},{7,6},{8,9},{9,8},{10,11... | collective-permute-start | bytes 1179656 | tf_op jit(solution)/shard_map/ppermute | solution.py:806
  9.0 1.5 %collective-permute-done.1.refs_1_ = f32[16,2560]{1,0:T(8,128)S(1)} collective-permute-done((f32[16,2560]{1,0:T(8,128)S(1)}, f32[16,2560]{1,0:T(8,128)S(1)}, u32[]{:S(2)}, u32[]{:S(2)}) %collective-permute-start.1) | collective-permute-done | bytes 163872 | tf_op jit(solution)/shard_map/ppermute | solution.py:803
  10.5 0.1 fusion
  10.6 0.0 collective-permute-start.2
  10.6 0.0 copy-done.7
  10.6 0.0 copy-done.6
  10.6 0.7 %prepare.1 = (s32[16,4,128]{2,1,0:T(4,128)S(1)}, bf16[16,128,256]{2,1,0:T(8,128)(2,1)S(1)}) custom-call(s32[1]{0:T(128)} %bitcast.bead, s32[2,4096]{1,0:T(2,128)S(1)} %copy-done.6, s32[3,2048]{1,0:T(4,128)S(1)} %copy-done.7), custom_call_target="tpu_custom_call" | custom-call | flops 10000000 | bytes 100000 | tf_op jit(solution)/shard_map/prepare/pallas_call | solution.py:320
  11.3 4.9 %pair_forces.4.refs_2_ = f32[16,1536]{1,0:T(8,128)S(1)} custom-call(s32[1]{0:T(128)} %bitcast.bead, s32[1]{0:T(128)} %bitcast.1.space, s32[3,32]{1,0:T(4,128)} %nbr.7, f32[16,2304]{1,0:T(8,128)S(1)} %get-tuple-element.33.refs_0_, f32[16,2560]{1,0:T(8,128)S(1)} %collective-permute-done.1.refs_1_), custom_call_target="tpu_custom_call" | custom-call | flops 10000000 | bytes 100000 | tf_op jit(solution)/shard_map/pair_forces/pallas_call | solution.py:440
  16.1 0.0 copy-start
  16.2 0.0 copy-start.1
  16.2 0.0 copy-start.4
  16.2 0.3 collective-permute-done.2.refs_2_
  16.4 0.0 copy-start.3
  16.5 0.0 copy-start.5
  16.5 2.8 %pair_forces.5.refs_3_ = f32[16,512]{1,0:T(8,128)S(1)} custom-call(s32[1]{0:T(128)} %bitcast.bead, s32[1]{0:T(128)} %bitcast.1.space, s32[3,32]{1,0:T(4,128)} %nbr.7, f32[16,2304]{1,0:T(8,128)S(1)} %get-tuple-element.33.refs_0_, f32[16,2560]{1,0:T(8,128)S(1)} %collective-permute-done.1.refs_1_, f32[16,256]{1,0:T(8,128)S(1)} %collective-permute-done.2.refs_2_), custom_call_target="tpu_custom_call" | custom-call | flops 10000000 | bytes 100000 | tf_op jit(solution)/shard_map/pair_forces/pallas_call | solution.py:440
  19.2 0.0 collective-permute-done.refs_1_
  19.3 0.0 copy-done
  19.3 0.0 copy-done.1
  19.3 0.0 copy-done.4
  19.3 0.0 copy-done.3
  19.3 0.0 copy-done.5
  19.3 5.4 %substeps.2 = (f32[6,16,1024]{2,1,0:T(8,128)S(1)}, f32[6,16,1024]{2,1,0:T(8,128)S(1)}, f32[16,1024]{1,0:T(8,128)S(1)}) custom-call(s32[1]{0:T(128)} %bitcast.bead, f32[6,16,1024]{2,1,0:T(8,128)S(1)} %get-tuple-element.31.refs_0_, f32[6,16,1024]{2,1,0:T(8,128)S(1)} %collective-permute-done.refs_1_, f32[16,1536]{1,0:T(8,128)S(1)} %pair_forces.4.refs_2_, ...), custom_call_target="tpu_custom_call" | custom-call | flops 10000000 | bytes 100000 | tf_op jit(solution)/shard_map/substeps/pallas_call | solution.py:568
  24.7 3.9 %collective-permute-start.8 = (f32[6,16,1024]{2,1,0:T(8,128)S(1)}, f32[6,16,1024]{2,1,0:T(8,128)S(1)}, u32[]{:S(2)}, u32[]{:S(2)}) collective-permute-start(f32[6,16,1024]{2,1,0:T(8,128)S(1)} %get-tuple-element.44), channel_id=1, source_target_pairs={{0,1},{1,0},{2,3},{3,2},{4,5},{5,4},{6,7},{7,6},{8,9},{9,8},{10,11... | collective-permute-start | bytes 1179656 | tf_op jit(solution)/shard_map/ppermute | solution.py:860
  28.6 0.0 collective-permute-done.3.refs_1_
  28.6 5.4 %substeps.3 = (f32[6,16,1024]{2,1,0:T(8,128)S(1)}, f32[6,16,1024]{2,1,0:T(8,128)S(1)}, f32[16,1024]{1,0:T(8,128)S(1)}, f32[16,256]{1,0:T(8,128)S(1)}, f32[16,256]{1,0:T(8,128)S(1)}) custom-call(s32[1]{0:T(128)} %bitcast.bead, f32[6,16,1024]{2,1,0:T(8,128)S(1)} %get-tuple-element.39.refs_0_, f32[6,16,1024]{2,1,0:T(8,128)S(1)} %collective-permute-done.3.refs_1_, ...), custom_call_target="tpu_custom_call" | custom-call | flops 10000000 | bytes 100000 | tf_op jit(solution)/shard_map/substeps/pallas_call | solution.py:568
  34.0 0.1 collective-permute-start.9
  34.1 4.8 %pair_forces.6.inner = f32[16,1536]{1,0:T(8,128)S(1)} custom-call(s32[1]{0:T(128)} %bitcast.bead, s32[1]{0:T(128)} %bitcast.1.space, s32[3,32]{1,0:T(4,128)} %nbr.7, f32[16,1024]{1,0:T(8,128)S(1)} %get-tuple-element.38.refs_11_.refs_0_, f32[16,1024]{1,0:T(8,128)S(1)} %get-tuple-element.41.refs_1_), custom_call_target="tpu_custom_call" | custom-call | flops 10000000 | bytes 100000 | tf_op jit(solution)/shard_map/pair_forces/pallas_call | solution.py:440
  38.9 2.1 %collective-permute-start.4 = (f32[16,1536]{1,0:T(8,128)S(1)}, f32[16,1536]{1,0:T(8,128)S(1)}, u32[]{:S(2)}, u32[]{:S(2)}) collective-permute-start(f32[16,1536]{1,0:T(8,128)S(1)} %pair_forces.6.inner), channel_id=1, source_target_pairs={{0,1},{1,0},{2,3},{3,2},{4,5},{5,4},{6,7},{7,6},{8,9},{9,8},{10,11... | collective-permute-start | bytes 294920 | tf_op jit(solution)/shard_map/ppermute | solution.py:896
  41.0 0.1 collective-permute-start.5
  41.0 0.0 copy-start.2
  41.0 2.9 %collective-permute-start.6 = (f32[16,256]{1,0:T(8,128)S(1)}, f32[16,256]{1,0:T(8,128)S(1)}, u32[]{:S(2)}, u32[]{:S(2)}) collective-permute-start(f32[16,256]{1,0:T(8,128)S(1)} %get-tuple-element.43), channel_id=1, source_target_pairs={{0,31},{1,2},{2,1},{3,4},{4,3},{5,6},{6,5},{7,8},{8,7},{9,10},{10,... | collective-permute-start | bytes 49160 | tf_op jit(solution)/shard_map/ppermute | solution.py:875
  44.0 4.6 %collective-permute-done.5.refs_2_ = f32[16,256]{1,0:T(8,128)S(1)} collective-permute-done((f32[16,256]{1,0:T(8,128)S(1)}, f32[16,256]{1,0:T(8,128)S(1)}, u32[]{:S(2)}, u32[]{:S(2)}) %collective-permute-start.5) | collective-permute-done | bytes 16416 | tf_op jit(solution)/shard_map/ppermute | solution.py:874
  48.6 0.0 collective-permute-done.6.refs_3_
  48.6 2.5 %pair_forces.7.outer = f32[16,512]{1,0:T(8,128)S(1)} custom-call(s32[1]{0:T(128)} %bitcast.bead, s32[1]{0:T(128)} %bitcast.1.space, s32[3,32]{1,0:T(4,128)} %nbr.7, f32[16,1024]{1,0:T(8,128)S(1)} %get-tuple-element.38.refs_11_.refs_0_, f32[16,1024]{1,0:T(8,128)S(1)} %get-tuple-element.41.refs_1_, f32[16,256]{1,0:T(8,128)S(1)} %collective-permute-done.5.refs_2_, ...), custom_call_target="tpu_custom_call" | custom-call | flops 10000000 | bytes 100000 | tf_op jit(solution)/shard_map/pair_forces/pallas_call | solution.py:440
  51.1 0.9 %collective-permute-start.7 = (f32[16,512]{1,0:T(8,128)S(1)}, f32[16,512]{1,0:T(8,128)S(1)}, u32[]{:S(2)}, u32[]{:S(2)}) collective-permute-start(f32[16,512]{1,0:T(8,128)S(1)} %pair_forces.7.outer), channel_id=1, source_target_pairs={{0,1},{1,0},{2,3},{3,2},{4,5},{5,4},{6,7},{7,6},{8,9},{9,8},{10,11... | collective-permute-start | bytes 98312 | tf_op jit(solution)/shard_map/ppermute | solution.py:897
  52.0 0.0 collective-permute-done.8.refs_2_.refs_0_
  52.0 0.0 copy-done.2
  52.0 1.1 %finish_block.2 = (f32[3,16,4096]{2,1,0:T(8,128)}, f32[3,16,4096]{2,1,0:T(8,128)}) custom-call(s32[1]{0:T(128)} %bitcast.bead, bf16[2,3,48,48]{3,2,1,0:T(8,128)(2,1)S(1)} %copy-done.2, f32[16,1536]{1,0:T(8,128)S(1)} %pair_forces.6.inner, f32[16,512]{1,0:T(8,128)S(1)} %pair_forces.7.outer, f32[6,16,1024]{2,1,0:T(8,128)S(1)} %get-tuple-element.46.refs_0_, ...), custom_call_target="tpu_custom_call" | custom-call | flops 10000000 | bytes 100000 | tf_op jit(solution)/shard_map/finish_block/pallas_call | solution.py:656
  53.1 2.0 %collective-permute-done.7.outer = f32[16,512]{1,0:T(8,128)S(1)} collective-permute-done((f32[16,512]{1,0:T(8,128)S(1)}, f32[16,512]{1,0:T(8,128)S(1)}, u32[]{:S(2)}, u32[]{:S(2)}) %collective-permute-start.7) | collective-permute-done | bytes 32800 | tf_op jit(solution)/shard_map/ppermute | solution.py:897
  55.1 0.0 collective-permute-done.4.inner
  55.1 0.0 collective-permute-done.9.refs_1_
  55.1 1.1 %finish_block.3 = (f32[3,16,4096]{2,1,0:T(8,128)}, f32[3,16,4096]{2,1,0:T(8,128)}) custom-call(s32[1]{0:T(128)} %bitcast.bead, bf16[2,3,48,48]{3,2,1,0:T(8,128)(2,1)S(1)} %copy-done.2, f32[16,1536]{1,0:T(8,128)S(1)} %collective-permute-done.4.inner, f32[16,512]{1,0:T(8,128)S(1)} %collective-permute-done.7.outer, ...), custom_call_target="tpu_custom_call", output_to_operand_aliasing={{0}: (6, {}), {1}: (7, {})} | custom-call | flops 10000000 | bytes 100000 | tf_op jit(solution)/shard_map/finish_block/pallas_call | solution.py:656
  (1 shorter events, 0.0 us)
Async XLA Ops:
  2.5 8.0 %collective-permute-start.1 = (f32[16,2560]{1,0:T(8,128)S(1)}, f32[16,2560]{1,0:T(8,128)S(1)}, u32[]{:S(2)}, u32[]{:S(2)}) collective-permute-start(f32[16,2560]{1,0:T(8,128)S(1)} %get-tuple-element.34), channel_id=1, source_target_pairs={{0,1},{1,0},{2,3},{3,2},{4,5},{5,4},{6,7},{7,6},{8,9},{9,8},{10,11... | collective-permute-start | bytes 491528 | tf_op jit(solution)/shard_map/ppermute | solution.py:803
  5.6 5.0 %copy-start.7 = (s32[3,2048]{1,0:T(4,128)S(1)}, s32[3,2048]{1,0:T(4,128)}, u32[]{:S(2)}) copy-start(s32[3,2048]{1,0:T(4,128)} %angles.1) | copy-start | bytes 73732
  6.9 3.7 %copy-start.6 = (s32[2,4096]{1,0:T(2,128)S(1)}, s32[2,4096]{1,0:T(2,128)}, u32[]{:S(2)}) copy-start(s32[2,4096]{1,0:T(2,128)} %bonds.1) | copy-start | bytes 98308
  6.9 12.4 %collective-permute-start = (f32[6,16,1024]{2,1,0:T(8,128)S(1)}, f32[6,16,1024]{2,1,0:T(8,128)S(1)}, u32[]{:S(2)}, u32[]{:S(2)}) collective-permute-start(f32[6,16,1024]{2,1,0:T(8,128)S(1)} %get-tuple-element.32), channel_id=1, source_target_pairs={{0,1},{1,0},{2,3},{3,2},{4,5},{5,4},{6,7},{7,6},{8,9},{9,8},{10,11... | collective-permute-start | bytes 1179656 | tf_op jit(solution)/shard_map/ppermute | solution.py:806
  7.0 21.6 %collective-permute-start.3 = (f32[6,16,1024]{2,1,0:T(8,128)S(1)}, f32[6,16,1024]{2,1,0:T(8,128)S(1)}, u32[]{:S(2)}, u32[]{:S(2)}) collective-permute-start(f32[6,16,1024]{2,1,0:T(8,128)S(1)} %get-tuple-element.40), channel_id=1, source_target_pairs={{0,1},{1,0},{2,3},{3,2},{4,5},{5,4},{6,7},{7,6},{8,9},{9,8},{10,11... | collective-permute-start | bytes 1179656 | tf_op jit(solution)/shard_map/ppermute | solution.py:806
  10.6 5.9 %collective-permute-start.2 = (f32[16,256]{1,0:T(8,128)S(1)}, f32[16,256]{1,0:T(8,128)S(1)}, u32[]{:S(2)}, u32[]{:S(2)}) collective-permute-start(f32[16,256]{1,0:T(8,128)S(1)} %fusion), channel_id=1, source_target_pairs={{0,2},{1,31},{2,4},{3,1},{4,6},{5,3},{6,8},{7,5},{8,10},{9,7},{10,... | collective-permute-start | bytes 49160 | tf_op jit(solution)/shard_map/ppermute | solution.py:811
  16.1 3.1 %copy-start = (bf16[2,288,48]{2,1,0:T(8,128)(2,1)S(1)}, bf16[2,288,48]{2,1,0:T(8,128)(2,1)}, u32[]{:S(2)}) copy-start(bf16[2,288,48]{2,1,0:T(8,128)(2,1)} %constant.25.clone.refs_9_) | copy-start | bytes 165892
  16.2 3.1 %copy-start.1 = (bf16[192,192]{1,0:T(8,128)(2,1)S(1)}, bf16[192,192]{1,0:T(8,128)(2,1)}, u32[]{:S(2)}) copy-start(bf16[192,192]{1,0:T(8,128)(2,1)} %constant.26.clone.refs_8_) | copy-start | bytes 221188
  16.2 3.1 %copy-start.4 = (bf16[2,32,192]{2,1,0:T(8,128)(2,1)S(1)}, bf16[2,32,192]{2,1,0:T(8,128)(2,1)}, u32[]{:S(2)}) copy-start(bf16[2,32,192]{2,1,0:T(8,128)(2,1)} %constant.24.clone.refs_10_) | copy-start | bytes 73732
  16.4 2.8 %copy-start.3 = (f32[4096]{0:T(1024)S(1)}, f32[4096]{0:T(1024)}, u32[]{:S(2)}) copy-start(f32[4096]{0:T(1024)} %param.15) | copy-start | bytes 49156
  16.5 2.8 %copy-start.5 = (f32[4096]{0:T(1024)S(1)}, f32[4096]{0:T(1024)}, u32[]{:S(2)}) copy-start(f32[4096]{0:T(1024)} %param.14) | copy-start | bytes 49156
  24.7 27.3 %collective-permute-start.8 = (f32[6,16,1024]{2,1,0:T(8,128)S(1)}, f32[6,16,1024]{2,1,0:T(8,128)S(1)}, u32[]{:S(2)}, u32[]{:S(2)}) collective-permute-start(f32[6,16,1024]{2,1,0:T(8,128)S(1)} %get-tuple-element.44), channel_id=1, source_target_pairs={{0,1},{1,0},{2,3},{3,2},{4,5},{5,4},{6,7},{7,6},{8,9},{9,8},{10,11... | collective-permute-start | bytes 1179656 | tf_op jit(solution)/shard_map/ppermute | solution.py:860
  34.0 21.1 %collective-permute-start.9 = (f32[6,16,1024]{2,1,0:T(8,128)S(1)}, f32[6,16,1024]{2,1,0:T(8,128)S(1)}, u32[]{:S(2)}, u32[]{:S(2)}) collective-permute-start(f32[6,16,1024]{2,1,0:T(8,128)S(1)} %get-tuple-element.45), channel_id=1, source_target_pairs={{0,1},{1,0},{2,3},{3,2},{4,5},{5,4},{6,7},{7,6},{8,9},{9,8},{10,11... | collective-permute-start | bytes 1179656 | tf_op jit(solution)/shard_map/ppermute | solution.py:860
  38.9 16.2 %collective-permute-start.4 = (f32[16,1536]{1,0:T(8,128)S(1)}, f32[16,1536]{1,0:T(8,128)S(1)}, u32[]{:S(2)}, u32[]{:S(2)}) collective-permute-start(f32[16,1536]{1,0:T(8,128)S(1)} %pair_forces.6.inner), channel_id=1, source_target_pairs={{0,1},{1,0},{2,3},{3,2},{4,5},{5,4},{6,7},{7,6},{8,9},{9,8},{10,11... | collective-permute-start | bytes 294920 | tf_op jit(solution)/shard_map/ppermute | solution.py:896
  41.0 7.6 %collective-permute-start.5 = (f32[16,256]{1,0:T(8,128)S(1)}, f32[16,256]{1,0:T(8,128)S(1)}, u32[]{:S(2)}, u32[]{:S(2)}) collective-permute-start(f32[16,256]{1,0:T(8,128)S(1)} %get-tuple-element.42), channel_id=1, source_target_pairs={{0,1},{1,0},{2,3},{3,2},{4,5},{5,4},{6,7},{7,6},{8,9},{9,8},{10,11... | collective-permute-start | bytes 49160 | tf_op jit(solution)/shard_map/ppermute | solution.py:874
  41.0 11.0 %copy-start.2 = (bf16[2,3,48,48]{3,2,1,0:T(8,128)(2,1)S(1)}, bf16[2,3,48,48]{3,2,1,0:T(8,128)(2,1)}, u32[]{:S(2)}) copy-start(bf16[2,3,48,48]{3,2,1,0:T(8,128)(2,1)} %constant.23.clone.expand) | copy-start | bytes 82948
  41.0 7.6 %collective-permute-start.6 = (f32[16,256]{1,0:T(8,128)S(1)}, f32[16,256]{1,0:T(8,128)S(1)}, u32[]{:S(2)}, u32[]{:S(2)}) collective-permute-start(f32[16,256]{1,0:T(8,128)S(1)} %get-tuple-element.43), channel_id=1, source_target_pairs={{0,31},{1,2},{2,1},{3,4},{4,3},{5,6},{6,5},{7,8},{8,7},{9,10},{10,... | collective-permute-start | bytes 49160 | tf_op jit(solution)/shard_map/ppermute | solution.py:875
  51.1 4.0 %collective-permute-start.7 = (f32[16,512]{1,0:T(8,128)S(1)}, f32[16,512]{1,0:T(8,128)S(1)}, u32[]{:S(2)}, u32[]{:S(2)}) collective-permute-start(f32[16,512]{1,0:T(8,128)S(1)} %pair_forces.7.outer), channel_id=1, source_target_pairs={{0,1},{1,0},{2,3},{3,2},{4,5},{5,4},{6,7},{7,6},{8,9},{9,8},{10,11... | collective-permute-start | bytes 98312 | tf_op jit(solution)/shard_map/ppermute | solution.py:897

commit v4 on v3

--- a/solution.py
+++ b/solution.py
@@ -18,6 +18,7 @@
 BPT = 128
 APT = 64
 ROWS = 4 * KEPT
+LOGS = 3 * KEPT
 
 time_step = 0.3
 spring_freq = 80.0
@@ -132,6 +133,25 @@
     return total
 
 
+def packed_left(table):
+    high, mid, low = np_split(table, 3)
+    zero = np.zeros_like(high)
+    return np.concatenate(
+        [
+            np.concatenate([high, high, high, mid], axis=1),
+            np.concatenate([low, mid, zero, zero], axis=1),
+        ],
+        axis=0,
+    )
+
+
+def packed_exact(left, x):
+    high, mid, low = split(x, 3)
+    out = mm(left, jnp.concatenate([high, mid, low, high], axis=0))
+    rows = out.shape[0] // 2
+    return out[:rows] + out[rows:]
+
+
 def contract_rows(beads):
     table = contract_table(BEADS, KEPT)
     tables = []
@@ -145,12 +165,25 @@
     out = np.zeros((ROWS, 3 * table.shape[1]))
     for c in range(KEPT):
         for k in range(3):
-            out[4 * c + 1 + k, k * table.shape[1] : (k + 1) * table.shape[1]] = table[c]
+            out[k * KEPT + c, k * table.shape[1] : (k + 1) * table.shape[1]] = table[c]
     return out
 
 
 def expand_left(table):
     return BEADS / KEPT * contract_left(table).T
+
+
+def pack_rows(target, x):
+    lanes = x.shape[1]
+    target[:, :lanes] = x[:8]
+    target[:4, lanes:] = x[8:12, : lanes // 2]
+    target[4:, lanes:] = x[8:12, lanes // 2 :]
+
+
+def unpacked(x):
+    lanes = x.shape[1] * 2 // 3
+    last = jnp.concatenate([x[:4, lanes:], x[4:, lanes:]], axis=1)
+    return jnp.concatenate([x[:, :lanes], last, jnp.zeros_like(last)], axis=0)
 
 
 def begin_kernel(chunks, bead, left, strengths, pos, *refs):
@@ -165,7 +198,7 @@
         starts.append(pl.multiple_of((owner * chunks + i % chunks) * lanes, TILE))
     for i, block in enumerate(blocks):
         copy = pltpu.make_async_copy(
-            pos.at[:, :, pl.ds(starts[i], lanes)], block.at[pl.ds(0, 3)], sems.at[i]
+            pos.at[:, :, pl.ds(starts[i], lanes)], block, sems.at[i]
         )
         copy.start()
         copies.append(copy)
@@ -179,13 +212,13 @@
         copy.wait()
     logs = math.log2(math.e) * jnp.log(rows[...])
     for t in range(slab // TILE):
-        whole[0:1, t * TILE : (t + 1) * TILE] = logs[t : t + 1]
+        whole[LOGS : LOGS + 1, t * TILE : (t + 1) * TILE] = logs[t : t + 1]
     for i, block in enumerate(blocks):
         copies[i].wait()
         x = jnp.concatenate([block[c] for c in range(3)], axis=0)
         where = pl.ds(starts[i], lanes)
         row = lax.broadcasted_iota(jnp.int32, (ROWS, lanes), 0)
-        whole[:, where] = jnp.where(row == 0, whole[:, where], exact(table[...], x))
+        whole[:, where] = jnp.where(row == LOGS, whole[:, where], exact(table[...], x))
 
     block, rim = slab // 2, GT * TILE
     size = block + rim
@@ -193,52 +226,50 @@
     def sides(which):
         first, other = (0, block - rim) if which == 0 else (block - rim, 0)
         mine[...] = whole[:, first : first + size]
-        theirs[:, :size] = whole[:, other : other + size]
         head, tail = whole[:, :rim], whole[:, slab - rim :]
         straight[...] = tail if which == 0 else head
-        theirs[:, size:] = head if which == 0 else tail
+        relay = head if which == 0 else tail
+        pack_rows(theirs, jnp.concatenate([whole[:, other : other + size], relay], axis=1))
 
     for which in range(2):
         pl.when(bead[0] == which)(functools.partial(sides, which))
 
 
 def fetch_kernel(chunks, bead, mom, *refs):
-    blocks = refs[2 * chunks : 4 * chunks]
-    sems = refs[-1]
+    *blocks, sems = refs
     lanes = blocks[0].shape[2]
     copies = []
     for i, block in reversed(list(enumerate(blocks))):
         owner = bead[0] if i < chunks else 1 - bead[0]
         start = pl.multiple_of((owner * chunks + i % chunks) * lanes, TILE)
-        copy = pltpu.make_async_copy(
-            mom.at[:, :, pl.ds(start, lanes)], block.at[pl.ds(3, 3)], sems.at[i]
-        )
+        copy = pltpu.make_async_copy(mom.at[:, :, pl.ds(start, lanes)], block, sems.at[i])
         copy.start()
         copies.append(copy)
     for copy in copies:
         copy.wait()
 
 
-def fetch(chunks, bead, mom, blocks):
+def fetch(chunks, bead, mom):
+    beads, slab = mom.shape[1:]
+    count = 2 * chunks
     return pl.pallas_call(
         functools.partial(fetch_kernel, chunks),
-        in_specs=[IN_SMEM] + [pl.BlockSpec(memory_space=pl.ANY)] + [IN_VMEM] * len(blocks),
-        out_specs=[IN_VMEM] * len(blocks),
-        out_shape=[vmem_out(x.shape, F32) for x in blocks],
-        scratch_shapes=[pltpu.SemaphoreType.DMA((len(blocks),))],
-        input_output_aliases={2 + i: i for i in range(len(blocks))},
+        in_specs=[IN_SMEM, pl.BlockSpec(memory_space=pl.ANY)],
+        out_specs=[IN_VMEM] * count,
+        out_shape=[vmem_out((3, beads, slab // count), F32)] * count,
+        scratch_shapes=[pltpu.SemaphoreType.DMA((count,))],
         compiler_params=PARAMS,
         cost_estimate=COST,
         name="fetch",
-    )(bead, far(mom), *[near(x) for x in blocks])
+    )(bead, far(mom))
 
 
 def begin(chunks, bead, left, strengths, pos):
     beads, slab = pos.shape[1:]
     block, rim = slab // 2, GT * TILE
     lanes = block // chunks
-    shapes = [(ROWS, block + rim), (ROWS, block + 2 * rim), (ROWS, rim)]
-    shapes += [(6, beads, lanes)] * (2 * chunks)
+    shapes = [(ROWS, block + rim), (8, 3 * (block + 2 * rim) // 2), (ROWS, rim)]
+    shapes += [(3, beads, lanes)] * (2 * chunks)
     return pl.pallas_call(
         functools.partial(begin_kernel, chunks),
         in_specs=[IN_SMEM] + [pl.BlockSpec(memory_space=pl.ANY)] * 3,
@@ -256,13 +287,32 @@
     )(bead, far(left), far(strengths), far(pos))
 
 
+def relay_kernel(own, received, out):
+    rim = GT * TILE
+    size = received.shape[1] * 2 // 3
+    more = jnp.concatenate([received[:, size - rim : size], received[4:, -rim:]], axis=0)
+    out[...] = own[...] + jnp.concatenate([more, jnp.zeros_like(more[:4])], axis=0)
+
+
+def relay(own, received):
+    return pl.pallas_call(
+        relay_kernel,
+        in_specs=[IN_VMEM] * 2,
+        out_specs=IN_VMEM,
+        out_shape=vmem_out(own.shape, F32),
+        compiler_params=PARAMS,
+        cost_estimate=COST,
+        name="relay",
+    )(near(own), near(received))
+
+
 def partial_kernel(bead, left, strengths, pos, out):
     comps, _, lanes = pos.shape
     logs = math.log2(math.e) * jnp.log(strengths[...])
     logs = jnp.concatenate([logs[t : t + 1] for t in range(lanes // TILE)], axis=1)
     row = lax.broadcasted_iota(jnp.int32, (ROWS, lanes), 0)
     x = jnp.concatenate([pos[c] for c in range(comps)], axis=0)
-    out[...] = jnp.where(row == 0, logs, exact(left[bead[0]], x))
+    out[...] = jnp.where(row == LOGS, logs, exact(left[bead[0]], x))
 
 
 def partial_rows(bead, left, strengths, pos):
@@ -283,7 +333,7 @@
     )(bead, left, strengths, pos)
 
 
-def prepare_kernel(group, bead, bonds, angles, ends, hot):
+def prepare_kernel(group, bead, bonds, angles, hot):
     lane = lax.broadcasted_iota(jnp.int32, (1, TILE), 1)
     atom = lax.broadcasted_iota(jnp.int32, (TILE, 2 * TILE), 0)
     low = lane < APT
@@ -303,10 +353,8 @@
             odd = t % 2
             window = slice((t // 2) * TILE, (t // 2 + 1) * TILE)
             first, middle, last = [angle_rows[e : e + 1, window] for e in range(3)]
-            outer = merge(first, last, odd)
             opposite = merge(last, first, odd)
             centre = merge(middle, middle, odd)
-            ends[i * group + t] = jnp.concatenate([one, other, outer, centre], axis=0)
             gains = jnp.concatenate([other, centre], axis=1)
             losses = jnp.concatenate([one, opposite], axis=1)
             table = (atom == gains).astype(F32) - (atom == losses).astype(F32)
@@ -320,35 +368,33 @@
     return pl.pallas_call(
         functools.partial(prepare_kernel, math.gcd(block_tiles, 4)),
         in_specs=[IN_SMEM, IN_VMEM, IN_VMEM],
-        out_specs=[IN_VMEM] * 2,
-        out_shape=[
-            vmem_out((block_tiles, 4, TILE), jnp.int32),
-            vmem_out((block_tiles, TILE, 2 * TILE), BF16),
-        ],
+        out_specs=IN_VMEM,
+        out_shape=vmem_out((block_tiles, TILE, 2 * TILE), BF16),
         compiler_params=PARAMS,
         cost_estimate=COST,
         name="prepare",
     )(bead, bond_ends, angle_ends)
 
 
-def pair_kernel(spots, seg_sizes, own_count, bead, space, nbr, *refs):
+def pair_kernel(spots, seg_sizes, own_count, packed, bead, space, nbr, *refs):
     total = sum(n for *_, n in seg_sizes)
     count = sum(n for n, *_ in seg_sizes)
     seg_refs = refs[:count]
-    out, feat_i, feat_m, feat_p, base, weights_a, weights_b = refs[count:]
+    target, feat_i, feat_m, feat_p, base, *weights, held = refs[count:]
+    out = held if packed else target
     column, own_spot, spot = spots((bead[0], space[0]))
     row = lax.broadcasted_iota(jnp.int32, (ROWS, TILE), 0)
-    slot = row % 4
+    slot = row // KEPT
     scale = math.sqrt(2.0 * math.log2(math.e) / range_sq)
     same = (
-        lax.broadcasted_iota(jnp.int32, (ROWS, ROWS), 0) // 4
-        == lax.broadcasted_iota(jnp.int32, (ROWS, ROWS), 1) // 4
+        lax.broadcasted_iota(jnp.int32, (ROWS, ROWS), 0) % KEPT
+        == lax.broadcasted_iota(jnp.int32, (ROWS, ROWS), 1) % KEPT
     ).astype(F32)
 
     def features(tile, c16):
         base[tile] = c16
-        logs = c16[0:1]
-        place = jnp.where(slot == 0, 0.0, c16)
+        logs = c16[LOGS : LOGS + 1]
+        place = jnp.where(slot == 3, 0.0, c16)
         scaled = place * scale
         high, low = [piece.astype(F32) for piece in split(scaled, 2)]
         square = jnp.dot(same, scaled * scaled, precision=HIGH, preferred_element_type=F32)
@@ -369,24 +415,41 @@
         p_high, p_low = [piece.astype(F32) for piece in split(place, 2)]
         feat_p[tile] = jnp.concatenate([one, p_high, p_low], axis=0).astype(BF16)
 
+    def piece(ref, begins, i):
+        moving = callable(begins)
+        at = (begins(bead[0]) if moving else begins) + i
+
+        def lanes(tile):
+            if moving:
+                return pl.ds(pl.multiple_of(tile * TILE, TILE), TILE)
+            return slice(tile * TILE, (tile + 1) * TILE)
+
+        if ref.shape[0] == ROWS:
+            return ref[:, lanes(at)]
+        tiles = ref.shape[1] * 2 // 3 // TILE
+        half = tiles // 2
+        upper = at >= half
+        last = ref[:, lanes(tiles + jnp.where(upper, at - half, at))]
+        last = jnp.where(upper, last[4:], last[:4])
+        return jnp.concatenate([ref[:, lanes(at)], last, jnp.zeros_like(last)], axis=0)
+
     tile = 0
     at = 0
     for number, begins, tiles in seg_sizes:
         group = seg_refs[at : at + number]
         at += number
-        for i in range(begins, begins + tiles):
-            c16 = group[0][:, i * TILE : (i + 1) * TILE]
+        for i in range(tiles):
+            c16 = piece(group[0], begins, i)
             for other in group[1:]:
-                more = other[:, i * TILE : (i + 1) * TILE]
-                c16 = c16 + jnp.where(row == 0, 0.0, more)
+                c16 = c16 + piece(other, begins, i)
             features(tile, c16)
             tile += 1
     assert tile == total
 
     groups = 6
     wide_row = lax.broadcasted_iota(jnp.int32, (groups * ROWS, TILE), 0)
-    pick = [((wide_row % ROWS) // 4 == c).astype(BF16) for c in range(KEPT)]
-    owner = row // 4
+    pick = [(wide_row % KEPT == c).astype(BF16) for c in range(KEPT)]
+    owner = row % KEPT
 
     def close(t, u):
         return spot(nbr[u, column(t)])
@@ -411,37 +474,46 @@
         sums = total_p[:ROWS]
         pulls = total_p[ROWS : 2 * ROWS] + total_p[2 * ROWS :]
         c16 = base[own_spot(t)]
-        factor = (2.0 / range_sq) * jnp.exp2(c16[0:1])
+        factor = (2.0 / range_sq) * jnp.exp2(c16[LOGS : LOGS + 1])
         result = jnp.zeros((ROWS, TILE), F32)
         for c in range(KEPT):
             lanes = slice(c * TILE, (c + 1) * TILE)
             force = factor * (c16 * sums[:, lanes] - pulls[:, lanes])
-            result = jnp.where((owner == c) & (slot > 0), force, result)
-        out[:, pl.ds(pl.multiple_of(t * TILE, TILE), TILE)] = result
-
-    weigh(0, weights_a)
-
-    def two_tiles(i, carry):
-        t = 2 * i
-        weigh(t + 1, weights_b)
-        pull(t, weights_a)
-        weigh(jnp.minimum(t + 2, own_count - 1), weights_a)
-        pull(t + 1, weights_b)
+            result = jnp.where((owner == c) & (slot < 3), force, result)
+        lane = t * TILE if isinstance(t, int) else pl.multiple_of(t * TILE, TILE)
+        out[:, pl.ds(lane, TILE)] = result
+
+    unroll = math.gcd(own_count, 4)
+    weigh(0, weights[0])
+
+    def some_tiles(t, last):
+        for j in range(unroll):
+            if not (last and j == unroll - 1):
+                weigh(t + j + 1, weights[(j + 1) % 2])
+            pull(t + j, weights[j % 2])
+
+    def loop(i, carry):
+        some_tiles(unroll * i, False)
         return carry
 
-    lax.fori_loop(0, own_count // 2, two_tiles, 0)
-
-
-def pair_forces(spots, segments, own_count, bead, space, neighbour_tiles):
+    lax.fori_loop(0, own_count // unroll - 1, loop, 0)
+    some_tiles(own_count - unroll, True)
+    if packed:
+        pack_rows(target, held[...])
+
+
+def pair_forces(spots, segments, own_count, bead, space, neighbour_tiles, packed=False):
     sizes = tuple((len(group), start, tiles) for group, start, tiles in segments)
     total = sum(n for *_, n in sizes)
     assert own_count % 2 == 0
     flat = [array for group, *_ in segments for array in group]
     return pl.pallas_call(
-        functools.partial(pair_kernel, spots, sizes, own_count),
+        functools.partial(pair_kernel, spots, sizes, own_count, packed),
         in_specs=[IN_SMEM] * 3 + [IN_VMEM] * len(flat),
         out_specs=IN_VMEM,
-        out_shape=vmem_out((ROWS, own_count * TILE), F32),
+        out_shape=vmem_out(
+            (8, 3 * own_count * TILE // 2) if packed else (ROWS, own_count * TILE), F32
+        ),
         scratch_shapes=[
             pltpu.VMEM((total, 6 * ROWS, TILE), BF16),
             pltpu.VMEM((total, TILE, 8 * ROWS), BF16),
@@ -449,6 +521,7 @@
             pltpu.VMEM((total, ROWS, TILE), F32),
             pltpu.VMEM((6 * TILE, KEPT * TILE), BF16),
             pltpu.VMEM((6 * TILE, KEPT * TILE), BF16),
+            pltpu.VMEM((ROWS, own_count * TILE), F32),
         ],
         compiler_params=PARAMS,
         cost_estimate=COST,
@@ -458,15 +531,17 @@
 
 def whole_force(inner, outer):
     rim = GT * TILE
-    return jnp.concatenate([outer[:, :rim], inner[...], outer[:, rim:]], axis=1)
+    inner, outer = unpacked(inner[...]), unpacked(outer[...])
+    return jnp.concatenate([outer[:, :rim], inner, outer[:, rim:]], axis=1)
 
 
 def step_kernel(parts, forces, chunk, chunks, group, edge, bead, *refs):
-    pieces = refs[:parts]
-    force = refs[parts] if forces == 1 else whole_force(*refs[parts : parts + 2])
-    at = parts + forces
-    mass_rows, strength_rows, ends, hot, motion, expand, contract = refs[at : at + 7]
-    before = refs[at + 7] if edge and chunk else None
+    pieces = refs[: 2 * parts]
+    at = 2 * parts
+    force = refs[at] if forces == 1 else whole_force(*refs[at : at + 2])
+    at += forces
+    mass_rows, strength_rows, hot, motion, expand, contract = refs[at : at + 6]
+    before = refs[at + 6] if edge and chunk else None
     outs = refs[len(refs) - parts - 1 - 2 * edge :]
     c_out = outs[parts]
     interval = time_step / SUBS
@@ -481,41 +556,35 @@
     masses = per_atom(mass_rows)
     inverse = 1.0 / masses
 
-    def gathered(plane):
+    def gathered(kind, c):
         if parts == 1:
-            return pieces[0][plane]
-        return jnp.concatenate([piece[plane] for piece in pieces], axis=0)
-
-    q = [gathered(c) for c in range(3)]
-    p = [gathered(3 + c) for c in range(3)]
+            return pieces[kind][c]
+        return jnp.concatenate([piece[c] for piece in pieces[kind::2]], axis=0)
+
+    q = [gathered(0, c) for c in range(3)]
+    p = [gathered(1, c) for c in range(3)]
     kick = exact(expand[bead[0]], force[:, first * TILE : first * TILE + width])
     v = [
         (p[c] + 0.5 * time_step * kick[c * BEADS : (c + 1) * BEADS]) * inverse for c in range(3)
     ]
-    places = []
-    for t in range(group):
-        places.append([jnp.broadcast_to(ends[first + t, e : e + 1], (3 * BEADS, TILE)) for e in range(4)])
-
-    def take(x, index):
-        return jnp.take_along_axis(x, index, axis=1, mode="promise_in_bounds")
 
     def bonded(q):
         forces = []
         for t in range(group):
             lanes = slice(t * TILE, (t + 1) * TILE)
             rows = jnp.concatenate([q[c][:, lanes] for c in range(3)], axis=0)
-            one, other, outer, centre = places[t]
-            stretch = take(rows, one) - take(rows, other)
-            arms = take(rows, outer) - take(rows, centre)
+            seen = mm(jnp.concatenate(split(rows, 2), axis=0), hot[first + t])
+            seen = seen[: 3 * BEADS] + seen[3 * BEADS :]
+            stretch, arms = seen[:, :TILE], seen[:, TILE:]
             s = [stretch[c * BEADS : (c + 1) * BEADS] for c in range(3)]
             a = [arms[c * BEADS : (c + 1) * BEADS] for c in range(3)]
             length = s[0] * s[0] + s[1] * s[1] + s[2] * s[2]
-            g = bond_stiff * (length - bond_rest)
+            g = bond_stiff * (bond_rest - length)
             turned = [pltpu.roll(x, APT, 1) for x in a]
             inner = a[0] * turned[0] + a[1] * turned[1] + a[2] * turned[2]
-            h = angle_stiff * (inner - angle_rest)
+            h = angle_stiff * (angle_rest - inner)
             bonds = jnp.concatenate([g * x for x in s], axis=0)
-            angles = jnp.concatenate([h * x for x in a], axis=0)
+            angles = jnp.concatenate([h * x for x in turned], axis=0)
             both = jnp.concatenate([bonds, angles], axis=1)
             out = lax.dot_general(
                 jnp.concatenate(split(both, 2), axis=0),
@@ -534,7 +603,7 @@
         factor = (0.5 if sub == 0 else 1.0) * interval * inverse
         v = [v[c] + factor * pushed[c] for c in range(3)]
         for c in range(3):
-            moved = exact(motion_l, jnp.concatenate([q[c], v[c]], axis=0))
+            moved = packed_exact(motion_l, jnp.concatenate([q[c], v[c]], axis=0))
             q[c], v[c] = moved[:BEADS], moved[BEADS:]
     pushed = bonded(q)
     p = [masses * v[c] + (0.5 * interval) * pushed[c] for c in range(3)]
@@ -547,7 +616,7 @@
     c16 = exact(contract[bead[0]], rows, 2)
     row = lax.broadcasted_iota(jnp.int32, (ROWS, width), 0)
     logs = math.log2(math.e) * jnp.log(per_atom(strength_rows))
-    c16 = jnp.where(row == 0, logs, c16)
+    c16 = jnp.where(row == LOGS, logs, c16)
     c_out[...] = c16
     if edge:
         rim = GT * TILE
@@ -557,8 +626,8 @@
         outs[-1][...] = jnp.where(bead[0] == 0, head, tail)
 
 
-def substeps(chunk, chunks, bead, pieces, force, mass, strength, ends, hot, motion, expand, contract, edge, before):
-    parts = len(pieces)
+def substeps(chunk, chunks, bead, pieces, force, mass, strength, hot, motion, expand, contract, edge, before):
+    parts = len(pieces) // 2
     lanes = pieces[0].shape[2]
     beads = BEADS // parts
     extra = [before] if edge and chunk else []
@@ -569,7 +638,7 @@
         functools.partial(
             step_kernel, parts, len(force), chunk, chunks, lanes // TILE, int(edge)
         ),
-        in_specs=[IN_SMEM] + [IN_VMEM] * (parts + len(force) + 7 + len(extra)),
+        in_specs=[IN_SMEM] + [IN_VMEM] * (2 * parts + len(force) + 6 + len(extra)),
         out_specs=[IN_VMEM] * len(shapes),
         out_shape=[vmem_out(s, F32) for s in shapes],
         compiler_params=PARAMS,
@@ -580,7 +649,6 @@
         *[near(x) for x in pieces + force],
         mass,
         strength,
-        near(ends),
         near(hot),
         motion,
         expand,
@@ -716,7 +784,7 @@
     )
     contract_l = stack([stacked_left(contract_left(t), 2) for t in turned])
     expand_l = stack([stacked_left(expand_left(t)) for t in turned])
-    motion = jnp.asarray(stacked_left(motion_table(BEADS, interval)))
+    motion = jnp.asarray(packed_left(motion_table(BEADS, interval)))
 
     def lanes_of(x, start, size):
         return lax.dynamic_slice_in_dim(x, start, size, x.ndim - 1)
@@ -741,23 +809,6 @@
         x = jnp.where(x >= all_tiles - GT, x - all_tiles, x)
         return jnp.where(x < -GT, x + all_tiles, x)
 
-    def spots_first(inner):
-        def spots(info):
-            first = info[0] * (block_tiles - GT)
-            outside = block_tiles + GT
-
-            def own(t):
-                return t + GT if inner else jnp.where(t < GT, t, t + block_tiles - 2 * GT)
-
-            def spot(tile):
-                x = relative(tile, info)
-                right = jnp.where(x >= slab_tiles, x - slab_tiles + outside, x - first)
-                return jnp.where(x < 0, x + GT + outside, right)
-
-            return lambda t: own(t) + info[0] * block_tiles, lambda t: own(t) + info[0] * GT, spot
-
-        return spots
-
     def spots_inner(info):
         def spot(tile):
             return relative(tile, info) - info[0] * block_tiles
@@ -801,23 +852,28 @@
             chunks, bead_at, begin_left, strength, pos
         )
         theirs = lax.ppermute(theirs, "bead", SWAP)
-        blocks = fetch(chunks, bead_at, mom, blocks)
+        moments = fetch(chunks, bead_at, mom)
         for chunk in range(chunks):
             other = lax.ppermute(blocks[chunks + chunk], "bead", SWAP)
-            pieces[chunk] = [blocks[chunk], other]
-        more = theirs[:, block + rim :]
-        row = lax.broadcasted_iota(jnp.int32, more.shape, 0)
-        straight = straight + jnp.where(row == 0, 0.0, more)
+            moment = lax.ppermute(moments[chunks + chunk], "bead", SWAP)
+            pieces[chunk] = [blocks[chunk], moments[chunk], other, moment]
+        straight = relay(straight, theirs)
         straight = lax.ppermute(
             straight, ("space", "bead"), permutation(lambda b: -1 if b else 1, 0)
         )
-        inside = [([mine, theirs], 0, block_tiles + GT)]
-        rim_tiles = [([straight], 0, GT)]
+        both = [mine, theirs]
+        inside = [(both, lambda b: b * GT, block_tiles)]
+        rim_tiles = [
+            (both, lambda b: b * GT, 2 * GT),
+            (both, lambda b: b * GT + block_tiles - 2 * GT, 2 * GT),
+            (both, lambda b: (1 - b) * block_tiles, GT),
+            ([straight], 0, GT),
+        ]
     else:
         part = partial_rows(bead_at, begin_left, strength, pos)
         summed = lax.psum(part, "bead")
-        first_row = lax.broadcasted_iota(jnp.int32, summed.shape, 0) == 0
-        summed = jnp.where(first_row, jnp.log2(strengths)[None, :], summed)
+        logs_row = lax.broadcasted_iota(jnp.int32, summed.shape, 0) == LOGS
+        summed = jnp.where(logs_row, jnp.log2(strengths)[None, :], summed)
         segments = [([summed], 0, slab_tiles), *[([x], 0, GT) for x in rims(summed)]]
         spots = spots_slab(True)
         for chunk in range(chunks):
@@ -829,13 +885,14 @@
                 )
                 back = [(i, (i - d) % bead_count) for i in range(bead_count)]
                 parts.append(lax.ppermute(piece, "bead", back) if d else piece)
-            pieces[chunk] = [jnp.concatenate(parts, 1)]
-
-    ends, hot = prepare(bead_at, bond_ends, angle_ends, block_tiles)
+            whole = jnp.concatenate(parts, 1)
+            pieces[chunk] = [whole[:3], whole[3:]]
+
+    hot = prepare(bead_at, bond_ends, angle_ends, block_tiles)
     if pair:
         ids = bead_at, space_at, neighbour_tiles
-        inner = pair_forces(spots_first(True), inside, block_tiles - 2 * GT, *ids)
-        outer = pair_forces(spots_first(False), inside + rim_tiles, 2 * GT, *ids)
+        inner = pair_forces(spots_inner, inside, block_tiles - 2 * GT, *ids, True)
+        outer = pair_forces(spots_outer, rim_tiles, 2 * GT, *ids, True)
         force = [inner, outer]
     else:
         force = [pair_forces(spots, segments, block_tiles, bead_at, space_at, neighbour_tiles)]
@@ -844,7 +901,7 @@
     for chunk in range(chunks):
         last = pair and chunk == chunks - 1
         outs = substeps(
-            chunk, chunks, bead_at, pieces[chunk], force, mass, strength, ends, hot, motion,
+            chunk, chunks, bead_at, pieces[chunk], force, mass, strength, hot, motion,
             expand_l, contract_l, last, contracted[0] if contracted else None,
         )
         if last:
@@ -877,16 +934,14 @@
     )
     chunk_tiles = lanes // TILE
     segments = [([x], 0, chunk_tiles) for x in contracted]
-    inner = pair_forces(
-        spots_inner, segments, block_tiles - 2 * GT, bead_at, space_at, neighbour_tiles
-    )
+    inner = pair_forces(spots_inner, segments, block_tiles - 2 * GT, *ids, True)
     segments = [
         ([contracted[0]], 0, 2 * GT),
         ([contracted[-1]], chunk_tiles - 2 * GT, 2 * GT),
         ([beside], 0, GT),
         ([across], 0, GT),
     ]
-    outer = pair_forces(spots_outer, segments, 2 * GT, bead_at, space_at, neighbour_tiles)
+    outer = pair_forces(spots_outer, segments, 2 * GT, *ids, True)
     others = [x[0] for x in returned]
     moves = [(i, 0, i) for i in range(chunks)]
     moves += [(chunks + i, 1, i) for i in range(chunks - 1)]

time: 56.4 us -> 67.4 us (1.20)
  waiting for transfers between devices: 8.43 us -> 22.6 us
  Pallas kernels: 31.7 us -> 26.8 us
  starting transfers between devices: 15.1 us -> 16.1 us
  local copies, waits for them, and re-layouts: 0.04 us -> 0.73 us
    ppermute x1, waiting for transfers between devices: 1.52 us -> 14.1 us  [body(): theirs = lax.ppermute(theirs, 'bead', SWAP)]
    ppermute x0 -> x2, starting transfers between devices: none -> 5.07 us  [body(): moment = lax.ppermute(moments[chunks + chunk], 'bead', SWAP)]
    pallas_call x2, Pallas kernels: 10.8 us -> 7.45 us  [substeps(): pl.pallas_call(functools.partial(step_kernel, parts, len(force), chunk, c...]
    ppermute x2, starting transfers between devices: 2.09 us -> 0.16 us  [body(): other = lax.ppermute(blocks[chunks + chunk], 'bead', SWAP)]
    pallas_call x4 -> x5, Pallas kernels: 15 us -> 13.3 us  [the longest x4 13.3 us: pair_forces(): pl.pallas_call(functools.partial(pair_kernel, spots, sizes, own_count, pa...]
    ppermute x1, waiting for transfers between devices: 4.64 us -> 6.25 us  [body(): beside = lax.ppermute(bead_edge, 'bead', SWAP)]
    ppermute x1, starting transfers between devices: 2.93 us -> 1.75 us  [body(): lax.ppermute(far_edge, ('space', 'bead'), permutation(lambda b: 1 if b el...]
    ppermute x1, starting transfers between devices: 3.06 us -> 1.95 us  [body(): theirs = lax.ppermute(theirs, 'bead', SWAP)]
  transfers between devices with their start and end apart: 10 -> 12, of which waited for: 4 -> 3; matrix products, arithmetic and copies ran while one was open for 0% -> 0% of each run, Pallas kernels for 51% -> 36%
where the time goes in v4:
time: 67.4 us; the launch traced here: 67.1 us
  Pallas kernels  26.8 us (40%)
  waiting for transfers between devices  22.6 us (34%)
  starting transfers between devices  16.1 us (24%)
  between operations  0.97 us (1%)
  local copies, waits for them, and re-layouts  0.73 us (1%)
    ppermute x1, waiting for transfers between devices, body(): theirs = lax.ppermute(theirs, 'bead', SWAP)  14.1 us
    pallas_call x4, Pallas kernels, pair_forces(): pl.pallas_call(functools.partial(pair_kernel, spots, sizes, own_count, pa...  13.3 us
    pallas_call x2, Pallas kernels, substeps(): pl.pallas_call(functools.partial(step_kernel, parts, len(force), chunk, c...  7.45 us
    ppermute x1, waiting for transfers between devices, body(): beside = lax.ppermute(bead_edge, 'bead', SWAP)  6.25 us
    ppermute x2, starting transfers between devices, body(): moment = lax.ppermute(moments[chunks + chunk], 'bead', SWAP)  5.07 us
    ppermute x2, starting transfers between devices, body(): back.append(lax.ppermute(outs[d], 'bead', on))  4.29 us
    ppermute x1, waiting for transfers between devices, body(): outer = lax.ppermute(outer, 'bead', SWAP)  2.16 us
    pallas_call x2, Pallas kernels, finish_block(): pl.pallas_call(functools.partial(finish_block_kernel, chunks, owner, move...  2.14 us
  transfers between devices with their start and end apart: 12, of which 3 were waited for; matrix products, arithmetic and copies ran while one was open for 0% of the time, Pallas kernels for 36%

profile of v4, /device:TPU:0, one launch (start us, length us, event | category | flops | bytes accessed | tf_op | source)
XLA Modules:
  0.0 67.1 jit_solution(13939314221662861410)
XLA Ops:
  0.6 1.3 %fetch.1 = (f32[3,16,1024]{2,1,0:T(8,128)S(1)}, f32[3,16,1024]{2,1,0:T(8,128)S(1)}, f32[3,16,1024]{2,1,0:T(8,128)S(1)}, f32[3,16,1024]{2,1,0:T(8,128)S(1)}) custom-call(s32[1]{0:T(128)} %bitcast.bead, f32[3,16,4096]{2,1,0:T(8,128)} %bitcast.14), custom_call_target="tpu_custom_call" | custom-call | flops 10000000 | bytes 100000 | tf_op jit(solution)/shard_map/fetch/pallas_call | solution.py:255
  1.9 3.1 %collective-permute-start.1 = (f32[3,16,1024]{2,1,0:T(8,128)S(1)}, f32[3,16,1024]{2,1,0:T(8,128)S(1)}, u32[]{:S(2)}, u32[]{:S(2)}) collective-permute-start(f32[3,16,1024]{2,1,0:T(8,128)S(1)} %get-tuple-element.28), channel_id=1, source_target_pairs={{0,1},{1,0},{2,3},{3,2},{4,5},{5,4},{6,7},{7,6},{8,9},{9,8},{10,11... | collective-permute-start | bytes 589832 | tf_op jit(solution)/shard_map/ppermute | solution.py:858
  5.0 1.9 %begin.1 = (f32[16,2304]{1,0:T(8,128)S(1)}, f32[8,3840]{1,0:T(8,128)S(1)}, f32[16,256]{1,0:T(8,128)S(1)}, f32[3,16,1024]{2,1,0:T(8,128)S(1)}, f32[3,16,1024]{2,1...) custom-call(s32[1]{0:T(128)} %bitcast.bead, bf16[2,48,144]{2,1,0:T(8,128)(2,1)} %constant.18.clone.left, ...), custom_call_target="tpu_custom_call" | custom-call | flops 10000000 | bytes 100000 | tf_op jit(solution)/shard_map/begin/pallas_call | solution.py:273
  6.9 0.1 collective-permute-start
  7.0 2.0 %collective-permute-start.5 = (f32[3,16,1024]{2,1,0:T(8,128)S(1)}, f32[3,16,1024]{2,1,0:T(8,128)S(1)}, u32[]{:S(2)}, u32[]{:S(2)}) collective-permute-start(f32[3,16,1024]{2,1,0:T(8,128)S(1)} %get-tuple-element.36), channel_id=1, source_target_pairs={{0,1},{1,0},{2,3},{3,2},{4,5},{5,4},{6,7},{7,6},{8,9},{9,8},{10,11... | collective-permute-start | bytes 589832 | tf_op jit(solution)/shard_map/ppermute | solution.py:858
  9.0 0.1 collective-permute-start.4
  9.0 1.9 %collective-permute-start.2 = (f32[8,3840]{1,0:T(8,128)S(1)}, f32[8,3840]{1,0:T(8,128)S(1)}, u32[]{:S(2)}, u32[]{:S(2)}) collective-permute-start(f32[8,3840]{1,0:T(8,128)S(1)} %get-tuple-element.30), channel_id=1, source_target_pairs={{0,1},{1,0},{2,3},{3,2},{4,5},{5,4},{6,7},{7,6},{8,9},{9,8},{10,11... | collective-permute-start | bytes 368648 | tf_op jit(solution)/shard_map/ppermute | solution.py:854
  11.0 14.1 %collective-permute-done.2.refs_1_.received.refs_3_.refs_5_ = f32[8,3840]{1,0:T(8,128)S(1)} collective-permute-done((f32[8,3840]{1,0:T(8,128)S(1)}, f32[8,3840]{1,0:T(8,128)S(1)}, u32[]{:S(2)}, u32[]{:S(2)}) %collective-permute-start.2) | collective-permute-done | bytes 122912 | tf_op jit(solution)/shard_map/ppermute | solution.py:854
  25.1 0.0 copy-start.7
  25.1 0.1 collective-permute-start.3
  25.2 0.7 %copy-done.6 = s32[2,4096]{1,0:T(2,128)S(1)} copy-done((s32[2,4096]{1,0:T(2,128)S(1)}, s32[2,4096]{1,0:T(2,128)}, u32[]{:S(2)}) %copy-start.6) | copy-done | bytes 32792
  25.9 0.0 copy-done.7
  25.9 0.7 prepare.1.refs_8_
  26.6 4.4 %pair_forces.4.refs_4_ = f32[8,2304]{1,0:T(8,128)S(1)} custom-call(s32[1]{0:T(128)} %bitcast.bead, s32[1]{0:T(128)} %bitcast.1.space, s32[3,32]{1,0:T(4,128)} %nbr.7, f32[16,2304]{1,0:T(8,128)S(1)} %get-tuple-element.29.refs_0_.refs_2_.refs_4_, f32[8,3840]{1,0:T(8,128)S(1)} %collective-permute-done.2.refs_1_.received.refs_3_.refs_5_), custom_call_target="tpu_custom_call" | custom-call | flops 10000000 | bytes 100000 | tf_op jit(solution)/shard_map/pair_forces/pallas_call | solution.py:510
  31.0 0.0 copy-start
  31.0 0.0 copy-start.2
  31.0 0.0 copy-start.4
  31.0 0.0 collective-permute-done.3.refs_6_
  31.1 0.0 copy-start.5
  31.1 2.3 %pair_forces.5.refs_5_ = f32[8,768]{1,0:T(8,128)S(1)} custom-call(s32[1]{0:T(128)} %bitcast.bead, s32[1]{0:T(128)} %bitcast.1.space, s32[3,32]{1,0:T(4,128)} %nbr.7, f32[16,2304]{1,0:T(8,128)S(1)} %get-tuple-element.29.refs_0_.refs_2_.refs_4_, f32[8,3840]{1,0:T(8,128)S(1)} %collective-permute-done.2.refs_1_.received.refs_3_.refs_5_, ...), custom_call_target="tpu_custom_call" | custom-call | flops 10000000 | bytes 100000 | tf_op jit(solution)/shard_map/pair_forces/pallas_call | solution.py:510
  33.3 0.0 collective-permute-done.1.refs_3_
  33.4 0.0 collective-permute-done.refs_2_
  33.4 0.0 copy-done
  33.4 0.0 copy-done.2
  33.4 0.0 copy-done.4
  33.4 0.0 copy-done.3
  33.4 0.0 copy-done.5
  33.4 3.7 %substeps.2 = (f32[6,16,1024]{2,1,0:T(8,128)S(1)}, f32[6,16,1024]{2,1,0:T(8,128)S(1)}, f32[16,1024]{1,0:T(8,128)S(1)}) custom-call(s32[1]{0:T(128)} %bitcast.bead, f32[3,16,1024]{2,1,0:T(8,128)S(1)} %get-tuple-element.25.refs_0_, f32[3,16,1024]{2,1,0:T(8,128)S(1)} %get-tuple-element.26.refs_1_, f32[3,16,1024]{2,1,0:T(8,128)S(1)} %collective-permute-done.refs_2_, ...), custom_call_target="tpu_custom_call" | custom-call | flops 10000000 | bytes 100000 | tf_op jit(solution)/shard_map/substeps/pallas_call | solution.py:637
  37.1 4.2 %collective-permute-start.10 = (f32[6,16,1024]{2,1,0:T(8,128)S(1)}, f32[6,16,1024]{2,1,0:T(8,128)S(1)}, u32[]{:S(2)}, u32[]{:S(2)}) collective-permute-start(f32[6,16,1024]{2,1,0:T(8,128)S(1)} %get-tuple-element.40), channel_id=1, source_target_pairs={{0,1},{1,0},{2,3},{3,2},{4,5},{5,4},{6,7},{7,6},{8,9},{9,8},{10,11... | collective-permute-start | bytes 1179656 | tf_op jit(solution)/shard_map/ppermute | solution.py:917
  41.4 0.0 collective-permute-done.5.refs_3_
  41.4 0.0 collective-permute-done.4.refs_2_
  41.4 3.7 %substeps.3 = (f32[6,16,1024]{2,1,0:T(8,128)S(1)}, f32[6,16,1024]{2,1,0:T(8,128)S(1)}, f32[16,1024]{1,0:T(8,128)S(1)}, f32[16,256]{1,0:T(8,128)S(1)}, f32[16,256]{1,0:T(8,128)S(1)}) custom-call(s32[1]{0:T(128)} %bitcast.bead, f32[3,16,1024]{2,1,0:T(8,128)S(1)} %get-tuple-element.33.refs_0_, f32[3,16,1024]{2,1,0:T(8,128)S(1)} %get-tuple-element.34.refs_1_, ...), custom_call_target="tpu_custom_call" | custom-call | flops 10000000 | bytes 100000 | tf_op jit(solution)/shard_map/substeps/pallas_call | solution.py:637
  45.1 0.1 collective-permute-start.11
  45.2 4.5 %pair_forces.6.inner = f32[8,2304]{1,0:T(8,128)S(1)} custom-call(s32[1]{0:T(128)} %bitcast.bead, s32[1]{0:T(128)} %bitcast.1.space, s32[3,32]{1,0:T(4,128)} %nbr.7, f32[16,1024]{1,0:T(8,128)S(1)} %get-tuple-element.32.refs_12_.refs_0_, f32[16,1024]{1,0:T(8,128)S(1)} %get-tuple-element.37.refs_1_), custom_call_target="tpu_custom_call" | custom-call | flops 10000000 | bytes 100000 | tf_op jit(solution)/shard_map/pair_forces/pallas_call | solution.py:510
  49.7 2.1 %collective-permute-start.6 = (f32[8,2304]{1,0:T(8,128)S(1)}, f32[8,2304]{1,0:T(8,128)S(1)}, u32[]{:S(2)}, u32[]{:S(2)}) collective-permute-start(f32[8,2304]{1,0:T(8,128)S(1)} %pair_forces.6.inner), channel_id=1, source_target_pairs={{0,1},{1,0},{2,3},{3,2},{4,5},{5,4},{6,7},{7,6},{8,9},{9,8},{10,11... | collective-permute-start | bytes 221192 | tf_op jit(solution)/shard_map/ppermute | solution.py:951
  51.8 0.1 collective-permute-start.7
  51.9 1.7 %collective-permute-start.8 = (f32[16,256]{1,0:T(8,128)S(1)}, f32[16,256]{1,0:T(8,128)S(1)}, u32[]{:S(2)}, u32[]{:S(2)}) collective-permute-start(f32[16,256]{1,0:T(8,128)S(1)} %get-tuple-element.39), channel_id=1, source_target_pairs={{0,31},{1,2},{2,1},{3,4},{4,3},{5,6},{6,5},{7,8},{8,7},{9,10},{10,... | collective-permute-start | bytes 49160 | tf_op jit(solution)/shard_map/ppermute | solution.py:932
  53.6 6.2 %collective-permute-done.7.refs_2_ = f32[16,256]{1,0:T(8,128)S(1)} collective-permute-done((f32[16,256]{1,0:T(8,128)S(1)}, f32[16,256]{1,0:T(8,128)S(1)}, u32[]{:S(2)}, u32[]{:S(2)}) %collective-permute-start.7) | collective-permute-done | bytes 16416 | tf_op jit(solution)/shard_map/ppermute | solution.py:931
  59.9 0.0 collective-permute-done.8.refs_3_
  59.9 2.1 %pair_forces.7.outer = f32[8,768]{1,0:T(8,128)S(1)} custom-call(s32[1]{0:T(128)} %bitcast.bead, s32[1]{0:T(128)} %bitcast.1.space, s32[3,32]{1,0:T(4,128)} %nbr.7, f32[16,1024]{1,0:T(8,128)S(1)} %get-tuple-element.32.refs_12_.refs_0_, f32[16,1024]{1,0:T(8,128)S(1)} %get-tuple-element.37.refs_1_, f32[16,256]{1,0:T(8,128)S(1)} %collective-permute-done.7.refs_2_, ...), custom_call_target="tpu_custom_call" | custom-call | flops 10000000 | bytes 100000 | tf_op jit(solution)/shard_map/pair_forces/pallas_call | solution.py:510
  62.0 0.6 collective-permute-start.9
  62.6 0.0 collective-permute-done.10.refs_2_.refs_0_
  62.6 0.0 copy-done.1
  62.6 1.1 %finish_block.2 = (f32[3,16,4096]{2,1,0:T(8,128)}, f32[3,16,4096]{2,1,0:T(8,128)}) custom-call(s32[1]{0:T(128)} %bitcast.bead, bf16[2,3,48,48]{3,2,1,0:T(8,128)(2,1)S(1)} %copy-done.1, f32[8,2304]{1,0:T(8,128)S(1)} %pair_forces.6.inner, f32[8,768]{1,0:T(8,128)S(1)} %pair_forces.7.outer, f32[6,16,1024]{2,1,0:T(8,128)S(1)} %get-tuple-element.42.refs_0_, ...), custom_call_target="tpu_custom_call" | custom-call | flops 10000000 | bytes 100000 | tf_op jit(solution)/shard_map/finish_block/pallas_call | solution.py:724
  63.7 2.2 %collective-permute-done.9.outer = f32[8,768]{1,0:T(8,128)S(1)} collective-permute-done((f32[8,768]{1,0:T(8,128)S(1)}, f32[8,768]{1,0:T(8,128)S(1)}, u32[]{:S(2)}, u32[]{:S(2)}) %collective-permute-start.9) | collective-permute-done | bytes 24608 | tf_op jit(solution)/shard_map/ppermute | solution.py:952
  65.9 0.0 collective-permute-done.6.inner
  65.9 0.0 collective-permute-done.11.refs_1_
  65.9 1.1 %finish_block.3 = (f32[3,16,4096]{2,1,0:T(8,128)}, f32[3,16,4096]{2,1,0:T(8,128)}) custom-call(s32[1]{0:T(128)} %bitcast.bead, bf16[2,3,48,48]{3,2,1,0:T(8,128)(2,1)S(1)} %copy-done.1, f32[8,2304]{1,0:T(8,128)S(1)} %collective-permute-done.6.inner, f32[8,768]{1,0:T(8,128)S(1)} %collective-permute-done.9.outer, ...), custom_call_target="tpu_custom_call", output_to_operand_aliasing={{0}: (6, {}), {1}: (7, {})} | custom-call | flops 10000000 | bytes 100000 | tf_op jit(solution)/shard_map/finish_block/pallas_call | solution.py:724
  (4 shorter events, 0.0 us)
Async XLA Ops:
  1.9 31.5 %collective-permute-start.1 = (f32[3,16,1024]{2,1,0:T(8,128)S(1)}, f32[3,16,1024]{2,1,0:T(8,128)S(1)}, u32[]{:S(2)}, u32[]{:S(2)}) collective-permute-start(f32[3,16,1024]{2,1,0:T(8,128)S(1)} %get-tuple-element.28), channel_id=1, source_target_pairs={{0,1},{1,0},{2,3},{3,2},{4,5},{5,4},{6,7},{7,6},{8,9},{9,8},{10,11... | collective-permute-start | bytes 589832 | tf_op jit(solution)/shard_map/ppermute | solution.py:858
  6.9 26.5 %collective-permute-start = (f32[3,16,1024]{2,1,0:T(8,128)S(1)}, f32[3,16,1024]{2,1,0:T(8,128)S(1)}, u32[]{:S(2)}, u32[]{:S(2)}) collective-permute-start(f32[3,16,1024]{2,1,0:T(8,128)S(1)} %get-tuple-element.27), channel_id=1, source_target_pairs={{0,1},{1,0},{2,3},{3,2},{4,5},{5,4},{6,7},{7,6},{8,9},{9,8},{10,11... | collective-permute-start | bytes 589832 | tf_op jit(solution)/shard_map/ppermute | solution.py:857
  7.0 34.4 %collective-permute-start.5 = (f32[3,16,1024]{2,1,0:T(8,128)S(1)}, f32[3,16,1024]{2,1,0:T(8,128)S(1)}, u32[]{:S(2)}, u32[]{:S(2)}) collective-permute-start(f32[3,16,1024]{2,1,0:T(8,128)S(1)} %get-tuple-element.36), channel_id=1, source_target_pairs={{0,1},{1,0},{2,3},{3,2},{4,5},{5,4},{6,7},{7,6},{8,9},{9,8},{10,11... | collective-permute-start | bytes 589832 | tf_op jit(solution)/shard_map/ppermute | solution.py:858
  9.0 32.4 %collective-permute-start.4 = (f32[3,16,1024]{2,1,0:T(8,128)S(1)}, f32[3,16,1024]{2,1,0:T(8,128)S(1)}, u32[]{:S(2)}, u32[]{:S(2)}) collective-permute-start(f32[3,16,1024]{2,1,0:T(8,128)S(1)} %get-tuple-element.35), channel_id=1, source_target_pairs={{0,1},{1,0},{2,3},{3,2},{4,5},{5,4},{6,7},{7,6},{8,9},{9,8},{10,11... | collective-permute-start | bytes 589832 | tf_op jit(solution)/shard_map/ppermute | solution.py:857
  9.0 16.1 %collective-permute-start.2 = (f32[8,3840]{1,0:T(8,128)S(1)}, f32[8,3840]{1,0:T(8,128)S(1)}, u32[]{:S(2)}, u32[]{:S(2)}) collective-permute-start(f32[8,3840]{1,0:T(8,128)S(1)} %get-tuple-element.30), channel_id=1, source_target_pairs={{0,1},{1,0},{2,3},{3,2},{4,5},{5,4},{6,7},{7,6},{8,9},{9,8},{10,11... | collective-permute-start | bytes 368648 | tf_op jit(solution)/shard_map/ppermute | solution.py:854
  25.1 0.8 %copy-start.6 = (s32[2,4096]{1,0:T(2,128)S(1)}, s32[2,4096]{1,0:T(2,128)}, u32[]{:S(2)}) copy-start(s32[2,4096]{1,0:T(2,128)} %bonds.1) | copy-start | bytes 98308
  25.1 0.8 %copy-start.7 = (s32[3,2048]{1,0:T(4,128)S(1)}, s32[3,2048]{1,0:T(4,128)}, u32[]{:S(2)}) copy-start(s32[3,2048]{1,0:T(4,128)} %angles.1) | copy-start | bytes 73732
  25.1 5.9 %collective-permute-start.3 = (f32[16,256]{1,0:T(8,128)S(1)}, f32[16,256]{1,0:T(8,128)S(1)}, u32[]{:S(2)}, u32[]{:S(2)}) collective-permute-start(f32[16,256]{1,0:T(8,128)S(1)} %relay.1), channel_id=1, source_target_pairs={{0,2},{1,31},{2,4},{3,1},{4,6},{5,3},{6,8},{7,5},{8,10},{9,7},{10,... | collective-permute-start | bytes 49160 | tf_op jit(solution)/shard_map/ppermute | solution.py:861
  31.0 2.4 %copy-start = (bf16[2,288,48]{2,1,0:T(8,128)(2,1)S(1)}, bf16[2,288,48]{2,1,0:T(8,128)(2,1)}, u32[]{:S(2)}) copy-start(bf16[2,288,48]{2,1,0:T(8,128)(2,1)} %constant.21.clone.refs_10_) | copy-start | bytes 165892
  31.0 2.4 %copy-start.2 = (bf16[128,256]{1,0:T(8,128)(2,1)S(1)}, bf16[128,256]{1,0:T(8,128)(2,1)}, u32[]{:S(2)}) copy-start(bf16[128,256]{1,0:T(8,128)(2,1)} %constant.22.clone.refs_9_) | copy-start | bytes 196612
  31.0 2.4 %copy-start.4 = (bf16[2,32,192]{2,1,0:T(8,128)(2,1)S(1)}, bf16[2,32,192]{2,1,0:T(8,128)(2,1)}, u32[]{:S(2)}) copy-start(bf16[2,32,192]{2,1,0:T(8,128)(2,1)} %constant.20.clone.refs_11_) | copy-start | bytes 73732
  31.1 2.3 %copy-start.3 = (f32[4096]{0:T(1024)S(1)}, f32[4096]{0:T(1024)}, u32[]{:S(2)}) copy-start(f32[4096]{0:T(1024)} %param.15) | copy-start | bytes 49156
  31.1 2.3 %copy-start.5 = (f32[4096]{0:T(1024)S(1)}, f32[4096]{0:T(1024)}, u32[]{:S(2)}) copy-start(f32[4096]{0:T(1024)} %param.14) | copy-start | bytes 49156
  37.1 25.5 %collective-permute-start.10 = (f32[6,16,1024]{2,1,0:T(8,128)S(1)}, f32[6,16,1024]{2,1,0:T(8,128)S(1)}, u32[]{:S(2)}, u32[]{:S(2)}) collective-permute-start(f32[6,16,1024]{2,1,0:T(8,128)S(1)} %get-tuple-element.40), channel_id=1, source_target_pairs={{0,1},{1,0},{2,3},{3,2},{4,5},{5,4},{6,7},{7,6},{8,9},{9,8},{10,11... | collective-permute-start | bytes 1179656 | tf_op jit(solution)/shard_map/ppermute | solution.py:917
  45.1 20.8 %collective-permute-start.11 = (f32[6,16,1024]{2,1,0:T(8,128)S(1)}, f32[6,16,1024]{2,1,0:T(8,128)S(1)}, u32[]{:S(2)}, u32[]{:S(2)}) collective-permute-start(f32[6,16,1024]{2,1,0:T(8,128)S(1)} %get-tuple-element.41), channel_id=1, source_target_pairs={{0,1},{1,0},{2,3},{3,2},{4,5},{5,4},{6,7},{7,6},{8,9},{9,8},{10,11... | collective-permute-start | bytes 1179656 | tf_op jit(solution)/shard_map/ppermute | solution.py:917
  49.7 16.2 %collective-permute-start.6 = (f32[8,2304]{1,0:T(8,128)S(1)}, f32[8,2304]{1,0:T(8,128)S(1)}, u32[]{:S(2)}, u32[]{:S(2)}) collective-permute-start(f32[8,2304]{1,0:T(8,128)S(1)} %pair_forces.6.inner), channel_id=1, source_target_pairs={{0,1},{1,0},{2,3},{3,2},{4,5},{5,4},{6,7},{7,6},{8,9},{9,8},{10,11... | collective-permute-start | bytes 221192 | tf_op jit(solution)/shard_map/ppermute | solution.py:951
  51.8 8.1 %collective-permute-start.7 = (f32[16,256]{1,0:T(8,128)S(1)}, f32[16,256]{1,0:T(8,128)S(1)}, u32[]{:S(2)}, u32[]{:S(2)}) collective-permute-start(f32[16,256]{1,0:T(8,128)S(1)} %get-tuple-element.38), channel_id=1, source_target_pairs={{0,1},{1,0},{2,3},{3,2},{4,5},{5,4},{6,7},{7,6},{8,9},{9,8},{10,11... | collective-permute-start | bytes 49160 | tf_op jit(solution)/shard_map/ppermute | solution.py:931
  51.9 10.8 %copy-start.1 = (bf16[2,3,48,48]{3,2,1,0:T(8,128)(2,1)S(1)}, bf16[2,3,48,48]{3,2,1,0:T(8,128)(2,1)}, u32[]{:S(2)}) copy-start(bf16[2,3,48,48]{3,2,1,0:T(8,128)(2,1)} %constant.19.clone.expand) | copy-start | bytes 82948
  51.9 8.0 %collective-permute-start.8 = (f32[16,256]{1,0:T(8,128)S(1)}, f32[16,256]{1,0:T(8,128)S(1)}, u32[]{:S(2)}, u32[]{:S(2)}) collective-permute-start(f32[16,256]{1,0:T(8,128)S(1)} %get-tuple-element.39), channel_id=1, source_target_pairs={{0,31},{1,2},{2,1},{3,4},{4,3},{5,6},{6,5},{7,8},{8,7},{9,10},{10,... | collective-permute-start | bytes 49160 | tf_op jit(solution)/shard_map/ppermute | solution.py:932
  62.0 3.9 %collective-permute-start.9 = (f32[8,768]{1,0:T(8,128)S(1)}, f32[8,768]{1,0:T(8,128)S(1)}, u32[]{:S(2)}, u32[]{:S(2)}) collective-permute-start(f32[8,768]{1,0:T(8,128)S(1)} %pair_forces.7.outer), channel_id=1, source_target_pairs={{0,1},{1,0},{2,3},{3,2},{4,5},{5,4},{6,7},{7,6},{8,9},{9,8},{10,11... | collective-permute-start | bytes 73736 | tf_op jit(solution)/shard_map/ppermute | solution.py:952

commit v5 on v4

--- a/solution.py
+++ b/solution.py
@@ -188,8 +188,8 @@
 
 def begin_kernel(chunks, bead, left, strengths, pos, *refs):
     mine, theirs, straight = refs[:3]
-    blocks = refs[3:-4]
-    whole, table, rows, sems = refs[-4:]
+    whole, table, rows, spare, sems = refs[-5:]
+    blocks = list(refs[3:-5]) + [spare.at[i] for i in range(chunks)]
     lanes = blocks[0].shape[2]
     slab = whole.shape[1]
     starts, copies = [], []
@@ -235,33 +235,37 @@
         pl.when(bead[0] == which)(functools.partial(sides, which))
 
 
-def fetch_kernel(chunks, bead, mom, *refs):
+def fetch_kernel(moves, chunks, bead, pos, mom, *refs):
     *blocks, sems = refs
     lanes = blocks[0].shape[2]
     copies = []
-    for i, block in reversed(list(enumerate(blocks))):
-        owner = bead[0] if i < chunks else 1 - bead[0]
-        start = pl.multiple_of((owner * chunks + i % chunks) * lanes, TILE)
-        copy = pltpu.make_async_copy(mom.at[:, :, pl.ds(start, lanes)], block, sems.at[i])
+    for i, (block, plane, source, owner, chunk) in enumerate(moves):
+        side = bead[0] if owner == 0 else 1 - bead[0]
+        start = pl.multiple_of((side * chunks + chunk) * lanes, TILE)
+        copy = pltpu.make_async_copy(
+            (pos, mom)[source].at[:, :, pl.ds(start, lanes)],
+            blocks[block].at[pl.ds(plane, 3)],
+            sems.at[i],
+        )
         copy.start()
         copies.append(copy)
     for copy in copies:
         copy.wait()
 
 
-def fetch(chunks, bead, mom):
+def fetch(moves, planes, chunks, bead, pos, mom):
     beads, slab = mom.shape[1:]
-    count = 2 * chunks
+    lanes = slab // (2 * chunks)
     return pl.pallas_call(
-        functools.partial(fetch_kernel, chunks),
-        in_specs=[IN_SMEM, pl.BlockSpec(memory_space=pl.ANY)],
-        out_specs=[IN_VMEM] * count,
-        out_shape=[vmem_out((3, beads, slab // count), F32)] * count,
-        scratch_shapes=[pltpu.SemaphoreType.DMA((count,))],
+        functools.partial(fetch_kernel, moves, chunks),
+        in_specs=[IN_SMEM] + [pl.BlockSpec(memory_space=pl.ANY)] * 2,
+        out_specs=[IN_VMEM] * len(planes),
+        out_shape=[vmem_out((n, beads, lanes), F32) for n in planes],
+        scratch_shapes=[pltpu.SemaphoreType.DMA((len(moves),))],
         compiler_params=PARAMS,
         cost_estimate=COST,
         name="fetch",
-    )(bead, far(mom))
+    )(bead, far(pos), far(mom))
 
 
 def begin(chunks, bead, left, strengths, pos):
@@ -269,7 +273,7 @@
     block, rim = slab // 2, GT * TILE
     lanes = block // chunks
     shapes = [(ROWS, block + rim), (8, 3 * (block + 2 * rim) // 2), (ROWS, rim)]
-    shapes += [(3, beads, lanes)] * (2 * chunks)
+    shapes += [(3, beads, lanes)] * chunks
     return pl.pallas_call(
         functools.partial(begin_kernel, chunks),
         in_specs=[IN_SMEM] + [pl.BlockSpec(memory_space=pl.ANY)] * 3,
@@ -279,6 +283,7 @@
             pltpu.VMEM((ROWS, slab), F32),
             pltpu.VMEM(left.shape[1:], left.dtype),
             pltpu.VMEM(strengths.shape, F32),
+            pltpu.VMEM((chunks, 3, beads, lanes), F32),
             pltpu.SemaphoreType.DMA((2 * chunks + 2,)),
         ],
         compiler_params=PARAMS,
@@ -535,9 +540,9 @@
     return jnp.concatenate([outer[:, :rim], inner, outer[:, rim:]], axis=1)
 
 
-def step_kernel(parts, forces, chunk, chunks, group, edge, bead, *refs):
-    pieces = refs[: 2 * parts]
-    at = 2 * parts
+def step_kernel(parts, count, forces, chunk, chunks, group, edge, bead, *refs):
+    pieces = refs[:count]
+    at = count
     force = refs[at] if forces == 1 else whole_force(*refs[at : at + 2])
     at += forces
     mass_rows, strength_rows, hot, motion, expand, contract = refs[at : at + 6]
@@ -556,10 +561,11 @@
     masses = per_atom(mass_rows)
     inverse = 1.0 / masses
 
+    places = [(piece, plane) for piece in pieces for plane in range(0, piece.shape[0], 3)]
+
     def gathered(kind, c):
-        if parts == 1:
-            return pieces[kind][c]
-        return jnp.concatenate([piece[c] for piece in pieces[kind::2]], axis=0)
+        found = [piece[plane + c] for piece, plane in places[kind::2]]
+        return found[0] if parts == 1 else jnp.concatenate(found, axis=0)
 
     q = [gathered(0, c) for c in range(3)]
     p = [gathered(1, c) for c in range(3)]
@@ -627,18 +633,17 @@
 
 
 def substeps(chunk, chunks, bead, pieces, force, mass, strength, hot, motion, expand, contract, edge, before):
-    parts = len(pieces) // 2
-    lanes = pieces[0].shape[2]
-    beads = BEADS // parts
+    beads, lanes = pieces[0].shape[1:]
+    parts = BEADS // beads
     extra = [before] if edge and chunk else []
     shapes = [(6, beads, lanes)] * parts + [(ROWS, lanes)]
     if edge:
         shapes += [(ROWS, GT * TILE)] * 2
     return pl.pallas_call(
         functools.partial(
-            step_kernel, parts, len(force), chunk, chunks, lanes // TILE, int(edge)
+            step_kernel, parts, len(pieces), len(force), chunk, chunks, lanes // TILE, int(edge)
         ),
-        in_specs=[IN_SMEM] + [IN_VMEM] * (2 * parts + len(force) + 6 + len(extra)),
+        in_specs=[IN_SMEM] + [IN_VMEM] * (len(pieces) + len(force) + 6 + len(extra)),
         out_specs=[IN_VMEM] * len(shapes),
         out_shape=[vmem_out(s, F32) for s in shapes],
         compiler_params=PARAMS,
@@ -848,15 +853,20 @@
 
     pieces = [[] for _ in range(chunks)]
     if pair:
-        mine, theirs, straight, *blocks = begin(
-            chunks, bead_at, begin_left, strength, pos
-        )
+        (lead,) = fetch([(0, 0, 0, 1, 0)], [3], chunks, bead_at, pos, mom)
+        other = lax.ppermute(lead, "bead", SWAP)
+        mine, theirs, straight, *own_q = begin(chunks, bead_at, begin_left, strength, pos)
         theirs = lax.ppermute(theirs, "bead", SWAP)
-        moments = fetch(chunks, bead_at, mom)
+        moves = [(0, 0, 1, 1, 0)]
+        for chunk in range(1, chunks):
+            moves += [(chunk, 0, 0, 1, chunk), (chunk, 3, 1, 1, chunk)]
+        moves += [(chunks + chunk, 0, 1, 0, chunk) for chunk in range(chunks)]
+        planes = [3] + [6] * (chunks - 1) + [3] * chunks
+        blocks = fetch(moves, planes, chunks, bead_at, pos, mom)
         for chunk in range(chunks):
-            other = lax.ppermute(blocks[chunks + chunk], "bead", SWAP)
-            moment = lax.ppermute(moments[chunks + chunk], "bead", SWAP)
-            pieces[chunk] = [blocks[chunk], moments[chunk], other, moment]
+            moment = lax.ppermute(blocks[chunk], "bead", SWAP)
+            pieces[chunk] = [own_q[chunk], blocks[chunks + chunk]]
+            pieces[chunk] += [moment] if chunk else [other, moment]
         straight = relay(straight, theirs)
         straight = lax.ppermute(
             straight, ("space", "bead"), permutation(lambda b: -1 if b else 1, 0)
@@ -885,8 +895,7 @@
                 )
                 back = [(i, (i - d) % bead_count) for i in range(bead_count)]
                 parts.append(lax.ppermute(piece, "bead", back) if d else piece)
-            whole = jnp.concatenate(parts, 1)
-            pieces[chunk] = [whole[:3], whole[3:]]
+            pieces[chunk] = [jnp.concatenate(parts, 1)]
 
     hot = prepare(bead_at, bond_ends, angle_ends, block_tiles)
     if pair:

time: 67.4 us -> 67.5 us (level)
  starting transfers between devices: 16.1 us -> 14.2 us
  Pallas kernels: 26.8 us -> 27.8 us
  waiting for transfers between devices: 22.6 us -> 23.5 us
    ppermute x1, starting transfers between devices: 1.95 us -> 0.14 us  [body(): theirs = lax.ppermute(theirs, 'bead', SWAP)]
    pallas_call x3 -> x4, Pallas kernels: 8.71 us -> 9.7 us  [the longest x2 7.44 us: substeps(): pl.pallas_call(functools.partial(step_kernel, parts, len(pieces), len(for...]
    ppermute x1, waiting for transfers between devices: 14.1 us -> 15.1 us  [body(): theirs = lax.ppermute(theirs, 'bead', SWAP)]
    ppermute x4 -> x3, starting transfers between devices: 5.23 us -> 5.15 us  [the longest x2 5.07 us: body(): moment = lax.ppermute(blocks[chunk], 'bead', SWAP)]
  transfers between devices with their start and end apart: 12 -> 11, of which waited for: 3 -> 3; matrix products, arithmetic and copies ran while one was open for 0% -> 0% of each run, Pallas kernels for 36% -> 38%
where the time goes in v5:
time: 67.5 us; the launch traced here: 67.2 us
  Pallas kernels  27.8 us (41%)
  waiting for transfers between devices  23.5 us (35%)
  starting transfers between devices  14.2 us (21%)
  between operations  0.99 us (1%)
  local copies, waits for them, and re-layouts  0.73 us (1%)
    ppermute x1, waiting for transfers between devices, body(): theirs = lax.ppermute(theirs, 'bead', SWAP)  15.1 us
    pallas_call x4, Pallas kernels, pair_forces(): pl.pallas_call(functools.partial(pair_kernel, spots, sizes, own_count, pa...  13.3 us
    pallas_call x2, Pallas kernels, substeps(): pl.pallas_call(functools.partial(step_kernel, parts, len(pieces), len(for...  7.44 us
    ppermute x1, waiting for transfers between devices, body(): beside = lax.ppermute(bead_edge, 'bead', SWAP)  6.23 us
    ppermute x2, starting transfers between devices, body(): moment = lax.ppermute(blocks[chunk], 'bead', SWAP)  5.07 us
    ppermute x2, starting transfers between devices, body(): back.append(lax.ppermute(outs[d], 'bead', on))  4.25 us
    pallas_call x2, Pallas kernels, fetch(): pl.pallas_call(functools.partial(fetch_kernel, moves, chunks), in_specs=[...  2.26 us
    ppermute x1, waiting for transfers between devices, body(): outer = lax.ppermute(outer, 'bead', SWAP)  2.15 us
  transfers between devices with their start and end apart: 11, of which 3 were waited for; matrix products, arithmetic and copies ran while one was open for 0% of the time, Pallas kernels for 38%

profile of v5, /device:TPU:0, one launch (start us, length us, event | category | flops | bytes accessed | tf_op | source)
XLA Modules:
  0.0 67.2 jit_solution(4949505144160166391)
XLA Ops:
  0.6 1.3 %fetch.2 = (f32[3,16,1024]{2,1,0:T(8,128)S(1)}, f32[6,16,1024]{2,1,0:T(8,128)S(1)}, f32[3,16,1024]{2,1,0:T(8,128)S(1)}, f32[3,16,1024]{2,1,0:T(8,128)S(1)}) custom-call(s32[1]{0:T(128)} %bitcast.bead, f32[3,16,4096]{2,1,0:T(8,128)} %bitcast.13, f32[3,16,4096]{2,1,0:T(8,128)} %bitcast.16), custom_call_target="tpu_custom_call" | custom-call | flops 10000000 | bytes 100000 | tf_op jit(solution)/shard_map/fetch/pallas_call | solution.py:259
  2.0 3.1 %collective-permute-start.4 = (f32[6,16,1024]{2,1,0:T(8,128)S(1)}, f32[6,16,1024]{2,1,0:T(8,128)S(1)}, u32[]{:S(2)}, u32[]{:S(2)}) collective-permute-start(f32[6,16,1024]{2,1,0:T(8,128)S(1)} %get-tuple-element.32), channel_id=1, source_target_pairs={{0,1},{1,0},{2,3},{3,2},{4,5},{5,4},{6,7},{7,6},{8,9},{9,8},{10,11... | collective-permute-start | bytes 1179656 | tf_op jit(solution)/shard_map/ppermute | solution.py:867
  5.0 0.9 %fetch.3 = f32[3,16,1024]{2,1,0:T(8,128)S(1)} custom-call(s32[1]{0:T(128)} %bitcast.bead, f32[3,16,4096]{2,1,0:T(8,128)} %bitcast.14, f32[3,16,4096]{2,1,0:T(8,128)} %bitcast.17), custom_call_target="tpu_custom_call" | custom-call | flops 10000000 | bytes 100000 | tf_op jit(solution)/shard_map/fetch/pallas_call | solution.py:259
  6.0 0.1 collective-permute-start
  6.1 2.0 %collective-permute-start.1 = (f32[3,16,1024]{2,1,0:T(8,128)S(1)}, f32[3,16,1024]{2,1,0:T(8,128)S(1)}, u32[]{:S(2)}, u32[]{:S(2)}) collective-permute-start(f32[3,16,1024]{2,1,0:T(8,128)S(1)} %get-tuple-element.25), channel_id=1, source_target_pairs={{0,1},{1,0},{2,3},{3,2},{4,5},{5,4},{6,7},{7,6},{8,9},{9,8},{10,11... | collective-permute-start | bytes 589832 | tf_op jit(solution)/shard_map/ppermute | solution.py:867
  8.1 1.9 %begin.1 = (f32[16,2304]{1,0:T(8,128)S(1)}, f32[8,3840]{1,0:T(8,128)S(1)}, f32[16,256]{1,0:T(8,128)S(1)}, f32[3,16,1024]{2,1,0:T(8,128)S(1)}, f32[3,16,1024]{2,1,0:T(8,128)S(1)}) custom-call(s32[1]{0:T(128)} %bitcast.bead, bf16[2,48,144]{2,1,0:T(8,128)(2,1)} %constant.18.clone.left, f32[32,128]{1,0:T(8,128)} %bitcast.8, f32[3,16,4096]{2,1,0:T(8,128)} %bitcast.15), custom_call_target="tpu_custom_call" | custom-call | flops 10000000 | bytes 100000 | tf_op jit(solution)/shard_map/begin/pallas_call | solution.py:277
  10.0 0.1 collective-permute-start.2
  10.1 15.1 %collective-permute-done.2.refs_1_.received.refs_3_.refs_5_ = f32[8,3840]{1,0:T(8,128)S(1)} collective-permute-done((f32[8,3840]{1,0:T(8,128)S(1)}, f32[8,3840]{1,0:T(8,128)S(1)}, u32[]{:S(2)}, u32[]{:S(2)}) %collective-permute-start.2) | collective-permute-done | bytes 122912 | tf_op jit(solution)/shard_map/ppermute | solution.py:859
  25.2 0.0 copy-start.6
  25.2 0.1 collective-permute-start.3
  25.3 0.7 %copy-done.6 = s32[2,4096]{1,0:T(2,128)S(1)} copy-done((s32[2,4096]{1,0:T(2,128)S(1)}, s32[2,4096]{1,0:T(2,128)}, u32[]{:S(2)}) %copy-start.6) | copy-done | bytes 32792
  26.0 0.0 copy-done.7
  26.0 0.7 prepare.1.refs_8_.refs_7_
  26.6 4.4 %pair_forces.4.refs_4_.refs_3_ = f32[8,2304]{1,0:T(8,128)S(1)} custom-call(s32[1]{0:T(128)} %bitcast.bead, s32[1]{0:T(128)} %bitcast.1.space, s32[3,32]{1,0:T(4,128)} %nbr.7, f32[16,2304]{1,0:T(8,128)S(1)} %get-tuple-element.26.refs_0_.refs_2_.refs_4_, f32[8,3840]{1,0:T(8,128)S(1)} %collective-permute-done.2.refs_1_.received.refs_3_.refs_5_), custom_call_target="tpu_custom_call" | custom-call | flops 10000000 | bytes 100000 | tf_op jit(solution)/shard_map/pair_forces/pallas_call | solution.py:515
  31.1 0.0 copy-start
  31.1 0.0 copy-start.2
  31.1 0.0 copy-start.4
  31.1 0.0 collective-permute-done.3.refs_6_
  31.1 0.0 copy-start.3
  31.2 0.0 copy-start.5
  31.2 2.3 %pair_forces.5.refs_5_.refs_4_ = f32[8,768]{1,0:T(8,128)S(1)} custom-call(s32[1]{0:T(128)} %bitcast.bead, s32[1]{0:T(128)} %bitcast.1.space, s32[3,32]{1,0:T(4,128)} %nbr.7, f32[16,2304]{1,0:T(8,128)S(1)} %get-tuple-element.26.refs_0_.refs_2_.refs_4_, f32[8,3840]{1,0:T(8,128)S(1)} %collective-permute-done.2.refs_1_.received.refs_3_.refs_5_, ...), custom_call_target="tpu_custom_call" | custom-call | flops 10000000 | bytes 100000 | tf_op jit(solution)/shard_map/pair_forces/pallas_call | solution.py:515
  33.4 0.0 collective-permute-done.refs_2_
  33.4 0.0 collective-permute-done.1.refs_3_
  33.5 0.0 copy-done
  33.5 0.0 copy-done.2
  33.5 0.0 copy-done.4
  33.5 0.0 copy-done.3
  33.5 0.0 copy-done.5
  33.5 3.7 %substeps.2 = (f32[6,16,1024]{2,1,0:T(8,128)S(1)}, f32[6,16,1024]{2,1,0:T(8,128)S(1)}, f32[16,1024]{1,0:T(8,128)S(1)}) custom-call(s32[1]{0:T(128)} %bitcast.bead, f32[3,16,1024]{2,1,0:T(8,128)S(1)} %get-tuple-element.23.refs_0_, f32[3,16,1024]{2,1,0:T(8,128)S(1)} %get-tuple-element.24.refs_1_, f32[3,16,1024]{2,1,0:T(8,128)S(1)} %collective-permute-done.refs_2_, ...), custom_call_target="tpu_custom_call" | custom-call | flops 10000000 | bytes 100000 | tf_op jit(solution)/shard_map/substeps/pallas_call | solution.py:642
  37.2 4.2 %collective-permute-start.9 = (f32[6,16,1024]{2,1,0:T(8,128)S(1)}, f32[6,16,1024]{2,1,0:T(8,128)S(1)}, u32[]{:S(2)}, u32[]{:S(2)}) collective-permute-start(f32[6,16,1024]{2,1,0:T(8,128)S(1)} %get-tuple-element.36), channel_id=1, source_target_pairs={{0,1},{1,0},{2,3},{3,2},{4,5},{5,4},{6,7},{7,6},{8,9},{9,8},{10,11... | collective-permute-start | bytes 1179656 | tf_op jit(solution)/shard_map/ppermute | solution.py:926
  41.4 0.0 collective-permute-done.4.refs_2_
  41.4 3.7 %substeps.3 = (f32[6,16,1024]{2,1,0:T(8,128)S(1)}, f32[6,16,1024]{2,1,0:T(8,128)S(1)}, f32[16,1024]{1,0:T(8,128)S(1)}, f32[16,256]{1,0:T(8,128)S(1)}, f32[16,256]{1,0:T(8,128)S(1)}) custom-call(s32[1]{0:T(128)} %bitcast.bead, f32[3,16,1024]{2,1,0:T(8,128)S(1)} %get-tuple-element.30.refs_0_, f32[3,16,1024]{2,1,0:T(8,128)S(1)} %get-tuple-element.31.refs_1_, ...), custom_call_target="tpu_custom_call" | custom-call | flops 10000000 | bytes 100000 | tf_op jit(solution)/shard_map/substeps/pallas_call | solution.py:642
  45.1 0.1 collective-permute-start.10
  45.2 4.5 %pair_forces.6.inner = f32[8,2304]{1,0:T(8,128)S(1)} custom-call(s32[1]{0:T(128)} %bitcast.bead, s32[1]{0:T(128)} %bitcast.1.space, s32[3,32]{1,0:T(4,128)} %nbr.7, f32[16,1024]{1,0:T(8,128)S(1)} %get-tuple-element.29.refs_11_.refs_0_, f32[16,1024]{1,0:T(8,128)S(1)} %get-tuple-element.33.refs_1_), custom_call_target="tpu_custom_call" | custom-call | flops 10000000 | bytes 100000 | tf_op jit(solution)/shard_map/pair_forces/pallas_call | solution.py:515
  49.8 2.1 %collective-permute-start.5 = (f32[8,2304]{1,0:T(8,128)S(1)}, f32[8,2304]{1,0:T(8,128)S(1)}, u32[]{:S(2)}, u32[]{:S(2)}) collective-permute-start(f32[8,2304]{1,0:T(8,128)S(1)} %pair_forces.6.inner), channel_id=1, source_target_pairs={{0,1},{1,0},{2,3},{3,2},{4,5},{5,4},{6,7},{7,6},{8,9},{9,8},{10,11... | collective-permute-start | bytes 221192 | tf_op jit(solution)/shard_map/ppermute | solution.py:960
  51.8 0.1 collective-permute-start.6
  51.9 1.8 %collective-permute-start.7 = (f32[16,256]{1,0:T(8,128)S(1)}, f32[16,256]{1,0:T(8,128)S(1)}, u32[]{:S(2)}, u32[]{:S(2)}) collective-permute-start(f32[16,256]{1,0:T(8,128)S(1)} %get-tuple-element.35), channel_id=1, source_target_pairs={{0,31},{1,2},{2,1},{3,4},{4,3},{5,6},{6,5},{7,8},{8,7},{9,10},{10,... | collective-permute-start | bytes 49160 | tf_op jit(solution)/shard_map/ppermute | solution.py:941
  53.7 6.2 %collective-permute-done.6.refs_2_ = f32[16,256]{1,0:T(8,128)S(1)} collective-permute-done((f32[16,256]{1,0:T(8,128)S(1)}, f32[16,256]{1,0:T(8,128)S(1)}, u32[]{:S(2)}, u32[]{:S(2)}) %collective-permute-start.6) | collective-permute-done | bytes 16416 | tf_op jit(solution)/shard_map/ppermute | solution.py:940
  59.9 0.0 collective-permute-done.7.refs_3_
  59.9 2.1 %pair_forces.7.outer = f32[8,768]{1,0:T(8,128)S(1)} custom-call(s32[1]{0:T(128)} %bitcast.bead, s32[1]{0:T(128)} %bitcast.1.space, s32[3,32]{1,0:T(4,128)} %nbr.7, f32[16,1024]{1,0:T(8,128)S(1)} %get-tuple-element.29.refs_11_.refs_0_, f32[16,1024]{1,0:T(8,128)S(1)} %get-tuple-element.33.refs_1_, f32[16,256]{1,0:T(8,128)S(1)} %collective-permute-done.6.refs_2_, ...), custom_call_target="tpu_custom_call" | custom-call | flops 10000000 | bytes 100000 | tf_op jit(solution)/shard_map/pair_forces/pallas_call | solution.py:515
  62.0 0.7 collective-permute-start.8
  62.7 0.0 collective-permute-done.9.refs_2_.refs_0_
  62.7 0.0 copy-done.1
  62.7 1.1 %finish_block.2 = (f32[3,16,4096]{2,1,0:T(8,128)}, f32[3,16,4096]{2,1,0:T(8,128)}) custom-call(s32[1]{0:T(128)} %bitcast.bead, bf16[2,3,48,48]{3,2,1,0:T(8,128)(2,1)S(1)} %copy-done.1, f32[8,2304]{1,0:T(8,128)S(1)} %pair_forces.6.inner, f32[8,768]{1,0:T(8,128)S(1)} %pair_forces.7.outer, f32[6,16,1024]{2,1,0:T(8,128)S(1)} %get-tuple-element.38.refs_0_, ...), custom_call_target="tpu_custom_call" | custom-call | flops 10000000 | bytes 100000 | tf_op jit(solution)/shard_map/finish_block/pallas_call | solution.py:729
  63.8 2.1 %collective-permute-done.8.outer = f32[8,768]{1,0:T(8,128)S(1)} collective-permute-done((f32[8,768]{1,0:T(8,128)S(1)}, f32[8,768]{1,0:T(8,128)S(1)}, u32[]{:S(2)}, u32[]{:S(2)}) %collective-permute-start.8) | collective-permute-done | bytes 24608 | tf_op jit(solution)/shard_map/ppermute | solution.py:961
  65.9 0.0 collective-permute-done.5.inner
  65.9 0.0 collective-permute-done.10.refs_1_
  65.9 1.1 %finish_block.3 = (f32[3,16,4096]{2,1,0:T(8,128)}, f32[3,16,4096]{2,1,0:T(8,128)}) custom-call(s32[1]{0:T(128)} %bitcast.bead, bf16[2,3,48,48]{3,2,1,0:T(8,128)(2,1)S(1)} %copy-done.1, f32[8,2304]{1,0:T(8,128)S(1)} %collective-permute-done.5.inner, f32[8,768]{1,0:T(8,128)S(1)} %collective-permute-done.8.outer, ...), custom_call_target="tpu_custom_call", output_to_operand_aliasing={{0}: (6, {}), {1}: (7, {})} | custom-call | flops 10000000 | bytes 100000 | tf_op jit(solution)/shard_map/finish_block/pallas_call | solution.py:729
  (3 shorter events, 0.0 us)
Async XLA Ops:
  2.0 39.5 %collective-permute-start.4 = (f32[6,16,1024]{2,1,0:T(8,128)S(1)}, f32[6,16,1024]{2,1,0:T(8,128)S(1)}, u32[]{:S(2)}, u32[]{:S(2)}) collective-permute-start(f32[6,16,1024]{2,1,0:T(8,128)S(1)} %get-tuple-element.32), channel_id=1, source_target_pairs={{0,1},{1,0},{2,3},{3,2},{4,5},{5,4},{6,7},{7,6},{8,9},{9,8},{10,11... | collective-permute-start | bytes 1179656 | tf_op jit(solution)/shard_map/ppermute | solution.py:867
  6.0 27.5 %collective-permute-start = (f32[3,16,1024]{2,1,0:T(8,128)S(1)}, f32[3,16,1024]{2,1,0:T(8,128)S(1)}, u32[]{:S(2)}, u32[]{:S(2)}) collective-permute-start(f32[3,16,1024]{2,1,0:T(8,128)S(1)} %fetch.3), channel_id=1, source_target_pairs={{0,1},{1,0},{2,3},{3,2},{4,5},{5,4},{6,7},{7,6},{8,9},{9,8},{10,11... | collective-permute-start | bytes 589832 | tf_op jit(solution)/shard_map/ppermute | solution.py:857
  6.1 27.4 %collective-permute-start.1 = (f32[3,16,1024]{2,1,0:T(8,128)S(1)}, f32[3,16,1024]{2,1,0:T(8,128)S(1)}, u32[]{:S(2)}, u32[]{:S(2)}) collective-permute-start(f32[3,16,1024]{2,1,0:T(8,128)S(1)} %get-tuple-element.25), channel_id=1, source_target_pairs={{0,1},{1,0},{2,3},{3,2},{4,5},{5,4},{6,7},{7,6},{8,9},{9,8},{10,11... | collective-permute-start | bytes 589832 | tf_op jit(solution)/shard_map/ppermute | solution.py:867
  10.0 15.2 %collective-permute-start.2 = (f32[8,3840]{1,0:T(8,128)S(1)}, f32[8,3840]{1,0:T(8,128)S(1)}, u32[]{:S(2)}, u32[]{:S(2)}) collective-permute-start(f32[8,3840]{1,0:T(8,128)S(1)} %get-tuple-element.27), channel_id=1, source_target_pairs={{0,1},{1,0},{2,3},{3,2},{4,5},{5,4},{6,7},{7,6},{8,9},{9,8},{10,11... | collective-permute-start | bytes 368648 | tf_op jit(solution)/shard_map/ppermute | solution.py:859
  25.2 0.8 %copy-start.6 = (s32[2,4096]{1,0:T(2,128)S(1)}, s32[2,4096]{1,0:T(2,128)}, u32[]{:S(2)}) copy-start(s32[2,4096]{1,0:T(2,128)} %bonds.1) | copy-start | bytes 98308
  25.2 0.8 %copy-start.7 = (s32[3,2048]{1,0:T(4,128)S(1)}, s32[3,2048]{1,0:T(4,128)}, u32[]{:S(2)}) copy-start(s32[3,2048]{1,0:T(4,128)} %angles.1) | copy-start | bytes 73732
  25.2 5.9 %collective-permute-start.3 = (f32[16,256]{1,0:T(8,128)S(1)}, f32[16,256]{1,0:T(8,128)S(1)}, u32[]{:S(2)}, u32[]{:S(2)}) collective-permute-start(f32[16,256]{1,0:T(8,128)S(1)} %relay.1), channel_id=1, source_target_pairs={{0,2},{1,31},{2,4},{3,1},{4,6},{5,3},{6,8},{7,5},{8,10},{9,7},{10,... | collective-permute-start | bytes 49160 | tf_op jit(solution)/shard_map/ppermute | solution.py:871
  31.1 2.4 %copy-start = (bf16[2,288,48]{2,1,0:T(8,128)(2,1)S(1)}, bf16[2,288,48]{2,1,0:T(8,128)(2,1)}, u32[]{:S(2)}) copy-start(bf16[2,288,48]{2,1,0:T(8,128)(2,1)} %constant.21.clone.refs_10_.refs_9_) | copy-start | bytes 165892
  31.1 2.4 %copy-start.2 = (bf16[128,256]{1,0:T(8,128)(2,1)S(1)}, bf16[128,256]{1,0:T(8,128)(2,1)}, u32[]{:S(2)}) copy-start(bf16[128,256]{1,0:T(8,128)(2,1)} %constant.22.clone.refs_9_.refs_8_) | copy-start | bytes 196612
  31.1 2.4 %copy-start.4 = (bf16[2,32,192]{2,1,0:T(8,128)(2,1)S(1)}, bf16[2,32,192]{2,1,0:T(8,128)(2,1)}, u32[]{:S(2)}) copy-start(bf16[2,32,192]{2,1,0:T(8,128)(2,1)} %constant.20.clone.refs_11_.refs_10_) | copy-start | bytes 73732
  31.1 2.3 %copy-start.3 = (f32[4096]{0:T(1024)S(1)}, f32[4096]{0:T(1024)}, u32[]{:S(2)}) copy-start(f32[4096]{0:T(1024)} %param.15) | copy-start | bytes 49156
  31.2 2.3 %copy-start.5 = (f32[4096]{0:T(1024)S(1)}, f32[4096]{0:T(1024)}, u32[]{:S(2)}) copy-start(f32[4096]{0:T(1024)} %param.14) | copy-start | bytes 49156
  37.2 25.5 %collective-permute-start.9 = (f32[6,16,1024]{2,1,0:T(8,128)S(1)}, f32[6,16,1024]{2,1,0:T(8,128)S(1)}, u32[]{:S(2)}, u32[]{:S(2)}) collective-permute-start(f32[6,16,1024]{2,1,0:T(8,128)S(1)} %get-tuple-element.36), channel_id=1, source_target_pairs={{0,1},{1,0},{2,3},{3,2},{4,5},{5,4},{6,7},{7,6},{8,9},{9,8},{10,11... | collective-permute-start | bytes 1179656 | tf_op jit(solution)/shard_map/ppermute | solution.py:926
  45.1 20.8 %collective-permute-start.10 = (f32[6,16,1024]{2,1,0:T(8,128)S(1)}, f32[6,16,1024]{2,1,0:T(8,128)S(1)}, u32[]{:S(2)}, u32[]{:S(2)}) collective-permute-start(f32[6,16,1024]{2,1,0:T(8,128)S(1)} %get-tuple-element.37), channel_id=1, source_target_pairs={{0,1},{1,0},{2,3},{3,2},{4,5},{5,4},{6,7},{7,6},{8,9},{9,8},{10,11... | collective-permute-start | bytes 1179656 | tf_op jit(solution)/shard_map/ppermute | solution.py:926
  49.8 16.2 %collective-permute-start.5 = (f32[8,2304]{1,0:T(8,128)S(1)}, f32[8,2304]{1,0:T(8,128)S(1)}, u32[]{:S(2)}, u32[]{:S(2)}) collective-permute-start(f32[8,2304]{1,0:T(8,128)S(1)} %pair_forces.6.inner), channel_id=1, source_target_pairs={{0,1},{1,0},{2,3},{3,2},{4,5},{5,4},{6,7},{7,6},{8,9},{9,8},{10,11... | collective-permute-start | bytes 221192 | tf_op jit(solution)/shard_map/ppermute | solution.py:960
  51.8 8.1 %collective-permute-start.6 = (f32[16,256]{1,0:T(8,128)S(1)}, f32[16,256]{1,0:T(8,128)S(1)}, u32[]{:S(2)}, u32[]{:S(2)}) collective-permute-start(f32[16,256]{1,0:T(8,128)S(1)} %get-tuple-element.34), channel_id=1, source_target_pairs={{0,1},{1,0},{2,3},{3,2},{4,5},{5,4},{6,7},{7,6},{8,9},{9,8},{10,11... | collective-permute-start | bytes 49160 | tf_op jit(solution)/shard_map/ppermute | solution.py:940
  51.9 10.8 %copy-start.1 = (bf16[2,3,48,48]{3,2,1,0:T(8,128)(2,1)S(1)}, bf16[2,3,48,48]{3,2,1,0:T(8,128)(2,1)}, u32[]{:S(2)}) copy-start(bf16[2,3,48,48]{3,2,1,0:T(8,128)(2,1)} %constant.19.clone.expand) | copy-start | bytes 82948
  51.9 8.0 %collective-permute-start.7 = (f32[16,256]{1,0:T(8,128)S(1)}, f32[16,256]{1,0:T(8,128)S(1)}, u32[]{:S(2)}, u32[]{:S(2)}) collective-permute-start(f32[16,256]{1,0:T(8,128)S(1)} %get-tuple-element.35), channel_id=1, source_target_pairs={{0,31},{1,2},{2,1},{3,4},{4,3},{5,6},{6,5},{7,8},{8,7},{9,10},{10,... | collective-permute-start | bytes 49160 | tf_op jit(solution)/shard_map/ppermute | solution.py:941
  62.0 3.9 %collective-permute-start.8 = (f32[8,768]{1,0:T(8,128)S(1)}, f32[8,768]{1,0:T(8,128)S(1)}, u32[]{:S(2)}, u32[]{:S(2)}) collective-permute-start(f32[8,768]{1,0:T(8,128)S(1)} %pair_forces.7.outer), channel_id=1, source_target_pairs={{0,1},{1,0},{2,3},{3,2},{4,5},{5,4},{6,7},{7,6},{8,9},{9,8},{10,11... | collective-permute-start | bytes 73736 | tf_op jit(solution)/shard_map/ppermute | solution.py:961

commit v6 on v5

--- a/solution.py
+++ b/solution.py
@@ -239,12 +239,12 @@
     *blocks, sems = refs
     lanes = blocks[0].shape[2]
     copies = []
-    for i, (block, plane, source, owner, chunk) in enumerate(moves):
+    for i, (block, plane, source, comp, comps, owner, chunk) in enumerate(moves):
         side = bead[0] if owner == 0 else 1 - bead[0]
         start = pl.multiple_of((side * chunks + chunk) * lanes, TILE)
         copy = pltpu.make_async_copy(
-            (pos, mom)[source].at[:, :, pl.ds(start, lanes)],
-            blocks[block].at[pl.ds(plane, 3)],
+            (pos, mom)[source].at[pl.ds(comp, comps), :, pl.ds(start, lanes)],
+            blocks[block].at[pl.ds(plane, comps)],
             sems.at[i],
         )
         copy.start()
@@ -561,10 +561,11 @@
     masses = per_atom(mass_rows)
     inverse = 1.0 / masses
 
-    places = [(piece, plane) for piece in pieces for plane in range(0, piece.shape[0], 3)]
+    planes = [(piece, plane) for piece in pieces for plane in range(piece.shape[0])]
 
     def gathered(kind, c):
-        found = [piece[plane + c] for piece, plane in places[kind::2]]
+        found = [planes[6 * part + 3 * kind + c] for part in range(parts)]
+        found = [piece[plane] for piece, plane in found]
         return found[0] if parts == 1 else jnp.concatenate(found, axis=0)
 
     q = [gathered(0, c) for c in range(3)]
@@ -853,16 +854,18 @@
 
     pieces = [[] for _ in range(chunks)]
     if pair:
-        (lead,) = fetch([(0, 0, 0, 1, 0)], [3], chunks, bead_at, pos, mom)
+        (lead,) = fetch([(0, 0, 0, 0, 2, 1, 0)], [2], chunks, bead_at, pos, mom)
         other = lax.ppermute(lead, "bead", SWAP)
         mine, theirs, straight, *own_q = begin(chunks, bead_at, begin_left, strength, pos)
         theirs = lax.ppermute(theirs, "bead", SWAP)
-        moves = [(0, 0, 1, 1, 0)]
+        moves = [(0, 0, 0, 2, 1, 1, 0), (0, 1, 1, 0, 3, 1, 0)]
+        blocks = fetch(moves, [4], chunks, bead_at, pos, mom)
+        moves = []
         for chunk in range(1, chunks):
-            moves += [(chunk, 0, 0, 1, chunk), (chunk, 3, 1, 1, chunk)]
-        moves += [(chunks + chunk, 0, 1, 0, chunk) for chunk in range(chunks)]
-        planes = [3] + [6] * (chunks - 1) + [3] * chunks
-        blocks = fetch(moves, planes, chunks, bead_at, pos, mom)
+            moves += [(chunk - 1, 0, 0, 0, 3, 1, chunk), (chunk - 1, 3, 1, 0, 3, 1, chunk)]
+        moves += [(chunks - 1 + chunk, 0, 1, 0, 3, 0, chunk) for chunk in range(chunks)]
+        planes = [6] * (chunks - 1) + [3] * chunks
+        blocks += fetch(moves, planes, chunks, bead_at, pos, mom)
         for chunk in range(chunks):
             moment = lax.ppermute(blocks[chunk], "bead", SWAP)
             pieces[chunk] = [own_q[chunk], blocks[chunks + chunk]]

time: 67.5 us -> 65.8 us (0.975)
  waiting for transfers between devices: 23.5 us -> 20.6 us
  Pallas kernels: 27.8 us -> 28.7 us
    ppermute x1, waiting for transfers between devices: 15.1 us -> 12.2 us  [body(): theirs = lax.ppermute(theirs, 'bead', SWAP)]
    ppermute x1, starting transfers between devices: 0.14 us -> 2.07 us  [body(): theirs = lax.ppermute(theirs, 'bead', SWAP)]
    ppermute x2, starting transfers between devices: 5.07 us -> 3.15 us  [body(): moment = lax.ppermute(blocks[chunk], 'bead', SWAP)]
    ppermute x1, starting transfers between devices: 1.79 us -> 2.93 us  [body(): lax.ppermute(far_edge, ('space', 'bead'), permutation(lambda b: 1 if b el...]
    pallas_call x2 -> x3, Pallas kernels: 2.26 us -> 3.15 us  [fetch(): pl.pallas_call(functools.partial(fetch_kernel, moves, chunks), in_specs=[...]
    ppermute x2, starting transfers between devices: 4.25 us -> 3.38 us  [body(): back.append(lax.ppermute(outs[d], 'bead', on))]
  transfers between devices with their start and end apart: 11 -> 11, of which waited for: 3 -> 3; matrix products, arithmetic and copies ran while one was open for 0% -> 0% of each run, Pallas kernels for 38% -> 40%
where the time goes in v6:
time: 65.8 us; the launch traced here: 65.5 us
  Pallas kernels  28.7 us (44%)
  waiting for transfers between devices  20.6 us (31%)
  starting transfers between devices  14.5 us (22%)
  between operations  1 us (2%)
  local copies, waits for them, and re-layouts  0.73 us (1%)
    pallas_call x4, Pallas kernels, pair_forces(): pl.pallas_call(functools.partial(pair_kernel, spots, sizes, own_count, pa...  13.4 us
    ppermute x1, waiting for transfers between devices, body(): theirs = lax.ppermute(theirs, 'bead', SWAP)  12.2 us
    pallas_call x2, Pallas kernels, substeps(): pl.pallas_call(functools.partial(step_kernel, parts, len(pieces), len(for...  7.47 us
    ppermute x1, waiting for transfers between devices, body(): beside = lax.ppermute(bead_edge, 'bead', SWAP)  6.23 us
    ppermute x2, starting transfers between devices, body(): back.append(lax.ppermute(outs[d], 'bead', on))  3.38 us
    pallas_call x3, Pallas kernels, fetch(): pl.pallas_call(functools.partial(fetch_kernel, moves, chunks), in_specs=[...  3.15 us
    ppermute x2, starting transfers between devices, body(): moment = lax.ppermute(blocks[chunk], 'bead', SWAP)  3.15 us
    ppermute x1, starting transfers between devices, body(): lax.ppermute(far_edge, ('space', 'bead'), permutation(lambda b: 1 if b el...  2.93 us
  transfers between devices with their start and end apart: 11, of which 3 were waited for; matrix products, arithmetic and copies ran while one was open for 0% of the time, Pallas kernels for 40%

profile of v6, /device:TPU:0, one launch (start us, length us, event | category | flops | bytes accessed | tf_op | source)
XLA Modules:
  0.0 65.5 jit_solution(14952555335221474438)
XLA Ops:
  0.6 1.3 %fetch.3 = (f32[6,16,1024]{2,1,0:T(8,128)S(1)}, f32[3,16,1024]{2,1,0:T(8,128)S(1)}, f32[3,16,1024]{2,1,0:T(8,128)S(1)}) custom-call(s32[1]{0:T(128)} %bitcast.bead, f32[3,16,4096]{2,1,0:T(8,128)} %bitcast.13, f32[3,16,4096]{2,1,0:T(8,128)} %bitcast.17), custom_call_target="tpu_custom_call" | custom-call | flops 10000000 | bytes 100000 | tf_op jit(solution)/shard_map/fetch/pallas_call | solution.py:259
  1.9 3.1 %collective-permute-start.4 = (f32[6,16,1024]{2,1,0:T(8,128)S(1)}, f32[6,16,1024]{2,1,0:T(8,128)S(1)}, u32[]{:S(2)}, u32[]{:S(2)}) collective-permute-start(f32[6,16,1024]{2,1,0:T(8,128)S(1)} %get-tuple-element.30), channel_id=1, source_target_pairs={{0,1},{1,0},{2,3},{3,2},{4,5},{5,4},{6,7},{7,6},{8,9},{9,8},{10,11... | collective-permute-start | bytes 1179656 | tf_op jit(solution)/shard_map/ppermute | solution.py:870
  5.0 1.0 %fetch.5 = f32[4,16,1024]{2,1,0:T(8,128)S(1)} custom-call(s32[1]{0:T(128)} %bitcast.bead, f32[3,16,4096]{2,1,0:T(8,128)} %bitcast.14, f32[3,16,4096]{2,1,0:T(8,128)} %bitcast.18), custom_call_target="tpu_custom_call" | custom-call | flops 10000000 | bytes 100000 | tf_op jit(solution)/shard_map/fetch/pallas_call | solution.py:259
  6.0 0.1 collective-permute-start.1
  6.0 1.9 %begin.1 = (f32[16,2304]{1,0:T(8,128)S(1)}, f32[8,3840]{1,0:T(8,128)S(1)}, f32[16,256]{1,0:T(8,128)S(1)}, f32[3,16,1024]{2,1,0:T(8,128)S(1)}, f32[3,16,1024]{2,1,0:T(8,128)S(1)}) custom-call(s32[1]{0:T(128)} %bitcast.bead, bf16[2,48,144]{2,1,0:T(8,128)(2,1)} %constant.18.clone.left, f32[32,128]{1,0:T(8,128)} %bitcast.8, f32[3,16,4096]{2,1,0:T(8,128)} %bitcast.15), custom_call_target="tpu_custom_call" | custom-call | flops 10000000 | bytes 100000 | tf_op jit(solution)/shard_map/begin/pallas_call | solution.py:277
  7.9 2.1 %collective-permute-start.2 = (f32[8,3840]{1,0:T(8,128)S(1)}, f32[8,3840]{1,0:T(8,128)S(1)}, u32[]{:S(2)}, u32[]{:S(2)}) collective-permute-start(f32[8,3840]{1,0:T(8,128)S(1)} %get-tuple-element.25), channel_id=1, source_target_pairs={{0,1},{1,0},{2,3},{3,2},{4,5},{5,4},{6,7},{7,6},{8,9},{9,8},{10,11... | collective-permute-start | bytes 368648 | tf_op jit(solution)/shard_map/ppermute | solution.py:860
  10.0 0.9 %fetch.4 = f32[2,16,1024]{2,1,0:T(8,128)S(1)} custom-call(s32[1]{0:T(128)} %bitcast.bead, f32[3,16,4096]{2,1,0:T(8,128)} %bitcast.16, f32[3,16,4096]{2,1,0:T(8,128)} %bitcast.19), custom_call_target="tpu_custom_call" | custom-call | flops 10000000 | bytes 100000 | tf_op jit(solution)/shard_map/fetch/pallas_call | solution.py:259
  10.9 0.1 collective-permute-start
  11.0 12.2 %collective-permute-done.2.refs_1_.received.refs_3_.refs_5_ = f32[8,3840]{1,0:T(8,128)S(1)} collective-permute-done((f32[8,3840]{1,0:T(8,128)S(1)}, f32[8,3840]{1,0:T(8,128)S(1)}, u32[]{:S(2)}, u32[]{:S(2)}) %collective-permute-start.2) | collective-permute-done | bytes 122912 | tf_op jit(solution)/shard_map/ppermute | solution.py:860
  23.2 0.1 collective-permute-start.3
  23.3 0.7 %copy-done.6 = s32[2,4096]{1,0:T(2,128)S(1)} copy-done((s32[2,4096]{1,0:T(2,128)S(1)}, s32[2,4096]{1,0:T(2,128)}, u32[]{:S(2)}) %copy-start.6) | copy-done | bytes 32792
  23.9 0.0 copy-done.7
  24.0 0.7 %prepare.1.refs_8_.refs_7_ = bf16[16,128,256]{2,1,0:T(8,128)(2,1)S(1)} custom-call(s32[1]{0:T(128)} %bitcast.bead, s32[2,4096]{1,0:T(2,128)S(1)} %copy-done.6, s32[3,2048]{1,0:T(4,128)S(1)} %copy-done.7), custom_call_target="tpu_custom_call" | custom-call | flops 10000000 | bytes 100000 | tf_op jit(solution)/shard_map/prepare/pallas_call | solution.py:373
  24.6 4.4 %pair_forces.4.refs_4_.refs_3_ = f32[8,2304]{1,0:T(8,128)S(1)} custom-call(s32[1]{0:T(128)} %bitcast.bead, s32[1]{0:T(128)} %bitcast.1.space, s32[3,32]{1,0:T(4,128)} %nbr.7, f32[16,2304]{1,0:T(8,128)S(1)} %get-tuple-element.24.refs_0_.refs_2_.refs_4_, f32[8,3840]{1,0:T(8,128)S(1)} %collective-permute-done.2.refs_1_.received.refs_3_.refs_5_), custom_call_target="tpu_custom_call" | custom-call | flops 10000000 | bytes 100000 | tf_op jit(solution)/shard_map/pair_forces/pallas_call | solution.py:515
  29.1 0.0 copy-start
  29.1 0.0 copy-start.2
  29.1 0.0 copy-start.4
  29.1 0.0 collective-permute-done.3.refs_6_
  29.1 0.0 copy-start.3
  29.1 0.0 copy-start.5
  29.1 2.3 %pair_forces.5.refs_5_.refs_4_ = f32[8,768]{1,0:T(8,128)S(1)} custom-call(s32[1]{0:T(128)} %bitcast.bead, s32[1]{0:T(128)} %bitcast.1.space, s32[3,32]{1,0:T(4,128)} %nbr.7, f32[16,2304]{1,0:T(8,128)S(1)} %get-tuple-element.24.refs_0_.refs_2_.refs_4_, f32[8,3840]{1,0:T(8,128)S(1)} %collective-permute-done.2.refs_1_.received.refs_3_.refs_5_, ...), custom_call_target="tpu_custom_call" | custom-call | flops 10000000 | bytes 100000 | tf_op jit(solution)/shard_map/pair_forces/pallas_call | solution.py:515
  31.4 0.0 collective-permute-done.refs_2_
  31.4 0.0 collective-permute-done.1.refs_3_
  31.4 0.0 copy-done
  31.4 0.0 copy-done.2
  31.5 0.0 copy-done.4
  31.5 0.0 copy-done.3
  31.5 0.0 copy-done.5
  31.5 3.7 %substeps.2 = (f32[6,16,1024]{2,1,0:T(8,128)S(1)}, f32[6,16,1024]{2,1,0:T(8,128)S(1)}, f32[16,1024]{1,0:T(8,128)S(1)}) custom-call(s32[1]{0:T(128)} %bitcast.bead, f32[3,16,1024]{2,1,0:T(8,128)S(1)} %get-tuple-element.22.refs_0_, f32[3,16,1024]{2,1,0:T(8,128)S(1)} %get-tuple-element.23.refs_1_, f32[2,16,1024]{2,1,0:T(8,128)S(1)} %collective-permute-done.refs_2_, ...), custom_call_target="tpu_custom_call" | custom-call | flops 10000000 | bytes 100000 | tf_op jit(solution)/shard_map/substeps/pallas_call | solution.py:643
  35.2 3.3 %collective-permute-start.9 = (f32[6,16,1024]{2,1,0:T(8,128)S(1)}, f32[6,16,1024]{2,1,0:T(8,128)S(1)}, u32[]{:S(2)}, u32[]{:S(2)}) collective-permute-start(f32[6,16,1024]{2,1,0:T(8,128)S(1)} %get-tuple-element.34), channel_id=1, source_target_pairs={{0,1},{1,0},{2,3},{3,2},{4,5},{5,4},{6,7},{7,6},{8,9},{9,8},{10,11... | collective-permute-start | bytes 1179656 | tf_op jit(solution)/shard_map/ppermute | solution.py:929
  38.5 0.0 collective-permute-done.4.refs_2_
  38.5 3.7 %substeps.3 = (f32[6,16,1024]{2,1,0:T(8,128)S(1)}, f32[6,16,1024]{2,1,0:T(8,128)S(1)}, f32[16,1024]{1,0:T(8,128)S(1)}, f32[16,256]{1,0:T(8,128)S(1)}, f32[16,256]{1,0:T(8,128)S(1)}) custom-call(s32[1]{0:T(128)} %bitcast.bead, f32[3,16,1024]{2,1,0:T(8,128)S(1)} %get-tuple-element.28.refs_0_, f32[3,16,1024]{2,1,0:T(8,128)S(1)} %get-tuple-element.29.refs_1_, ...), custom_call_target="tpu_custom_call" | custom-call | flops 10000000 | bytes 100000 | tf_op jit(solution)/shard_map/substeps/pallas_call | solution.py:643
  42.3 0.1 collective-permute-start.10
  42.3 4.6 %pair_forces.6.inner = f32[8,2304]{1,0:T(8,128)S(1)} custom-call(s32[1]{0:T(128)} %bitcast.bead, s32[1]{0:T(128)} %bitcast.1.space, s32[3,32]{1,0:T(4,128)} %nbr.7, f32[16,1024]{1,0:T(8,128)S(1)} %get-tuple-element.27.refs_11_.refs_0_, f32[16,1024]{1,0:T(8,128)S(1)} %get-tuple-element.31.refs_1_), custom_call_target="tpu_custom_call" | custom-call | flops 10000000 | bytes 100000 | tf_op jit(solution)/shard_map/pair_forces/pallas_call | solution.py:515
  46.9 2.1 %collective-permute-start.5 = (f32[8,2304]{1,0:T(8,128)S(1)}, f32[8,2304]{1,0:T(8,128)S(1)}, u32[]{:S(2)}, u32[]{:S(2)}) collective-permute-start(f32[8,2304]{1,0:T(8,128)S(1)} %pair_forces.6.inner), channel_id=1, source_target_pairs={{0,1},{1,0},{2,3},{3,2},{4,5},{5,4},{6,7},{7,6},{8,9},{9,8},{10,11... | collective-permute-start | bytes 221192 | tf_op jit(solution)/shard_map/ppermute | solution.py:963
  49.0 0.1 collective-permute-start.6
  49.1 2.9 %collective-permute-start.7 = (f32[16,256]{1,0:T(8,128)S(1)}, f32[16,256]{1,0:T(8,128)S(1)}, u32[]{:S(2)}, u32[]{:S(2)}) collective-permute-start(f32[16,256]{1,0:T(8,128)S(1)} %get-tuple-element.33), channel_id=1, source_target_pairs={{0,31},{1,2},{2,1},{3,4},{4,3},{5,6},{6,5},{7,8},{8,7},{9,10},{10,... | collective-permute-start | bytes 49160 | tf_op jit(solution)/shard_map/ppermute | solution.py:944
  52.0 6.2 %collective-permute-done.6.refs_2_ = f32[16,256]{1,0:T(8,128)S(1)} collective-permute-done((f32[16,256]{1,0:T(8,128)S(1)}, f32[16,256]{1,0:T(8,128)S(1)}, u32[]{:S(2)}, u32[]{:S(2)}) %collective-permute-start.6) | collective-permute-done | bytes 16416 | tf_op jit(solution)/shard_map/ppermute | solution.py:943
  58.2 0.0 collective-permute-done.7.refs_3_
  58.2 2.1 %pair_forces.7.outer = f32[8,768]{1,0:T(8,128)S(1)} custom-call(s32[1]{0:T(128)} %bitcast.bead, s32[1]{0:T(128)} %bitcast.1.space, s32[3,32]{1,0:T(4,128)} %nbr.7, f32[16,1024]{1,0:T(8,128)S(1)} %get-tuple-element.27.refs_11_.refs_0_, f32[16,1024]{1,0:T(8,128)S(1)} %get-tuple-element.31.refs_1_, f32[16,256]{1,0:T(8,128)S(1)} %collective-permute-done.6.refs_2_, ...), custom_call_target="tpu_custom_call" | custom-call | flops 10000000 | bytes 100000 | tf_op jit(solution)/shard_map/pair_forces/pallas_call | solution.py:515
  60.3 0.6 collective-permute-start.8
  61.0 0.0 collective-permute-done.9.refs_2_.refs_0_
  61.0 0.0 copy-done.1
  61.0 1.1 %finish_block.2 = (f32[3,16,4096]{2,1,0:T(8,128)}, f32[3,16,4096]{2,1,0:T(8,128)}) custom-call(s32[1]{0:T(128)} %bitcast.bead, bf16[2,3,48,48]{3,2,1,0:T(8,128)(2,1)S(1)} %copy-done.1, f32[8,2304]{1,0:T(8,128)S(1)} %pair_forces.6.inner, f32[8,768]{1,0:T(8,128)S(1)} %pair_forces.7.outer, f32[6,16,1024]{2,1,0:T(8,128)S(1)} %get-tuple-element.36.refs_0_, ...), custom_call_target="tpu_custom_call" | custom-call | flops 10000000 | bytes 100000 | tf_op jit(solution)/shard_map/finish_block/pallas_call | solution.py:730
  62.1 2.2 %collective-permute-done.8.outer = f32[8,768]{1,0:T(8,128)S(1)} collective-permute-done((f32[8,768]{1,0:T(8,128)S(1)}, f32[8,768]{1,0:T(8,128)S(1)}, u32[]{:S(2)}, u32[]{:S(2)}) %collective-permute-start.8) | collective-permute-done | bytes 24608 | tf_op jit(solution)/shard_map/ppermute | solution.py:964
  64.2 0.0 collective-permute-done.5.inner
  64.2 0.0 collective-permute-done.10.refs_1_
  64.2 1.1 %finish_block.3 = (f32[3,16,4096]{2,1,0:T(8,128)}, f32[3,16,4096]{2,1,0:T(8,128)}) custom-call(s32[1]{0:T(128)} %bitcast.bead, bf16[2,3,48,48]{3,2,1,0:T(8,128)(2,1)S(1)} %copy-done.1, f32[8,2304]{1,0:T(8,128)S(1)} %collective-permute-done.5.inner, f32[8,768]{1,0:T(8,128)S(1)} %collective-permute-done.8.outer, ...), custom_call_target="tpu_custom_call", output_to_operand_aliasing={{0}: (6, {}), {1}: (7, {})} | custom-call | flops 10000000 | bytes 100000 | tf_op jit(solution)/shard_map/finish_block/pallas_call | solution.py:730
  (4 shorter events, 0.0 us)
Async XLA Ops:
  1.9 36.6 %collective-permute-start.4 = (f32[6,16,1024]{2,1,0:T(8,128)S(1)}, f32[6,16,1024]{2,1,0:T(8,128)S(1)}, u32[]{:S(2)}, u32[]{:S(2)}) collective-permute-start(f32[6,16,1024]{2,1,0:T(8,128)S(1)} %get-tuple-element.30), channel_id=1, source_target_pairs={{0,1},{1,0},{2,3},{3,2},{4,5},{5,4},{6,7},{7,6},{8,9},{9,8},{10,11... | collective-permute-start | bytes 1179656 | tf_op jit(solution)/shard_map/ppermute | solution.py:870
  6.0 25.5 %collective-permute-start.1 = (f32[4,16,1024]{2,1,0:T(8,128)S(1)}, f32[4,16,1024]{2,1,0:T(8,128)S(1)}, u32[]{:S(2)}, u32[]{:S(2)}) collective-permute-start(f32[4,16,1024]{2,1,0:T(8,128)S(1)} %fetch.5), channel_id=1, source_target_pairs={{0,1},{1,0},{2,3},{3,2},{4,5},{5,4},{6,7},{7,6},{8,9},{9,8},{10,11... | collective-permute-start | bytes 786440 | tf_op jit(solution)/shard_map/ppermute | solution.py:870
  7.9 15.2 %collective-permute-start.2 = (f32[8,3840]{1,0:T(8,128)S(1)}, f32[8,3840]{1,0:T(8,128)S(1)}, u32[]{:S(2)}, u32[]{:S(2)}) collective-permute-start(f32[8,3840]{1,0:T(8,128)S(1)} %get-tuple-element.25), channel_id=1, source_target_pairs={{0,1},{1,0},{2,3},{3,2},{4,5},{5,4},{6,7},{7,6},{8,9},{9,8},{10,11... | collective-permute-start | bytes 368648 | tf_op jit(solution)/shard_map/ppermute | solution.py:860
  10.9 20.5 %collective-permute-start = (f32[2,16,1024]{2,1,0:T(8,128)S(1)}, f32[2,16,1024]{2,1,0:T(8,128)S(1)}, u32[]{:S(2)}, u32[]{:S(2)}) collective-permute-start(f32[2,16,1024]{2,1,0:T(8,128)S(1)} %fetch.4), channel_id=1, source_target_pairs={{0,1},{1,0},{2,3},{3,2},{4,5},{5,4},{6,7},{7,6},{8,9},{9,8},{10,11... | collective-permute-start | bytes 393224 | tf_op jit(solution)/shard_map/ppermute | solution.py:858
  23.2 0.8 %copy-start.6 = (s32[2,4096]{1,0:T(2,128)S(1)}, s32[2,4096]{1,0:T(2,128)}, u32[]{:S(2)}) copy-start(s32[2,4096]{1,0:T(2,128)} %bonds.1) | copy-start | bytes 98308
  23.2 0.8 %copy-start.7 = (s32[3,2048]{1,0:T(4,128)S(1)}, s32[3,2048]{1,0:T(4,128)}, u32[]{:S(2)}) copy-start(s32[3,2048]{1,0:T(4,128)} %angles.1) | copy-start | bytes 73732
  23.2 5.9 %collective-permute-start.3 = (f32[16,256]{1,0:T(8,128)S(1)}, f32[16,256]{1,0:T(8,128)S(1)}, u32[]{:S(2)}, u32[]{:S(2)}) collective-permute-start(f32[16,256]{1,0:T(8,128)S(1)} %relay.1), channel_id=1, source_target_pairs={{0,2},{1,31},{2,4},{3,1},{4,6},{5,3},{6,8},{7,5},{8,10},{9,7},{10,... | collective-permute-start | bytes 49160 | tf_op jit(solution)/shard_map/ppermute | solution.py:874
  29.1 2.4 %copy-start = (bf16[2,288,48]{2,1,0:T(8,128)(2,1)S(1)}, bf16[2,288,48]{2,1,0:T(8,128)(2,1)}, u32[]{:S(2)}) copy-start(bf16[2,288,48]{2,1,0:T(8,128)(2,1)} %constant.21.clone.refs_10_.refs_9_) | copy-start | bytes 165892
  29.1 2.4 %copy-start.2 = (bf16[128,256]{1,0:T(8,128)(2,1)S(1)}, bf16[128,256]{1,0:T(8,128)(2,1)}, u32[]{:S(2)}) copy-start(bf16[128,256]{1,0:T(8,128)(2,1)} %constant.22.clone.refs_9_.refs_8_) | copy-start | bytes 196612
  29.1 2.4 %copy-start.4 = (bf16[2,32,192]{2,1,0:T(8,128)(2,1)S(1)}, bf16[2,32,192]{2,1,0:T(8,128)(2,1)}, u32[]{:S(2)}) copy-start(bf16[2,32,192]{2,1,0:T(8,128)(2,1)} %constant.20.clone.refs_11_.refs_10_) | copy-start | bytes 73732
  29.1 2.3 %copy-start.3 = (f32[4096]{0:T(1024)S(1)}, f32[4096]{0:T(1024)}, u32[]{:S(2)}) copy-start(f32[4096]{0:T(1024)} %param.15) | copy-start | bytes 49156
  29.1 2.3 %copy-start.5 = (f32[4096]{0:T(1024)S(1)}, f32[4096]{0:T(1024)}, u32[]{:S(2)}) copy-start(f32[4096]{0:T(1024)} %param.14) | copy-start | bytes 49156
  35.2 25.8 %collective-permute-start.9 = (f32[6,16,1024]{2,1,0:T(8,128)S(1)}, f32[6,16,1024]{2,1,0:T(8,128)S(1)}, u32[]{:S(2)}, u32[]{:S(2)}) collective-permute-start(f32[6,16,1024]{2,1,0:T(8,128)S(1)} %get-tuple-element.34), channel_id=1, source_target_pairs={{0,1},{1,0},{2,3},{3,2},{4,5},{5,4},{6,7},{7,6},{8,9},{9,8},{10,11... | collective-permute-start | bytes 1179656 | tf_op jit(solution)/shard_map/ppermute | solution.py:929
  42.3 22.0 %collective-permute-start.10 = (f32[6,16,1024]{2,1,0:T(8,128)S(1)}, f32[6,16,1024]{2,1,0:T(8,128)S(1)}, u32[]{:S(2)}, u32[]{:S(2)}) collective-permute-start(f32[6,16,1024]{2,1,0:T(8,128)S(1)} %get-tuple-element.35), channel_id=1, source_target_pairs={{0,1},{1,0},{2,3},{3,2},{4,5},{5,4},{6,7},{7,6},{8,9},{9,8},{10,11... | collective-permute-start | bytes 1179656 | tf_op jit(solution)/shard_map/ppermute | solution.py:929
  46.9 17.3 %collective-permute-start.5 = (f32[8,2304]{1,0:T(8,128)S(1)}, f32[8,2304]{1,0:T(8,128)S(1)}, u32[]{:S(2)}, u32[]{:S(2)}) collective-permute-start(f32[8,2304]{1,0:T(8,128)S(1)} %pair_forces.6.inner), channel_id=1, source_target_pairs={{0,1},{1,0},{2,3},{3,2},{4,5},{5,4},{6,7},{7,6},{8,9},{9,8},{10,11... | collective-permute-start | bytes 221192 | tf_op jit(solution)/shard_map/ppermute | solution.py:963
  49.0 9.2 %collective-permute-start.6 = (f32[16,256]{1,0:T(8,128)S(1)}, f32[16,256]{1,0:T(8,128)S(1)}, u32[]{:S(2)}, u32[]{:S(2)}) collective-permute-start(f32[16,256]{1,0:T(8,128)S(1)} %get-tuple-element.32), channel_id=1, source_target_pairs={{0,1},{1,0},{2,3},{3,2},{4,5},{5,4},{6,7},{7,6},{8,9},{9,8},{10,11... | collective-permute-start | bytes 49160 | tf_op jit(solution)/shard_map/ppermute | solution.py:943
  49.1 11.9 %copy-start.1 = (bf16[2,3,48,48]{3,2,1,0:T(8,128)(2,1)S(1)}, bf16[2,3,48,48]{3,2,1,0:T(8,128)(2,1)}, u32[]{:S(2)}) copy-start(bf16[2,3,48,48]{3,2,1,0:T(8,128)(2,1)} %constant.19.clone.expand) | copy-start | bytes 82948
  49.1 9.2 %collective-permute-start.7 = (f32[16,256]{1,0:T(8,128)S(1)}, f32[16,256]{1,0:T(8,128)S(1)}, u32[]{:S(2)}, u32[]{:S(2)}) collective-permute-start(f32[16,256]{1,0:T(8,128)S(1)} %get-tuple-element.33), channel_id=1, source_target_pairs={{0,31},{1,2},{2,1},{3,4},{4,3},{5,6},{6,5},{7,8},{8,7},{9,10},{10,... | collective-permute-start | bytes 49160 | tf_op jit(solution)/shard_map/ppermute | solution.py:944
  60.3 3.9 %collective-permute-start.8 = (f32[8,768]{1,0:T(8,128)S(1)}, f32[8,768]{1,0:T(8,128)S(1)}, u32[]{:S(2)}, u32[]{:S(2)}) collective-permute-start(f32[8,768]{1,0:T(8,128)S(1)} %pair_forces.7.outer), channel_id=1, source_target_pairs={{0,1},{1,0},{2,3},{3,2},{4,5},{5,4},{6,7},{7,6},{8,9},{9,8},{10,11... | collective-permute-start | bytes 73736 | tf_op jit(solution)/shard_map/ppermute | solution.py:964

commit v7 on v6

--- a/solution.py
+++ b/solution.py
@@ -488,7 +488,7 @@
         lane = t * TILE if isinstance(t, int) else pl.multiple_of(t * TILE, TILE)
         out[:, pl.ds(lane, TILE)] = result
 
-    unroll = math.gcd(own_count, 4)
+    unroll = own_count if own_count <= 6 else math.gcd(own_count, 4)
     weigh(0, weights[0])
 
     def some_tiles(t, last):
@@ -543,7 +543,7 @@
 def step_kernel(parts, count, forces, chunk, chunks, group, edge, bead, *refs):
     pieces = refs[:count]
     at = count
-    force = refs[at] if forces == 1 else whole_force(*refs[at : at + 2])
+    force = refs[at : at + forces]
     at += forces
     mass_rows, strength_rows, hot, motion, expand, contract = refs[at : at + 6]
     before = refs[at + 6] if edge and chunk else None
@@ -570,7 +570,11 @@
 
     q = [gathered(0, c) for c in range(3)]
     p = [gathered(1, c) for c in range(3)]
-    kick = exact(expand[bead[0]], force[:, first * TILE : first * TILE + width])
+    if force[0].shape[0] == ROWS:
+        kicks = force[0][:, first * TILE : first * TILE + width]
+    else:
+        kicks = jnp.concatenate([unpacked(x[...]) for x in force], axis=1)
+    kick = exact(expand[bead[0]], kicks)
     v = [
         (p[c] + 0.5 * time_step * kick[c * BEADS : (c + 1) * BEADS]) * inverse for c in range(3)
     ]
@@ -821,6 +825,31 @@
 
         return lambda t: t + GT + info[0] * block_tiles, lambda t: t + GT, spot
 
+    def spots_start(info):
+        left_at = 2 * GT + jnp.where(info[0] == 0, GT, 0)
+
+        def spot(tile):
+            x = relative(tile, info) - info[0] * block_tiles
+            return jnp.where(x < 0, x + GT + left_at, x)
+
+        return lambda t: t + info[0] * block_tiles, lambda t: t, spot
+
+    def spots_late(info):
+        chunk_tiles = lanes // TILE
+        right_at = block_tiles - chunk_tiles + GT + jnp.where(info[0] == 0, 0, GT)
+
+        def place(x):
+            return x - chunk_tiles + GT
+
+        def spot(tile):
+            x = relative(tile, info) - info[0] * block_tiles
+            return jnp.where(x >= block_tiles, x - block_tiles + right_at, place(x))
+
+        def own(t):
+            return t + chunk_tiles
+
+        return lambda t: own(t) + info[0] * block_tiles, lambda t: place(own(t)), spot
+
     def spots_outer(info):
         bead_at = 4 * GT
         far_at = bead_at + GT
@@ -875,13 +904,12 @@
             straight, ("space", "bead"), permutation(lambda b: -1 if b else 1, 0)
         )
         both = [mine, theirs]
-        inside = [(both, lambda b: b * GT, block_tiles)]
-        rim_tiles = [
-            (both, lambda b: b * GT, 2 * GT),
-            (both, lambda b: b * GT + block_tiles - 2 * GT, 2 * GT),
-            (both, lambda b: (1 - b) * block_tiles, GT),
-            ([straight], 0, GT),
-        ]
+        edge_tiles = [(both, lambda b: (1 - b) * block_tiles, GT), ([straight], 0, GT)]
+        chunk_tiles = lanes // TILE
+        early = [(both, lambda b: b * GT, chunk_tiles + GT)]
+        start_tiles = [(both, lambda b: b * GT, 2 * GT)] + edge_tiles
+        late = [(both, lambda b: b * GT + chunk_tiles - GT, block_tiles - chunk_tiles + GT)]
+        late += edge_tiles
     else:
         part = partial_rows(bead_at, begin_left, strength, pos)
         summed = lax.psum(part, "bead")
@@ -903,14 +931,17 @@
     hot = prepare(bead_at, bond_ends, angle_ends, block_tiles)
     if pair:
         ids = bead_at, space_at, neighbour_tiles
-        inner = pair_forces(spots_inner, inside, block_tiles - 2 * GT, *ids, True)
-        outer = pair_forces(spots_outer, rim_tiles, 2 * GT, *ids, True)
-        force = [inner, outer]
+        inner = pair_forces(spots_inner, early, chunk_tiles - GT, *ids, True)
+        outer = pair_forces(spots_start, start_tiles, GT, *ids, True)
+        force = [outer, inner]
     else:
         force = [pair_forces(spots, segments, block_tiles, bead_at, space_at, neighbour_tiles)]
 
     own_out, returned, contracted = [], [], []
     for chunk in range(chunks):
+        if pair and chunk:
+            count = block_tiles - chunk_tiles
+            force = [pair_forces(spots_late, late, count, *ids, True)]
         last = pair and chunk == chunks - 1
         outs = substeps(
             chunk, chunks, bead_at, pieces[chunk], force, mass, strength, hot, motion,
@@ -944,7 +975,6 @@
     across = lax.ppermute(
         far_edge, ("space", "bead"), permutation(lambda b: 1 if b else -1, 1)
     )
-    chunk_tiles = lanes // TILE
     segments = [([x], 0, chunk_tiles) for x in contracted]
     inner = pair_forces(spots_inner, segments, block_tiles - 2 * GT, *ids, True)
     segments = [

time: 65.8 us -> 64.7 us (0.983)
  starting transfers between devices: 14.5 us -> 12.1 us
  Pallas kernels: 28.7 us -> 29.4 us
    ppermute x1, waiting for transfers between devices: 6.23 us -> 2.95 us  [body(): beside = lax.ppermute(bead_edge, 'bead', SWAP)]
    ppermute x1, waiting for transfers between devices: 0.01 us -> 1.88 us  [body(): lax.ppermute(straight, ('space', 'bead'), permutation(lambda b: -1 if b e...]
    ppermute x1, waiting for transfers between devices: 0.01 us -> 1.38 us  [body(): lax.ppermute(far_edge, ('space', 'bead'), permutation(lambda b: 1 if b el...]
    ppermute x2, starting transfers between devices: 3.38 us -> 2.11 us  [body(): back.append(lax.ppermute(outs[d], 'bead', on))]
    pallas_call x4 -> x5, Pallas kernels: 13.4 us -> 14.1 us  [pair_forces(): pl.pallas_call(functools.partial(pair_kernel, spots, sizes, own_count, pa...]
  transfers between devices with their start and end apart: 11 -> 11, of which waited for: 3 -> 5; matrix products, arithmetic and copies ran while one was open for 0% -> 0% of each run, Pallas kernels for 40% -> 42%
where the time goes in v7:
time: 64.7 us; the launch traced here: 64.3 us
  Pallas kernels  29.4 us (45%)
  waiting for transfers between devices  21.1 us (33%)
  starting transfers between devices  12.1 us (19%)
  between operations  1.02 us (2%)
  local copies, waits for them, and re-layouts  0.72 us (1%)
    pallas_call x5, Pallas kernels, pair_forces(): pl.pallas_call(functools.partial(pair_kernel, spots, sizes, own_count, pa...  14.1 us
    ppermute x1, waiting for transfers between devices, body(): theirs = lax.ppermute(theirs, 'bead', SWAP)  12.2 us
    pallas_call x2, Pallas kernels, substeps(): pl.pallas_call(functools.partial(step_kernel, parts, len(pieces), len(for...  7.45 us
    pallas_call x3, Pallas kernels, fetch(): pl.pallas_call(functools.partial(fetch_kernel, moves, chunks), in_specs=[...  3.15 us
    ppermute x2, starting transfers between devices, body(): moment = lax.ppermute(blocks[chunk], 'bead', SWAP)  3.15 us
    ppermute x1, waiting for transfers between devices, body(): beside = lax.ppermute(bead_edge, 'bead', SWAP)  2.95 us
    ppermute x1, waiting for transfers between devices, body(): outer = lax.ppermute(outer, 'bead', SWAP)  2.7 us
    ppermute x1, starting transfers between devices, body(): lax.ppermute(far_edge, ('space', 'bead'), permutation(lambda b: 1 if b el...  2.43 us
  transfers between devices with their start and end apart: 11, of which 5 were waited for; matrix products, arithmetic and copies ran while one was open for 0% of the time, Pallas kernels for 42%

profile of v7, /device:TPU:0, one launch (start us, length us, event | category | flops | bytes accessed | tf_op | source)
XLA Modules:
  0.0 64.3 jit_solution(10961393620852881389)
XLA Ops:
  0.6 1.3 %fetch.3 = (f32[6,16,1024]{2,1,0:T(8,128)S(1)}, f32[3,16,1024]{2,1,0:T(8,128)S(1)}, f32[3,16,1024]{2,1,0:T(8,128)S(1)}) custom-call(s32[1]{0:T(128)} %bitcast.bead, f32[3,16,4096]{2,1,0:T(8,128)} %bitcast.13, f32[3,16,4096]{2,1,0:T(8,128)} %bitcast.17), custom_call_target="tpu_custom_call" | custom-call | flops 10000000 | bytes 100000 | tf_op jit(solution)/shard_map/fetch/pallas_call | solution.py:259
  1.9 3.1 %collective-permute-start.4 = (f32[6,16,1024]{2,1,0:T(8,128)S(1)}, f32[6,16,1024]{2,1,0:T(8,128)S(1)}, u32[]{:S(2)}, u32[]{:S(2)}) collective-permute-start(f32[6,16,1024]{2,1,0:T(8,128)S(1)} %get-tuple-element.30), channel_id=1, source_target_pairs={{0,1},{1,0},{2,3},{3,2},{4,5},{5,4},{6,7},{7,6},{8,9},{9,8},{10,11... | collective-permute-start | bytes 1179656 | tf_op jit(solution)/shard_map/ppermute | solution.py:899
  5.0 1.0 %fetch.5 = f32[4,16,1024]{2,1,0:T(8,128)S(1)} custom-call(s32[1]{0:T(128)} %bitcast.bead, f32[3,16,4096]{2,1,0:T(8,128)} %bitcast.14, f32[3,16,4096]{2,1,0:T(8,128)} %bitcast.18), custom_call_target="tpu_custom_call" | custom-call | flops 10000000 | bytes 100000 | tf_op jit(solution)/shard_map/fetch/pallas_call | solution.py:259
  6.0 0.1 collective-permute-start.1
  6.0 1.9 %begin.1 = (f32[16,2304]{1,0:T(8,128)S(1)}, f32[8,3840]{1,0:T(8,128)S(1)}, f32[16,256]{1,0:T(8,128)S(1)}, f32[3,16,1024]{2,1,0:T(8,128)S(1)}, f32[3,16,1024]{2,1,0:T(8,128)S(1)}) custom-call(s32[1]{0:T(128)} %bitcast.bead, bf16[2,48,144]{2,1,0:T(8,128)(2,1)} %constant.18.clone.left, f32[32,128]{1,0:T(8,128)} %bitcast.8, f32[3,16,4096]{2,1,0:T(8,128)} %bitcast.15), custom_call_target="tpu_custom_call" | custom-call | flops 10000000 | bytes 100000 | tf_op jit(solution)/shard_map/begin/pallas_call | solution.py:277
  7.9 2.1 %collective-permute-start.2 = (f32[8,3840]{1,0:T(8,128)S(1)}, f32[8,3840]{1,0:T(8,128)S(1)}, u32[]{:S(2)}, u32[]{:S(2)}) collective-permute-start(f32[8,3840]{1,0:T(8,128)S(1)} %get-tuple-element.25), channel_id=1, source_target_pairs={{0,1},{1,0},{2,3},{3,2},{4,5},{5,4},{6,7},{7,6},{8,9},{9,8},{10,11... | collective-permute-start | bytes 368648 | tf_op jit(solution)/shard_map/ppermute | solution.py:889
  10.0 0.9 %fetch.4 = f32[2,16,1024]{2,1,0:T(8,128)S(1)} custom-call(s32[1]{0:T(128)} %bitcast.bead, f32[3,16,4096]{2,1,0:T(8,128)} %bitcast.16, f32[3,16,4096]{2,1,0:T(8,128)} %bitcast.19), custom_call_target="tpu_custom_call" | custom-call | flops 10000000 | bytes 100000 | tf_op jit(solution)/shard_map/fetch/pallas_call | solution.py:259
  10.9 0.1 collective-permute-start
  11.0 12.2 %collective-permute-done.2.received.refs_1_.refs_3_ = f32[8,3840]{1,0:T(8,128)S(1)} collective-permute-done((f32[8,3840]{1,0:T(8,128)S(1)}, f32[8,3840]{1,0:T(8,128)S(1)}, u32[]{:S(2)}, u32[]{:S(2)}) %collective-permute-start.2) | collective-permute-done | bytes 122912 | tf_op jit(solution)/shard_map/ppermute | solution.py:889
  23.2 0.0 copy-start.6
  23.2 0.1 collective-permute-start.3
  23.3 0.7 %copy-done.6 = s32[2,4096]{1,0:T(2,128)S(1)} copy-done((s32[2,4096]{1,0:T(2,128)S(1)}, s32[2,4096]{1,0:T(2,128)}, u32[]{:S(2)}) %copy-start.6) | copy-done | bytes 32792
  23.9 0.0 copy-done.7
  24.0 0.7 %prepare.1.refs_8_.refs_6_ = bf16[16,128,256]{2,1,0:T(8,128)(2,1)S(1)} custom-call(s32[1]{0:T(128)} %bitcast.bead, s32[2,4096]{1,0:T(2,128)S(1)} %copy-done.6, s32[3,2048]{1,0:T(4,128)S(1)} %copy-done.7), custom_call_target="tpu_custom_call" | custom-call | flops 10000000 | bytes 100000 | tf_op jit(solution)/shard_map/prepare/pallas_call | solution.py:373
  24.6 2.6 %pair_forces.6.refs_5_ = f32[8,1152]{1,0:T(8,128)S(1)} custom-call(s32[1]{0:T(128)} %bitcast.bead, s32[1]{0:T(128)} %bitcast.1.space, s32[3,32]{1,0:T(4,128)} %nbr.9, f32[16,2304]{1,0:T(8,128)S(1)} %get-tuple-element.24.refs_0_.refs_2_, f32[8,3840]{1,0:T(8,128)S(1)} %collective-permute-done.2.received.refs_1_.refs_3_), custom_call_target="tpu_custom_call" | custom-call | flops 10000000 | bytes 100000 | tf_op jit(solution)/shard_map/pair_forces/pallas_call | solution.py:515
  27.2 0.0 copy-start
  27.2 0.0 copy-start.2
  27.2 0.0 copy-start.4
  27.2 1.9 %collective-permute-done.3.refs_4_ = f32[16,256]{1,0:T(8,128)S(1)} collective-permute-done((f32[16,256]{1,0:T(8,128)S(1)}, f32[16,256]{1,0:T(8,128)S(1)}, u32[]{:S(2)}, u32[]{:S(2)}) %collective-permute-start.3) | collective-permute-done | bytes 16416 | tf_op jit(solution)/shard_map/ppermute | solution.py:903
  29.1 1.7 %pair_forces.5.refs_4_ = f32[8,384]{1,0:T(8,128)S(1)} custom-call(s32[1]{0:T(128)} %bitcast.bead, s32[1]{0:T(128)} %bitcast.1.space, s32[3,32]{1,0:T(4,128)} %nbr.9, f32[16,2304]{1,0:T(8,128)S(1)} %get-tuple-element.24.refs_0_.refs_2_, f32[8,3840]{1,0:T(8,128)S(1)} %collective-permute-done.2.received.refs_1_.refs_3_, ...), custom_call_target="tpu_custom_call" | custom-call | flops 10000000 | bytes 100000 | tf_op jit(solution)/shard_map/pair_forces/pallas_call | solution.py:515
  30.9 0.0 collective-permute-done.refs_2_
  30.9 0.0 collective-permute-done.1.refs_3_
  30.9 0.0 copy-done
  30.9 0.0 copy-done.2
  30.9 0.0 copy-done.4
  30.9 0.0 copy-done.3
  30.9 0.0 copy-done.5
  30.9 3.7 %substeps.2 = (f32[6,16,1024]{2,1,0:T(8,128)S(1)}, f32[6,16,1024]{2,1,0:T(8,128)S(1)}, f32[16,1024]{1,0:T(8,128)S(1)}) custom-call(s32[1]{0:T(128)} %bitcast.bead, f32[3,16,1024]{2,1,0:T(8,128)S(1)} %get-tuple-element.22.refs_0_, f32[3,16,1024]{2,1,0:T(8,128)S(1)} %get-tuple-element.23.refs_1_, f32[2,16,1024]{2,1,0:T(8,128)S(1)} %collective-permute-done.refs_2_, ...), custom_call_target="tpu_custom_call" | custom-call | flops 10000000 | bytes 100000 | tf_op jit(solution)/shard_map/substeps/pallas_call | solution.py:647
  34.7 1.5 %collective-permute-start.9 = (f32[6,16,1024]{2,1,0:T(8,128)S(1)}, f32[6,16,1024]{2,1,0:T(8,128)S(1)}, u32[]{:S(2)}, u32[]{:S(2)}) collective-permute-start(f32[6,16,1024]{2,1,0:T(8,128)S(1)} %get-tuple-element.34), channel_id=1, source_target_pairs={{0,1},{1,0},{2,3},{3,2},{4,5},{5,4},{6,7},{7,6},{8,9},{9,8},{10,11... | collective-permute-start | bytes 1179656 | tf_op jit(solution)/shard_map/ppermute | solution.py:960
  36.1 3.1 %pair_forces.7.refs_3_ = f32[8,1536]{1,0:T(8,128)S(1)} custom-call(s32[1]{0:T(128)} %bitcast.bead, s32[1]{0:T(128)} %bitcast.1.space, s32[3,32]{1,0:T(4,128)} %nbr.9, f32[16,2304]{1,0:T(8,128)S(1)} %get-tuple-element.24.refs_0_.refs_2_, f32[8,3840]{1,0:T(8,128)S(1)} %collective-permute-done.2.received.refs_1_.refs_3_, ...), custom_call_target="tpu_custom_call" | custom-call | flops 10000000 | bytes 100000 | tf_op jit(solution)/shard_map/pair_forces/pallas_call | solution.py:515
  39.2 0.0 collective-permute-done.4.refs_2_
  39.2 3.7 %substeps.3 = (f32[6,16,1024]{2,1,0:T(8,128)S(1)}, f32[6,16,1024]{2,1,0:T(8,128)S(1)}, f32[16,1024]{1,0:T(8,128)S(1)}, f32[16,256]{1,0:T(8,128)S(1)}, f32[16,256]{1,0:T(8,128)S(1)}) custom-call(s32[1]{0:T(128)} %bitcast.bead, f32[3,16,1024]{2,1,0:T(8,128)S(1)} %get-tuple-element.28.refs_0_, f32[3,16,1024]{2,1,0:T(8,128)S(1)} %get-tuple-element.29.refs_1_, ...), custom_call_target="tpu_custom_call" | custom-call | flops 10000000 | bytes 100000 | tf_op jit(solution)/shard_map/substeps/pallas_call | solution.py:647
  43.0 0.6 collective-permute-start.10
  43.6 4.6 %pair_forces.8.inner = f32[8,2304]{1,0:T(8,128)S(1)} custom-call(s32[1]{0:T(128)} %bitcast.bead, s32[1]{0:T(128)} %bitcast.1.space, s32[3,32]{1,0:T(4,128)} %nbr.9, f32[16,1024]{1,0:T(8,128)S(1)} %get-tuple-element.27.refs_10_.refs_0_, f32[16,1024]{1,0:T(8,128)S(1)} %get-tuple-element.31.refs_1_), custom_call_target="tpu_custom_call" | custom-call | flops 10000000 | bytes 100000 | tf_op jit(solution)/shard_map/pair_forces/pallas_call | solution.py:515
  48.2 1.5 %collective-permute-start.5 = (f32[8,2304]{1,0:T(8,128)S(1)}, f32[8,2304]{1,0:T(8,128)S(1)}, u32[]{:S(2)}, u32[]{:S(2)}) collective-permute-start(f32[8,2304]{1,0:T(8,128)S(1)} %pair_forces.8.inner), channel_id=1, source_target_pairs={{0,1},{1,0},{2,3},{3,2},{4,5},{5,4},{6,7},{7,6},{8,9},{9,8},{10,11... | collective-permute-start | bytes 221192 | tf_op jit(solution)/shard_map/ppermute | solution.py:993
  49.7 0.6 collective-permute-start.6
  50.3 2.4 %collective-permute-start.7 = (f32[16,256]{1,0:T(8,128)S(1)}, f32[16,256]{1,0:T(8,128)S(1)}, u32[]{:S(2)}, u32[]{:S(2)}) collective-permute-start(f32[16,256]{1,0:T(8,128)S(1)} %get-tuple-element.33), channel_id=1, source_target_pairs={{0,31},{1,2},{2,1},{3,4},{4,3},{5,6},{6,5},{7,8},{8,7},{9,10},{10,... | collective-permute-start | bytes 49160 | tf_op jit(solution)/shard_map/ppermute | solution.py:975
  52.7 2.9 %collective-permute-done.6.refs_2_ = f32[16,256]{1,0:T(8,128)S(1)} collective-permute-done((f32[16,256]{1,0:T(8,128)S(1)}, f32[16,256]{1,0:T(8,128)S(1)}, u32[]{:S(2)}, u32[]{:S(2)}) %collective-permute-start.6) | collective-permute-done | bytes 16416 | tf_op jit(solution)/shard_map/ppermute | solution.py:974
  55.6 1.4 %collective-permute-done.7.refs_3_ = f32[16,256]{1,0:T(8,128)S(1)} collective-permute-done((f32[16,256]{1,0:T(8,128)S(1)}, f32[16,256]{1,0:T(8,128)S(1)}, u32[]{:S(2)}, u32[]{:S(2)}) %collective-permute-start.7) | collective-permute-done | bytes 16416 | tf_op jit(solution)/shard_map/ppermute | solution.py:975
  57.0 2.1 %pair_forces.9.outer = f32[8,768]{1,0:T(8,128)S(1)} custom-call(s32[1]{0:T(128)} %bitcast.bead, s32[1]{0:T(128)} %bitcast.1.space, s32[3,32]{1,0:T(4,128)} %nbr.9, f32[16,1024]{1,0:T(8,128)S(1)} %get-tuple-element.27.refs_10_.refs_0_, f32[16,1024]{1,0:T(8,128)S(1)} %get-tuple-element.31.refs_1_, f32[16,256]{1,0:T(8,128)S(1)} %collective-permute-done.6.refs_2_, ...), custom_call_target="tpu_custom_call" | custom-call | flops 10000000 | bytes 100000 | tf_op jit(solution)/shard_map/pair_forces/pallas_call | solution.py:515
  59.1 0.1 collective-permute-start.8
  59.2 0.0 collective-permute-done.9.refs_2_.refs_0_
  59.2 0.0 copy-done.1
  59.2 1.1 %finish_block.2 = (f32[3,16,4096]{2,1,0:T(8,128)}, f32[3,16,4096]{2,1,0:T(8,128)}) custom-call(s32[1]{0:T(128)} %bitcast.bead, bf16[2,3,48,48]{3,2,1,0:T(8,128)(2,1)S(1)} %copy-done.1, f32[8,2304]{1,0:T(8,128)S(1)} %pair_forces.8.inner, f32[8,768]{1,0:T(8,128)S(1)} %pair_forces.9.outer, f32[6,16,1024]{2,1,0:T(8,128)S(1)} %get-tuple-element.36.refs_0_, ...), custom_call_target="tpu_custom_call" | custom-call | flops 10000000 | bytes 100000 | tf_op jit(solution)/shard_map/finish_block/pallas_call | solution.py:734
  60.3 2.7 %collective-permute-done.8.outer = f32[8,768]{1,0:T(8,128)S(1)} collective-permute-done((f32[8,768]{1,0:T(8,128)S(1)}, f32[8,768]{1,0:T(8,128)S(1)}, u32[]{:S(2)}, u32[]{:S(2)}) %collective-permute-start.8) | collective-permute-done | bytes 24608 | tf_op jit(solution)/shard_map/ppermute | solution.py:994
  63.0 0.0 collective-permute-done.5.inner
  63.0 0.0 collective-permute-done.10.refs_1_
  63.0 1.1 %finish_block.3 = (f32[3,16,4096]{2,1,0:T(8,128)}, f32[3,16,4096]{2,1,0:T(8,128)}) custom-call(s32[1]{0:T(128)} %bitcast.bead, bf16[2,3,48,48]{3,2,1,0:T(8,128)(2,1)S(1)} %copy-done.1, f32[8,2304]{1,0:T(8,128)S(1)} %collective-permute-done.5.inner, f32[8,768]{1,0:T(8,128)S(1)} %collective-permute-done.8.outer, ...), custom_call_target="tpu_custom_call", output_to_operand_aliasing={{0}: (6, {}), {1}: (7, {})} | custom-call | flops 10000000 | bytes 100000 | tf_op jit(solution)/shard_map/finish_block/pallas_call | solution.py:734
  (5 shorter events, 0.0 us)
Async XLA Ops:
  1.9 37.3 %collective-permute-start.4 = (f32[6,16,1024]{2,1,0:T(8,128)S(1)}, f32[6,16,1024]{2,1,0:T(8,128)S(1)}, u32[]{:S(2)}, u32[]{:S(2)}) collective-permute-start(f32[6,16,1024]{2,1,0:T(8,128)S(1)} %get-tuple-element.30), channel_id=1, source_target_pairs={{0,1},{1,0},{2,3},{3,2},{4,5},{5,4},{6,7},{7,6},{8,9},{9,8},{10,11... | collective-permute-start | bytes 1179656 | tf_op jit(solution)/shard_map/ppermute | solution.py:899
  6.0 24.9 %collective-permute-start.1 = (f32[4,16,1024]{2,1,0:T(8,128)S(1)}, f32[4,16,1024]{2,1,0:T(8,128)S(1)}, u32[]{:S(2)}, u32[]{:S(2)}) collective-permute-start(f32[4,16,1024]{2,1,0:T(8,128)S(1)} %fetch.5), channel_id=1, source_target_pairs={{0,1},{1,0},{2,3},{3,2},{4,5},{5,4},{6,7},{7,6},{8,9},{9,8},{10,11... | collective-permute-start | bytes 786440 | tf_op jit(solution)/shard_map/ppermute | solution.py:899
  7.9 15.2 %collective-permute-start.2 = (f32[8,3840]{1,0:T(8,128)S(1)}, f32[8,3840]{1,0:T(8,128)S(1)}, u32[]{:S(2)}, u32[]{:S(2)}) collective-permute-start(f32[8,3840]{1,0:T(8,128)S(1)} %get-tuple-element.25), channel_id=1, source_target_pairs={{0,1},{1,0},{2,3},{3,2},{4,5},{5,4},{6,7},{7,6},{8,9},{9,8},{10,11... | collective-permute-start | bytes 368648 | tf_op jit(solution)/shard_map/ppermute | solution.py:889
  10.9 19.9 %collective-permute-start = (f32[2,16,1024]{2,1,0:T(8,128)S(1)}, f32[2,16,1024]{2,1,0:T(8,128)S(1)}, u32[]{:S(2)}, u32[]{:S(2)}) collective-permute-start(f32[2,16,1024]{2,1,0:T(8,128)S(1)} %fetch.4), channel_id=1, source_target_pairs={{0,1},{1,0},{2,3},{3,2},{4,5},{5,4},{6,7},{7,6},{8,9},{9,8},{10,11... | collective-permute-start | bytes 393224 | tf_op jit(solution)/shard_map/ppermute | solution.py:887
  23.2 0.8 %copy-start.6 = (s32[2,4096]{1,0:T(2,128)S(1)}, s32[2,4096]{1,0:T(2,128)}, u32[]{:S(2)}) copy-start(s32[2,4096]{1,0:T(2,128)} %bonds.1) | copy-start | bytes 98308
  23.2 0.8 %copy-start.7 = (s32[3,2048]{1,0:T(4,128)S(1)}, s32[3,2048]{1,0:T(4,128)}, u32[]{:S(2)}) copy-start(s32[3,2048]{1,0:T(4,128)} %angles.1) | copy-start | bytes 73732
  23.2 5.9 %collective-permute-start.3 = (f32[16,256]{1,0:T(8,128)S(1)}, f32[16,256]{1,0:T(8,128)S(1)}, u32[]{:S(2)}, u32[]{:S(2)}) collective-permute-start(f32[16,256]{1,0:T(8,128)S(1)} %relay.1), channel_id=1, source_target_pairs={{0,2},{1,31},{2,4},{3,1},{4,6},{5,3},{6,8},{7,5},{8,10},{9,7},{10,... | collective-permute-start | bytes 49160 | tf_op jit(solution)/shard_map/ppermute | solution.py:903
  27.2 3.7 %copy-start = (bf16[2,288,48]{2,1,0:T(8,128)(2,1)S(1)}, bf16[2,288,48]{2,1,0:T(8,128)(2,1)}, u32[]{:S(2)}) copy-start(bf16[2,288,48]{2,1,0:T(8,128)(2,1)} %constant.21.clone.refs_10_.refs_8_) | copy-start | bytes 165892
  27.2 3.7 %copy-start.2 = (bf16[128,256]{1,0:T(8,128)(2,1)S(1)}, bf16[128,256]{1,0:T(8,128)(2,1)}, u32[]{:S(2)}) copy-start(bf16[128,256]{1,0:T(8,128)(2,1)} %constant.22.clone.refs_9_.refs_7_) | copy-start | bytes 196612
  27.2 3.7 %copy-start.4 = (bf16[2,32,192]{2,1,0:T(8,128)(2,1)S(1)}, bf16[2,32,192]{2,1,0:T(8,128)(2,1)}, u32[]{:S(2)}) copy-start(bf16[2,32,192]{2,1,0:T(8,128)(2,1)} %constant.20.clone.refs_11_.refs_9_) | copy-start | bytes 73732
  29.1 1.8 %copy-start.3 = (f32[4096]{0:T(1024)S(1)}, f32[4096]{0:T(1024)}, u32[]{:S(2)}) copy-start(f32[4096]{0:T(1024)} %param.15) | copy-start | bytes 49156
  29.1 1.8 %copy-start.5 = (f32[4096]{0:T(1024)S(1)}, f32[4096]{0:T(1024)}, u32[]{:S(2)}) copy-start(f32[4096]{0:T(1024)} %param.14) | copy-start | bytes 49156
  34.7 24.6 %collective-permute-start.9 = (f32[6,16,1024]{2,1,0:T(8,128)S(1)}, f32[6,16,1024]{2,1,0:T(8,128)S(1)}, u32[]{:S(2)}, u32[]{:S(2)}) collective-permute-start(f32[6,16,1024]{2,1,0:T(8,128)S(1)} %get-tuple-element.34), channel_id=1, source_target_pairs={{0,1},{1,0},{2,3},{3,2},{4,5},{5,4},{6,7},{7,6},{8,9},{9,8},{10,11... | collective-permute-start | bytes 1179656 | tf_op jit(solution)/shard_map/ppermute | solution.py:960
  43.0 20.1 %collective-permute-start.10 = (f32[6,16,1024]{2,1,0:T(8,128)S(1)}, f32[6,16,1024]{2,1,0:T(8,128)S(1)}, u32[]{:S(2)}, u32[]{:S(2)}) collective-permute-start(f32[6,16,1024]{2,1,0:T(8,128)S(1)} %get-tuple-element.35), channel_id=1, source_target_pairs={{0,1},{1,0},{2,3},{3,2},{4,5},{5,4},{6,7},{7,6},{8,9},{9,8},{10,11... | collective-permute-start | bytes 1179656 | tf_op jit(solution)/shard_map/ppermute | solution.py:960
  48.2 14.9 %collective-permute-start.5 = (f32[8,2304]{1,0:T(8,128)S(1)}, f32[8,2304]{1,0:T(8,128)S(1)}, u32[]{:S(2)}, u32[]{:S(2)}) collective-permute-start(f32[8,2304]{1,0:T(8,128)S(1)} %pair_forces.8.inner), channel_id=1, source_target_pairs={{0,1},{1,0},{2,3},{3,2},{4,5},{5,4},{6,7},{7,6},{8,9},{9,8},{10,11... | collective-permute-start | bytes 221192 | tf_op jit(solution)/shard_map/ppermute | solution.py:993
  49.7 6.0 %collective-permute-start.6 = (f32[16,256]{1,0:T(8,128)S(1)}, f32[16,256]{1,0:T(8,128)S(1)}, u32[]{:S(2)}, u32[]{:S(2)}) collective-permute-start(f32[16,256]{1,0:T(8,128)S(1)} %get-tuple-element.32), channel_id=1, source_target_pairs={{0,1},{1,0},{2,3},{3,2},{4,5},{5,4},{6,7},{7,6},{8,9},{9,8},{10,11... | collective-permute-start | bytes 49160 | tf_op jit(solution)/shard_map/ppermute | solution.py:974
  50.3 9.0 %copy-start.1 = (bf16[2,3,48,48]{3,2,1,0:T(8,128)(2,1)S(1)}, bf16[2,3,48,48]{3,2,1,0:T(8,128)(2,1)}, u32[]{:S(2)}) copy-start(bf16[2,3,48,48]{3,2,1,0:T(8,128)(2,1)} %constant.19.clone.expand) | copy-start | bytes 82948
  50.3 6.8 %collective-permute-start.7 = (f32[16,256]{1,0:T(8,128)S(1)}, f32[16,256]{1,0:T(8,128)S(1)}, u32[]{:S(2)}, u32[]{:S(2)}) collective-permute-start(f32[16,256]{1,0:T(8,128)S(1)} %get-tuple-element.33), channel_id=1, source_target_pairs={{0,31},{1,2},{2,1},{3,4},{4,3},{5,6},{6,5},{7,8},{8,7},{9,10},{10,... | collective-permute-start | bytes 49160 | tf_op jit(solution)/shard_map/ppermute | solution.py:975
  59.1 3.9 %collective-permute-start.8 = (f32[8,768]{1,0:T(8,128)S(1)}, f32[8,768]{1,0:T(8,128)S(1)}, u32[]{:S(2)}, u32[]{:S(2)}) collective-permute-start(f32[8,768]{1,0:T(8,128)S(1)} %pair_forces.9.outer), channel_id=1, source_target_pairs={{0,1},{1,0},{2,3},{3,2},{4,5},{5,4},{6,7},{7,6},{8,9},{9,8},{10,11... | collective-permute-start | bytes 73736 | tf_op jit(solution)/shard_map/ppermute | solution.py:994

commit v8 on v6

--- a/solution.py
+++ b/solution.py
@@ -541,13 +541,24 @@
 
 
 def step_kernel(parts, count, forces, chunk, chunks, group, edge, bead, *refs):
-    pieces = refs[:count]
+    pieces = list(refs[:count])
     at = count
     force = refs[at] if forces == 1 else whole_force(*refs[at : at + 2])
     at += forces
     mass_rows, strength_rows, hot, motion, expand, contract = refs[at : at + 6]
-    before = refs[at + 6] if edge and chunk else None
-    outs = refs[len(refs) - parts - 1 - 2 * edge :]
+    at += 6
+    before = refs[at] if edge and chunk else None
+    at += 1 if edge and chunk else 0
+    if parts > 1:
+        held, sem = refs[-2:]
+        start = pl.multiple_of((bead[0] * chunks + chunk) * (group * TILE), TILE)
+        own_momenta = pltpu.make_async_copy(
+            refs[at].at[:, :, pl.ds(start, group * TILE)], held, sem
+        )
+        own_momenta.start()
+        pieces.insert(1, held)
+        at += 1
+    outs = refs[at : at + parts + 1 + 2 * edge]
     c_out = outs[parts]
     interval = time_step / SUBS
     width = group * TILE
@@ -569,11 +580,6 @@
         return found[0] if parts == 1 else jnp.concatenate(found, axis=0)
 
     q = [gathered(0, c) for c in range(3)]
-    p = [gathered(1, c) for c in range(3)]
-    kick = exact(expand[bead[0]], force[:, first * TILE : first * TILE + width])
-    v = [
-        (p[c] + 0.5 * time_step * kick[c * BEADS : (c + 1) * BEADS]) * inverse for c in range(3)
-    ]
 
     def bonded(q):
         forces = []
@@ -605,8 +611,16 @@
             for c in range(3)
         ]
 
+    pushed = bonded(q)
+    if parts > 1:
+        own_momenta.wait()
+    p = [gathered(1, c) for c in range(3)]
+    kick = exact(expand[bead[0]], force[:, first * TILE : first * TILE + width])
+    v = [
+        (p[c] + 0.5 * time_step * kick[c * BEADS : (c + 1) * BEADS]) * inverse for c in range(3)
+    ]
     for sub in range(SUBS):
-        pushed = bonded(q)
+        pushed = bonded(q) if sub else pushed
         factor = (0.5 if sub == 0 else 1.0) * interval * inverse
         v = [v[c] + factor * pushed[c] for c in range(3)]
         for c in range(3):
@@ -633,10 +647,14 @@
         outs[-1][...] = jnp.where(bead[0] == 0, head, tail)
 
 
-def substeps(chunk, chunks, bead, pieces, force, mass, strength, hot, motion, expand, contract, edge, before):
+def substeps(chunk, chunks, bead, pieces, force, mass, strength, hot, motion, expand, contract, edge, before, mom):
     beads, lanes = pieces[0].shape[1:]
     parts = BEADS // beads
-    extra = [before] if edge and chunk else []
+    extra = [near(before)] if edge and chunk else []
+    scratch = []
+    if parts > 1:
+        extra.append(far(mom))
+        scratch = [pltpu.VMEM((3, beads, lanes), F32), pltpu.SemaphoreType.DMA]
     shapes = [(6, beads, lanes)] * parts + [(ROWS, lanes)]
     if edge:
         shapes += [(ROWS, GT * TILE)] * 2
@@ -644,7 +662,10 @@
         functools.partial(
             step_kernel, parts, len(pieces), len(force), chunk, chunks, lanes // TILE, int(edge)
         ),
-        in_specs=[IN_SMEM] + [IN_VMEM] * (len(pieces) + len(force) + 6 + len(extra)),
+        in_specs=[IN_SMEM]
+        + [IN_VMEM] * (len(pieces) + len(force) + 5 + len(extra) + (parts == 1))
+        + [pl.BlockSpec(memory_space=pl.ANY)] * (parts > 1),
+        scratch_shapes=scratch,
         out_specs=[IN_VMEM] * len(shapes),
         out_shape=[vmem_out(s, F32) for s in shapes],
         compiler_params=PARAMS,
@@ -659,7 +680,7 @@
         motion,
         expand,
         contract,
-        *[near(x) for x in extra],
+        *extra,
     )
 
 
@@ -863,12 +884,11 @@
         moves = []
         for chunk in range(1, chunks):
             moves += [(chunk - 1, 0, 0, 0, 3, 1, chunk), (chunk - 1, 3, 1, 0, 3, 1, chunk)]
-        moves += [(chunks - 1 + chunk, 0, 1, 0, 3, 0, chunk) for chunk in range(chunks)]
-        planes = [6] * (chunks - 1) + [3] * chunks
+        planes = [6] * (chunks - 1)
         blocks += fetch(moves, planes, chunks, bead_at, pos, mom)
         for chunk in range(chunks):
             moment = lax.ppermute(blocks[chunk], "bead", SWAP)
-            pieces[chunk] = [own_q[chunk], blocks[chunks + chunk]]
+            pieces[chunk] = [own_q[chunk]]
             pieces[chunk] += [moment] if chunk else [other, moment]
         straight = relay(straight, theirs)
         straight = lax.ppermute(
@@ -914,7 +934,7 @@
         last = pair and chunk == chunks - 1
         outs = substeps(
             chunk, chunks, bead_at, pieces[chunk], force, mass, strength, hot, motion,
-            expand_l, contract_l, last, contracted[0] if contracted else None,
+            expand_l, contract_l, last, contracted[0] if contracted else None, mom,
         )
         if last:
             *outs, bead_edge, far_edge = outs

time: 65.8 us -> 66.4 us (level)
  Pallas kernels: 28.7 us -> 30.3 us
  waiting for transfers between devices: 20.6 us -> 19.5 us
    pallas_call x2, Pallas kernels: 7.47 us -> 9.29 us  [substeps(): pl.pallas_call(functools.partial(step_kernel, parts, len(pieces), len(for...]
    ppermute x1, waiting for transfers between devices: 6.23 us -> 5.16 us  [body(): beside = lax.ppermute(bead_edge, 'bead', SWAP)]
  transfers between devices with their start and end apart: 11 -> 11, of which waited for: 3 -> 3; matrix products, arithmetic and copies ran while one was open for 0% -> 0% of each run, Pallas kernels for 40% -> 43%
where the time goes in v8:
time: 66.4 us; the launch traced here: 66 us
  Pallas kernels  30.3 us (46%)
  waiting for transfers between devices  19.5 us (29%)
  starting transfers between devices  14.5 us (22%)
  between operations  1.02 us (2%)
  local copies, waits for them, and re-layouts  0.73 us (1%)
    pallas_call x4, Pallas kernels, pair_forces(): pl.pallas_call(functools.partial(pair_kernel, spots, sizes, own_count, pa...  13.3 us
    ppermute x1, waiting for transfers between devices, body(): theirs = lax.ppermute(theirs, 'bead', SWAP)  12.2 us
    pallas_call x2, Pallas kernels, substeps(): pl.pallas_call(functools.partial(step_kernel, parts, len(pieces), len(for...  9.29 us
    ppermute x1, waiting for transfers between devices, body(): beside = lax.ppermute(bead_edge, 'bead', SWAP)  5.16 us
    ppermute x2, starting transfers between devices, body(): back.append(lax.ppermute(outs[d], 'bead', on))  3.46 us
    ppermute x2, starting transfers between devices, body(): moment = lax.ppermute(blocks[chunk], 'bead', SWAP)  3.15 us
    pallas_call x3, Pallas kernels, fetch(): pl.pallas_call(functools.partial(fetch_kernel, moves, chunks), in_specs=[...  2.93 us
    ppermute x1, starting transfers between devices, body(): lax.ppermute(far_edge, ('space', 'bead'), permutation(lambda b: 1 if b el...  2.9 us
  transfers between devices with their start and end apart: 11, of which 3 were waited for; matrix products, arithmetic and copies ran while one was open for 0% of the time, Pallas kernels for 43%

profile of v8, /device:TPU:0, one launch (start us, length us, event | category | flops | bytes accessed | tf_op | source)
XLA Modules:
  0.0 66.0 jit_solution(1238322413473429184)
XLA Ops:
  0.6 1.0 %fetch.5 = f32[6,16,1024]{2,1,0:T(8,128)S(1)} custom-call(s32[1]{0:T(128)} %bitcast.bead, f32[3,16,4096]{2,1,0:T(8,128)} %bitcast.18, f32[3,16,4096]{2,1,0:T(8,128)} %bitcast.13), custom_call_target="tpu_custom_call" | custom-call | flops 10000000 | bytes 100000 | tf_op jit(solution)/shard_map/fetch/pallas_call | solution.py:259
  1.7 3.1 %collective-permute-start.4 = (f32[6,16,1024]{2,1,0:T(8,128)S(1)}, f32[6,16,1024]{2,1,0:T(8,128)S(1)}, u32[]{:S(2)}, u32[]{:S(2)}) collective-permute-start(f32[6,16,1024]{2,1,0:T(8,128)S(1)} %fetch.5), channel_id=1, source_target_pairs={{0,1},{1,0},{2,3},{3,2},{4,5},{5,4},{6,7},{7,6},{8,9},{9,8},{10,11... | collective-permute-start | bytes 1179656 | tf_op jit(solution)/shard_map/ppermute | solution.py:890
  4.7 1.0 %fetch.4 = f32[4,16,1024]{2,1,0:T(8,128)S(1)} custom-call(s32[1]{0:T(128)} %bitcast.bead, f32[3,16,4096]{2,1,0:T(8,128)} %bitcast.19, f32[3,16,4096]{2,1,0:T(8,128)} %bitcast.14), custom_call_target="tpu_custom_call" | custom-call | flops 10000000 | bytes 100000 | tf_op jit(solution)/shard_map/fetch/pallas_call | solution.py:259
  5.7 0.1 collective-permute-start.1
  5.8 1.9 %begin.1 = (f32[16,2304]{1,0:T(8,128)S(1)}, f32[8,3840]{1,0:T(8,128)S(1)}, f32[16,256]{1,0:T(8,128)S(1)}, f32[3,16,1024]{2,1,0:T(8,128)S(1)}, f32[3,16,1024]{2,1,0:T(8,128)S(1)}) custom-call(s32[1]{0:T(128)} %bitcast.bead, bf16[2,48,144]{2,1,0:T(8,128)(2,1)} %constant.18.clone.left, f32[32,128]{1,0:T(8,128)} %bitcast.8, f32[3,16,4096]{2,1,0:T(8,128)} %bitcast.20), custom_call_target="tpu_custom_call" | custom-call | flops 10000000 | bytes 100000 | tf_op jit(solution)/shard_map/begin/pallas_call | solution.py:277
  7.7 2.1 %collective-permute-start.2 = (f32[8,3840]{1,0:T(8,128)S(1)}, f32[8,3840]{1,0:T(8,128)S(1)}, u32[]{:S(2)}, u32[]{:S(2)}) collective-permute-start(f32[8,3840]{1,0:T(8,128)S(1)} %get-tuple-element.21), channel_id=1, source_target_pairs={{0,1},{1,0},{2,3},{3,2},{4,5},{5,4},{6,7},{7,6},{8,9},{9,8},{10,11... | collective-permute-start | bytes 368648 | tf_op jit(solution)/shard_map/ppermute | solution.py:881
  9.8 0.9 %fetch.3 = f32[2,16,1024]{2,1,0:T(8,128)S(1)} custom-call(s32[1]{0:T(128)} %bitcast.bead, f32[3,16,4096]{2,1,0:T(8,128)} %bitcast.21, f32[3,16,4096]{2,1,0:T(8,128)} %bitcast.15), custom_call_target="tpu_custom_call" | custom-call | flops 10000000 | bytes 100000 | tf_op jit(solution)/shard_map/fetch/pallas_call | solution.py:259
  10.7 0.1 collective-permute-start
  10.8 12.2 %collective-permute-done.2.refs_1_.received.refs_3_.refs_5_ = f32[8,3840]{1,0:T(8,128)S(1)} collective-permute-done((f32[8,3840]{1,0:T(8,128)S(1)}, f32[8,3840]{1,0:T(8,128)S(1)}, u32[]{:S(2)}, u32[]{:S(2)}) %collective-permute-start.2) | collective-permute-done | bytes 122912 | tf_op jit(solution)/shard_map/ppermute | solution.py:881
  23.0 0.1 collective-permute-start.3
  23.0 0.7 %copy-done.6 = s32[2,4096]{1,0:T(2,128)S(1)} copy-done((s32[2,4096]{1,0:T(2,128)S(1)}, s32[2,4096]{1,0:T(2,128)}, u32[]{:S(2)}) %copy-start.6) | copy-done | bytes 32792
  23.7 0.0 copy-done.7
  23.7 0.7 %prepare.1.refs_7_.refs_6_ = bf16[16,128,256]{2,1,0:T(8,128)(2,1)S(1)} custom-call(s32[1]{0:T(128)} %bitcast.bead, s32[2,4096]{1,0:T(2,128)S(1)} %copy-done.6, s32[3,2048]{1,0:T(4,128)S(1)} %copy-done.7), custom_call_target="tpu_custom_call" | custom-call | flops 10000000 | bytes 100000 | tf_op jit(solution)/shard_map/prepare/pallas_call | solution.py:373
  24.4 4.4 %pair_forces.4.refs_3_.refs_2_ = f32[8,2304]{1,0:T(8,128)S(1)} custom-call(s32[1]{0:T(128)} %bitcast.bead, s32[1]{0:T(128)} %bitcast.1.space, s32[3,32]{1,0:T(4,128)} %nbr.7, f32[16,2304]{1,0:T(8,128)S(1)} %get-tuple-element.20.refs_0_.refs_2_.refs_4_, f32[8,3840]{1,0:T(8,128)S(1)} %collective-permute-done.2.refs_1_.received.refs_3_.refs_5_), custom_call_target="tpu_custom_call" | custom-call | flops 10000000 | bytes 100000 | tf_op jit(solution)/shard_map/pair_forces/pallas_call | solution.py:515
  28.9 0.0 copy-start
  28.9 0.0 copy-start.2
  28.9 0.0 copy-start.3
  28.9 0.0 copy-start.4
  28.9 0.0 copy-start.5
  28.9 0.0 collective-permute-done.3.refs_6_
  28.9 2.3 %pair_forces.5.refs_4_.refs_3_ = f32[8,768]{1,0:T(8,128)S(1)} custom-call(s32[1]{0:T(128)} %bitcast.bead, s32[1]{0:T(128)} %bitcast.1.space, s32[3,32]{1,0:T(4,128)} %nbr.7, f32[16,2304]{1,0:T(8,128)S(1)} %get-tuple-element.20.refs_0_.refs_2_.refs_4_, f32[8,3840]{1,0:T(8,128)S(1)} %collective-permute-done.2.refs_1_.received.refs_3_.refs_5_, ...), custom_call_target="tpu_custom_call" | custom-call | flops 10000000 | bytes 100000 | tf_op jit(solution)/shard_map/pair_forces/pallas_call | solution.py:515
  31.2 0.0 collective-permute-done.refs_1_
  31.2 0.0 collective-permute-done.1.refs_2_
  31.2 0.0 copy-done
  31.2 0.0 copy-done.2
  31.2 0.0 copy-done.3
  31.2 0.0 copy-done.4
  31.3 0.0 copy-done.5
  31.3 4.5 %substeps.2 = (f32[6,16,1024]{2,1,0:T(8,128)S(1)}, f32[6,16,1024]{2,1,0:T(8,128)S(1)}, f32[16,1024]{1,0:T(8,128)S(1)}) custom-call(s32[1]{0:T(128)} %bitcast.bead, f32[3,16,1024]{2,1,0:T(8,128)S(1)} %get-tuple-element.19.refs_0_, f32[2,16,1024]{2,1,0:T(8,128)S(1)} %collective-permute-done.refs_1_, f32[4,16,1024]{2,1,0:T(8,128)S(1)} %collective-permute-done.1.refs_2_, ...), custom_call_target="tpu_custom_call" | custom-call | flops 10000000 | bytes 100000 | tf_op jit(solution)/shard_map/substeps/pallas_call | solution.py:661
  35.8 3.4 %collective-permute-start.9 = (f32[6,16,1024]{2,1,0:T(8,128)S(1)}, f32[6,16,1024]{2,1,0:T(8,128)S(1)}, u32[]{:S(2)}, u32[]{:S(2)}) collective-permute-start(f32[6,16,1024]{2,1,0:T(8,128)S(1)} %get-tuple-element.28), channel_id=1, source_target_pairs={{0,1},{1,0},{2,3},{3,2},{4,5},{5,4},{6,7},{7,6},{8,9},{9,8},{10,11... | collective-permute-start | bytes 1179656 | tf_op jit(solution)/shard_map/ppermute | solution.py:949
  39.2 0.0 collective-permute-done.4.refs_1_
  39.2 4.8 %substeps.3 = (f32[6,16,1024]{2,1,0:T(8,128)S(1)}, f32[6,16,1024]{2,1,0:T(8,128)S(1)}, f32[16,1024]{1,0:T(8,128)S(1)}, f32[16,256]{1,0:T(8,128)S(1)}, f32[16,256]{1,0:T(8,128)S(1)}) custom-call(s32[1]{0:T(128)} %bitcast.bead, f32[3,16,1024]{2,1,0:T(8,128)S(1)} %get-tuple-element.24.refs_0_, f32[6,16,1024]{2,1,0:T(8,128)S(1)} %collective-permute-done.4.refs_1_, ...), custom_call_target="tpu_custom_call" | custom-call | flops 10000000 | bytes 100000 | tf_op jit(solution)/shard_map/substeps/pallas_call | solution.py:661
  43.9 0.1 collective-permute-start.10
  44.0 4.5 %pair_forces.6.inner = f32[8,2304]{1,0:T(8,128)S(1)} custom-call(s32[1]{0:T(128)} %bitcast.bead, s32[1]{0:T(128)} %bitcast.1.space, s32[3,32]{1,0:T(4,128)} %nbr.7, f32[16,1024]{1,0:T(8,128)S(1)} %get-tuple-element.23.refs_10_.refs_0_, f32[16,1024]{1,0:T(8,128)S(1)} %get-tuple-element.25.refs_1_), custom_call_target="tpu_custom_call" | custom-call | flops 10000000 | bytes 100000 | tf_op jit(solution)/shard_map/pair_forces/pallas_call | solution.py:515
  48.6 2.1 %collective-permute-start.5 = (f32[8,2304]{1,0:T(8,128)S(1)}, f32[8,2304]{1,0:T(8,128)S(1)}, u32[]{:S(2)}, u32[]{:S(2)}) collective-permute-start(f32[8,2304]{1,0:T(8,128)S(1)} %pair_forces.6.inner), channel_id=1, source_target_pairs={{0,1},{1,0},{2,3},{3,2},{4,5},{5,4},{6,7},{7,6},{8,9},{9,8},{10,11... | collective-permute-start | bytes 221192 | tf_op jit(solution)/shard_map/ppermute | solution.py:983
  50.7 0.1 collective-permute-start.6
  50.7 2.9 %collective-permute-start.7 = (f32[16,256]{1,0:T(8,128)S(1)}, f32[16,256]{1,0:T(8,128)S(1)}, u32[]{:S(2)}, u32[]{:S(2)}) collective-permute-start(f32[16,256]{1,0:T(8,128)S(1)} %get-tuple-element.27), channel_id=1, source_target_pairs={{0,31},{1,2},{2,1},{3,4},{4,3},{5,6},{6,5},{7,8},{8,7},{9,10},{10,... | collective-permute-start | bytes 49160 | tf_op jit(solution)/shard_map/ppermute | solution.py:964
  53.6 5.2 %collective-permute-done.6.refs_2_ = f32[16,256]{1,0:T(8,128)S(1)} collective-permute-done((f32[16,256]{1,0:T(8,128)S(1)}, f32[16,256]{1,0:T(8,128)S(1)}, u32[]{:S(2)}, u32[]{:S(2)}) %collective-permute-start.6) | collective-permute-done | bytes 16416 | tf_op jit(solution)/shard_map/ppermute | solution.py:963
  58.8 0.0 collective-permute-done.7.refs_3_
  58.8 2.1 %pair_forces.7.outer = f32[8,768]{1,0:T(8,128)S(1)} custom-call(s32[1]{0:T(128)} %bitcast.bead, s32[1]{0:T(128)} %bitcast.1.space, s32[3,32]{1,0:T(4,128)} %nbr.7, f32[16,1024]{1,0:T(8,128)S(1)} %get-tuple-element.23.refs_10_.refs_0_, f32[16,1024]{1,0:T(8,128)S(1)} %get-tuple-element.25.refs_1_, f32[16,256]{1,0:T(8,128)S(1)} %collective-permute-done.6.refs_2_, ...), custom_call_target="tpu_custom_call" | custom-call | flops 10000000 | bytes 100000 | tf_op jit(solution)/shard_map/pair_forces/pallas_call | solution.py:515
  60.9 0.6 collective-permute-start.8
  61.6 0.0 collective-permute-done.9.refs_2_.refs_0_
  61.6 0.0 copy-done.1
  61.6 1.1 %finish_block.2 = (f32[3,16,4096]{2,1,0:T(8,128)}, f32[3,16,4096]{2,1,0:T(8,128)}) custom-call(s32[1]{0:T(128)} %bitcast.bead, bf16[2,3,48,48]{3,2,1,0:T(8,128)(2,1)S(1)} %copy-done.1, f32[8,2304]{1,0:T(8,128)S(1)} %pair_forces.6.inner, f32[8,768]{1,0:T(8,128)S(1)} %pair_forces.7.outer, f32[6,16,1024]{2,1,0:T(8,128)S(1)} %get-tuple-element.30.refs_0_, ...), custom_call_target="tpu_custom_call" | custom-call | flops 10000000 | bytes 100000 | tf_op jit(solution)/shard_map/finish_block/pallas_call | solution.py:751
  62.7 2.2 %collective-permute-done.8.outer = f32[8,768]{1,0:T(8,128)S(1)} collective-permute-done((f32[8,768]{1,0:T(8,128)S(1)}, f32[8,768]{1,0:T(8,128)S(1)}, u32[]{:S(2)}, u32[]{:S(2)}) %collective-permute-start.8) | collective-permute-done | bytes 24608 | tf_op jit(solution)/shard_map/ppermute | solution.py:984
  64.8 0.0 collective-permute-done.5.inner
  64.8 0.0 collective-permute-done.10.refs_1_
  64.8 1.1 %finish_block.3 = (f32[3,16,4096]{2,1,0:T(8,128)}, f32[3,16,4096]{2,1,0:T(8,128)}) custom-call(s32[1]{0:T(128)} %bitcast.bead, bf16[2,3,48,48]{3,2,1,0:T(8,128)(2,1)S(1)} %copy-done.1, f32[8,2304]{1,0:T(8,128)S(1)} %collective-permute-done.5.inner, f32[8,768]{1,0:T(8,128)S(1)} %collective-permute-done.8.outer, ...), custom_call_target="tpu_custom_call", output_to_operand_aliasing={{0}: (6, {}), {1}: (7, {})} | custom-call | flops 10000000 | bytes 100000 | tf_op jit(solution)/shard_map/finish_block/pallas_call | solution.py:751
  (4 shorter events, 0.0 us)
Async XLA Ops:
  1.7 37.5 %collective-permute-start.4 = (f32[6,16,1024]{2,1,0:T(8,128)S(1)}, f32[6,16,1024]{2,1,0:T(8,128)S(1)}, u32[]{:S(2)}, u32[]{:S(2)}) collective-permute-start(f32[6,16,1024]{2,1,0:T(8,128)S(1)} %fetch.5), channel_id=1, source_target_pairs={{0,1},{1,0},{2,3},{3,2},{4,5},{5,4},{6,7},{7,6},{8,9},{9,8},{10,11... | collective-permute-start | bytes 1179656 | tf_op jit(solution)/shard_map/ppermute | solution.py:890
  5.7 25.5 %collective-permute-start.1 = (f32[4,16,1024]{2,1,0:T(8,128)S(1)}, f32[4,16,1024]{2,1,0:T(8,128)S(1)}, u32[]{:S(2)}, u32[]{:S(2)}) collective-permute-start(f32[4,16,1024]{2,1,0:T(8,128)S(1)} %fetch.4), channel_id=1, source_target_pairs={{0,1},{1,0},{2,3},{3,2},{4,5},{5,4},{6,7},{7,6},{8,9},{9,8},{10,11... | collective-permute-start | bytes 786440 | tf_op jit(solution)/shard_map/ppermute | solution.py:890
  7.7 15.2 %collective-permute-start.2 = (f32[8,3840]{1,0:T(8,128)S(1)}, f32[8,3840]{1,0:T(8,128)S(1)}, u32[]{:S(2)}, u32[]{:S(2)}) collective-permute-start(f32[8,3840]{1,0:T(8,128)S(1)} %get-tuple-element.21), channel_id=1, source_target_pairs={{0,1},{1,0},{2,3},{3,2},{4,5},{5,4},{6,7},{7,6},{8,9},{9,8},{10,11... | collective-permute-start | bytes 368648 | tf_op jit(solution)/shard_map/ppermute | solution.py:881
  10.7 20.5 %collective-permute-start = (f32[2,16,1024]{2,1,0:T(8,128)S(1)}, f32[2,16,1024]{2,1,0:T(8,128)S(1)}, u32[]{:S(2)}, u32[]{:S(2)}) collective-permute-start(f32[2,16,1024]{2,1,0:T(8,128)S(1)} %fetch.3), channel_id=1, source_target_pairs={{0,1},{1,0},{2,3},{3,2},{4,5},{5,4},{6,7},{7,6},{8,9},{9,8},{10,11... | collective-permute-start | bytes 393224 | tf_op jit(solution)/shard_map/ppermute | solution.py:879
  23.0 0.8 %copy-start.6 = (s32[2,4096]{1,0:T(2,128)S(1)}, s32[2,4096]{1,0:T(2,128)}, u32[]{:S(2)}) copy-start(s32[2,4096]{1,0:T(2,128)} %bonds.1) | copy-start | bytes 98308
  23.0 0.8 %copy-start.7 = (s32[3,2048]{1,0:T(4,128)S(1)}, s32[3,2048]{1,0:T(4,128)}, u32[]{:S(2)}) copy-start(s32[3,2048]{1,0:T(4,128)} %angles.1) | copy-start | bytes 73732
  23.0 5.9 %collective-permute-start.3 = (f32[16,256]{1,0:T(8,128)S(1)}, f32[16,256]{1,0:T(8,128)S(1)}, u32[]{:S(2)}, u32[]{:S(2)}) collective-permute-start(f32[16,256]{1,0:T(8,128)S(1)} %relay.1), channel_id=1, source_target_pairs={{0,2},{1,31},{2,4},{3,1},{4,6},{5,3},{6,8},{7,5},{8,10},{9,7},{10,... | collective-permute-start | bytes 49160 | tf_op jit(solution)/shard_map/ppermute | solution.py:894
  28.9 2.4 %copy-start = (bf16[2,288,48]{2,1,0:T(8,128)(2,1)S(1)}, bf16[2,288,48]{2,1,0:T(8,128)(2,1)}, u32[]{:S(2)}) copy-start(bf16[2,288,48]{2,1,0:T(8,128)(2,1)} %constant.21.clone.refs_9_.refs_8_) | copy-start | bytes 165892
  28.9 2.4 %copy-start.2 = (bf16[128,256]{1,0:T(8,128)(2,1)S(1)}, bf16[128,256]{1,0:T(8,128)(2,1)}, u32[]{:S(2)}) copy-start(bf16[128,256]{1,0:T(8,128)(2,1)} %constant.22.clone.refs_8_.refs_7_) | copy-start | bytes 196612
  28.9 2.4 %copy-start.3 = (f32[4096]{0:T(1024)S(1)}, f32[4096]{0:T(1024)}, u32[]{:S(2)}) copy-start(f32[4096]{0:T(1024)} %param.15) | copy-start | bytes 49156
  28.9 2.4 %copy-start.4 = (bf16[2,32,192]{2,1,0:T(8,128)(2,1)S(1)}, bf16[2,32,192]{2,1,0:T(8,128)(2,1)}, u32[]{:S(2)}) copy-start(bf16[2,32,192]{2,1,0:T(8,128)(2,1)} %constant.20.clone.refs_10_.refs_9_) | copy-start | bytes 73732
  28.9 2.4 %copy-start.5 = (f32[4096]{0:T(1024)S(1)}, f32[4096]{0:T(1024)}, u32[]{:S(2)}) copy-start(f32[4096]{0:T(1024)} %param.14) | copy-start | bytes 49156
  35.8 25.8 %collective-permute-start.9 = (f32[6,16,1024]{2,1,0:T(8,128)S(1)}, f32[6,16,1024]{2,1,0:T(8,128)S(1)}, u32[]{:S(2)}, u32[]{:S(2)}) collective-permute-start(f32[6,16,1024]{2,1,0:T(8,128)S(1)} %get-tuple-element.28), channel_id=1, source_target_pairs={{0,1},{1,0},{2,3},{3,2},{4,5},{5,4},{6,7},{7,6},{8,9},{9,8},{10,11... | collective-permute-start | bytes 1179656 | tf_op jit(solution)/shard_map/ppermute | solution.py:949
  43.9 20.9 %collective-permute-start.10 = (f32[6,16,1024]{2,1,0:T(8,128)S(1)}, f32[6,16,1024]{2,1,0:T(8,128)S(1)}, u32[]{:S(2)}, u32[]{:S(2)}) collective-permute-start(f32[6,16,1024]{2,1,0:T(8,128)S(1)} %get-tuple-element.29), channel_id=1, source_target_pairs={{0,1},{1,0},{2,3},{3,2},{4,5},{5,4},{6,7},{7,6},{8,9},{9,8},{10,11... | collective-permute-start | bytes 1179656 | tf_op jit(solution)/shard_map/ppermute | solution.py:949
  48.6 16.2 %collective-permute-start.5 = (f32[8,2304]{1,0:T(8,128)S(1)}, f32[8,2304]{1,0:T(8,128)S(1)}, u32[]{:S(2)}, u32[]{:S(2)}) collective-permute-start(f32[8,2304]{1,0:T(8,128)S(1)} %pair_forces.6.inner), channel_id=1, source_target_pairs={{0,1},{1,0},{2,3},{3,2},{4,5},{5,4},{6,7},{7,6},{8,9},{9,8},{10,11... | collective-permute-start | bytes 221192 | tf_op jit(solution)/shard_map/ppermute | solution.py:983
  50.7 8.1 %collective-permute-start.6 = (f32[16,256]{1,0:T(8,128)S(1)}, f32[16,256]{1,0:T(8,128)S(1)}, u32[]{:S(2)}, u32[]{:S(2)}) collective-permute-start(f32[16,256]{1,0:T(8,128)S(1)} %get-tuple-element.26), channel_id=1, source_target_pairs={{0,1},{1,0},{2,3},{3,2},{4,5},{5,4},{6,7},{7,6},{8,9},{9,8},{10,11... | collective-permute-start | bytes 49160 | tf_op jit(solution)/shard_map/ppermute | solution.py:963
  50.7 10.8 %copy-start.1 = (bf16[2,3,48,48]{3,2,1,0:T(8,128)(2,1)S(1)}, bf16[2,3,48,48]{3,2,1,0:T(8,128)(2,1)}, u32[]{:S(2)}) copy-start(bf16[2,3,48,48]{3,2,1,0:T(8,128)(2,1)} %constant.19.clone.expand) | copy-start | bytes 82948
  50.7 8.1 %collective-permute-start.7 = (f32[16,256]{1,0:T(8,128)S(1)}, f32[16,256]{1,0:T(8,128)S(1)}, u32[]{:S(2)}, u32[]{:S(2)}) collective-permute-start(f32[16,256]{1,0:T(8,128)S(1)} %get-tuple-element.27), channel_id=1, source_target_pairs={{0,31},{1,2},{2,1},{3,4},{4,3},{5,6},{6,5},{7,8},{8,7},{9,10},{10,... | collective-permute-start | bytes 49160 | tf_op jit(solution)/shard_map/ppermute | solution.py:964
  60.9 3.9 %collective-permute-start.8 = (f32[8,768]{1,0:T(8,128)S(1)}, f32[8,768]{1,0:T(8,128)S(1)}, u32[]{:S(2)}, u32[]{:S(2)}) collective-permute-start(f32[8,768]{1,0:T(8,128)S(1)} %pair_forces.7.outer), channel_id=1, source_target_pairs={{0,1},{1,0},{2,3},{3,2},{4,5},{5,4},{6,7},{7,6},{8,9},{9,8},{10,11... | collective-permute-start | bytes 73736 | tf_op jit(solution)/shard_map/ppermute | solution.py:984

commit v9 on v6

--- a/solution.py
+++ b/solution.py
@@ -196,18 +196,18 @@
     for i in range(2 * chunks):
         owner = bead[0] if i < chunks else 1 - bead[0]
         starts.append(pl.multiple_of((owner * chunks + i % chunks) * lanes, TILE))
+    small = [
+        pltpu.make_async_copy(left.at[bead[0]], table, sems.at[2 * chunks]),
+        pltpu.make_async_copy(strengths, rows, sems.at[2 * chunks + 1]),
+    ]
+    for copy in small:
+        copy.start()
     for i, block in enumerate(blocks):
         copy = pltpu.make_async_copy(
             pos.at[:, :, pl.ds(starts[i], lanes)], block, sems.at[i]
         )
         copy.start()
         copies.append(copy)
-    small = [
-        pltpu.make_async_copy(left.at[bead[0]], table, sems.at[len(copies)]),
-        pltpu.make_async_copy(strengths, rows, sems.at[len(copies) + 1]),
-    ]
-    for copy in small:
-        copy.start()
     for copy in small:
         copy.wait()
     logs = math.log2(math.e) * jnp.log(rows[...])
@@ -854,12 +854,10 @@
 
     pieces = [[] for _ in range(chunks)]
     if pair:
-        (lead,) = fetch([(0, 0, 0, 0, 2, 1, 0)], [2], chunks, bead_at, pos, mom)
-        other = lax.ppermute(lead, "bead", SWAP)
         mine, theirs, straight, *own_q = begin(chunks, bead_at, begin_left, strength, pos)
         theirs = lax.ppermute(theirs, "bead", SWAP)
-        moves = [(0, 0, 0, 2, 1, 1, 0), (0, 1, 1, 0, 3, 1, 0)]
-        blocks = fetch(moves, [4], chunks, bead_at, pos, mom)
+        moves = [(0, 0, 0, 0, 3, 1, 0), (0, 3, 1, 0, 3, 1, 0)]
+        blocks = fetch(moves, [6], chunks, bead_at, pos, mom)
         moves = []
         for chunk in range(1, chunks):
             moves += [(chunk - 1, 0, 0, 0, 3, 1, chunk), (chunk - 1, 3, 1, 0, 3, 1, chunk)]
@@ -868,8 +866,7 @@
         blocks += fetch(moves, planes, chunks, bead_at, pos, mom)
         for chunk in range(chunks):
             moment = lax.ppermute(blocks[chunk], "bead", SWAP)
-            pieces[chunk] = [own_q[chunk], blocks[chunks + chunk]]
-            pieces[chunk] += [moment] if chunk else [other, moment]
+            pieces[chunk] = [own_q[chunk], blocks[chunks + chunk], moment]
         straight = relay(straight, theirs)
         straight = lax.ppermute(
             straight, ("space", "bead"), permutation(lambda b: -1 if b else 1, 0)

time: 65.8 us -> 67.2 us (1.021)
  waiting for transfers between devices: 20.6 us -> 23.4 us
  Pallas kernels: 28.7 us -> 27.7 us
    ppermute x1, waiting for transfers between devices: 12.2 us -> 15 us  [body(): theirs = lax.ppermute(theirs, 'bead', SWAP)]
    ppermute x1, starting transfers between devices: 2.93 us -> 1.8 us  [body(): lax.ppermute(far_edge, ('space', 'bead'), permutation(lambda b: 1 if b el...]
    pallas_call x3 -> x2, Pallas kernels: 3.15 us -> 2.29 us  [fetch(): pl.pallas_call(functools.partial(fetch_kernel, moves, chunks), in_specs=[...]
    ppermute x2, starting transfers between devices: 3.38 us -> 4.23 us  [body(): back.append(lax.ppermute(outs[d], 'bead', on))]
  transfers between devices with their start and end apart: 11 -> 10, of which waited for: 3 -> 3; matrix products, arithmetic and copies ran while one was open for 0% -> 0% of each run, Pallas kernels for 40% -> 38%
where the time goes in v9:
time: 67.2 us; the launch traced here: 66.9 us
  Pallas kernels  27.7 us (41%)
  waiting for transfers between devices  23.4 us (35%)
  starting transfers between devices  14.1 us (21%)
  between operations  0.99 us (1%)
  local copies, waits for them, and re-layouts  0.73 us (1%)
    ppermute x1, waiting for transfers between devices, body(): theirs = lax.ppermute(theirs, 'bead', SWAP)  15 us
    pallas_call x4, Pallas kernels, pair_forces(): pl.pallas_call(functools.partial(pair_kernel, spots, sizes, own_count, pa...  13.3 us
    pallas_call x2, Pallas kernels, substeps(): pl.pallas_call(functools.partial(step_kernel, parts, len(pieces), len(for...  7.46 us
    ppermute x1, waiting for transfers between devices, body(): beside = lax.ppermute(bead_edge, 'bead', SWAP)  6.24 us
    ppermute x2, starting transfers between devices, body(): back.append(lax.ppermute(outs[d], 'bead', on))  4.23 us
    ppermute x2, starting transfers between devices, body(): moment = lax.ppermute(blocks[chunk], 'bead', SWAP)  3.15 us
    pallas_call x2, Pallas kernels, fetch(): pl.pallas_call(functools.partial(fetch_kernel, moves, chunks), in_specs=[...  2.29 us
    ppermute x1, waiting for transfers between devices, body(): outer = lax.ppermute(outer, 'bead', SWAP)  2.15 us
  transfers between devices with their start and end apart: 10, of which 3 were waited for; matrix products, arithmetic and copies ran while one was open for 0% of the time, Pallas kernels for 38%

profile of v9, /device:TPU:0, one launch (start us, length us, event | category | flops | bytes accessed | tf_op | source)
XLA Modules:
  0.0 66.9 jit_solution(3661419247076857830)
XLA Ops:
  0.6 1.0 %fetch.3 = f32[6,16,1024]{2,1,0:T(8,128)S(1)} custom-call(s32[1]{0:T(128)} %bitcast.bead, f32[3,16,4096]{2,1,0:T(8,128)} %bitcast.13, f32[3,16,4096]{2,1,0:T(8,128)} %bitcast.16), custom_call_target="tpu_custom_call" | custom-call | flops 10000000 | bytes 100000 | tf_op jit(solution)/shard_map/fetch/pallas_call | solution.py:259
  1.7 3.1 %collective-permute-start = (f32[6,16,1024]{2,1,0:T(8,128)S(1)}, f32[6,16,1024]{2,1,0:T(8,128)S(1)}, u32[]{:S(2)}, u32[]{:S(2)}) collective-permute-start(f32[6,16,1024]{2,1,0:T(8,128)S(1)} %fetch.3), channel_id=1, source_target_pairs={{0,1},{1,0},{2,3},{3,2},{4,5},{5,4},{6,7},{7,6},{8,9},{9,8},{10,11... | collective-permute-start | bytes 1179656 | tf_op jit(solution)/shard_map/ppermute | solution.py:868
  4.7 1.3 %fetch.2 = (f32[6,16,1024]{2,1,0:T(8,128)S(1)}, f32[3,16,1024]{2,1,0:T(8,128)S(1)}, f32[3,16,1024]{2,1,0:T(8,128)S(1)}) custom-call(s32[1]{0:T(128)} %bitcast.bead, f32[3,16,4096]{2,1,0:T(8,128)} %bitcast.14, f32[3,16,4096]{2,1,0:T(8,128)} %bitcast.17), custom_call_target="tpu_custom_call" | custom-call | flops 10000000 | bytes 100000 | tf_op jit(solution)/shard_map/fetch/pallas_call | solution.py:259
  6.0 0.1 collective-permute-start.3
  6.1 1.8 %begin.1 = (f32[16,2304]{1,0:T(8,128)S(1)}, f32[8,3840]{1,0:T(8,128)S(1)}, f32[16,256]{1,0:T(8,128)S(1)}, f32[3,16,1024]{2,1,0:T(8,128)S(1)}, f32[3,16,1024]{2,1,0:T(8,128)S(1)}) custom-call(s32[1]{0:T(128)} %bitcast.bead, bf16[2,48,144]{2,1,0:T(8,128)(2,1)} %constant.18.clone.left, f32[32,128]{1,0:T(8,128)} %bitcast.8, f32[3,16,4096]{2,1,0:T(8,128)} %bitcast.15), custom_call_target="tpu_custom_call" | custom-call | flops 10000000 | bytes 100000 | tf_op jit(solution)/shard_map/begin/pallas_call | solution.py:277
  7.9 2.1 %collective-permute-start.1 = (f32[8,3840]{1,0:T(8,128)S(1)}, f32[8,3840]{1,0:T(8,128)S(1)}, u32[]{:S(2)}, u32[]{:S(2)}) collective-permute-start(f32[8,3840]{1,0:T(8,128)S(1)} %get-tuple-element.25), channel_id=1, source_target_pairs={{0,1},{1,0},{2,3},{3,2},{4,5},{5,4},{6,7},{7,6},{8,9},{9,8},{10,11... | collective-permute-start | bytes 368648 | tf_op jit(solution)/shard_map/ppermute | solution.py:858
  9.9 15.0 %collective-permute-done.1.refs_1_.received.refs_3_.refs_5_ = f32[8,3840]{1,0:T(8,128)S(1)} collective-permute-done((f32[8,3840]{1,0:T(8,128)S(1)}, f32[8,3840]{1,0:T(8,128)S(1)}, u32[]{:S(2)}, u32[]{:S(2)}) %collective-permute-start.1) | collective-permute-done | bytes 122912 | tf_op jit(solution)/shard_map/ppermute | solution.py:858
  24.9 0.0 copy-start.6
  24.9 0.0 copy-start.7
  24.9 0.1 collective-permute-start.2
  25.0 0.7 %copy-done.6 = s32[2,4096]{1,0:T(2,128)S(1)} copy-done((s32[2,4096]{1,0:T(2,128)S(1)}, s32[2,4096]{1,0:T(2,128)}, u32[]{:S(2)}) %copy-start.6) | copy-done | bytes 32792
  25.7 0.0 copy-done.7
  25.7 0.7 prepare.1.refs_7_
  26.4 4.4 %pair_forces.4.refs_3_ = f32[8,2304]{1,0:T(8,128)S(1)} custom-call(s32[1]{0:T(128)} %bitcast.bead, s32[1]{0:T(128)} %bitcast.1.space, s32[3,32]{1,0:T(4,128)} %nbr.7, f32[16,2304]{1,0:T(8,128)S(1)} %get-tuple-element.24.refs_0_.refs_2_.refs_4_, f32[8,3840]{1,0:T(8,128)S(1)} %collective-permute-done.1.refs_1_.received.refs_3_.refs_5_), custom_call_target="tpu_custom_call" | custom-call | flops 10000000 | bytes 100000 | tf_op jit(solution)/shard_map/pair_forces/pallas_call | solution.py:515
  30.8 0.0 copy-start
  30.8 0.0 copy-start.2
  30.8 0.0 copy-start.4
  30.9 0.0 collective-permute-done.2.refs_6_
  30.9 0.0 copy-start.3
  30.9 0.0 copy-start.5
  30.9 2.3 %pair_forces.5.refs_4_ = f32[8,768]{1,0:T(8,128)S(1)} custom-call(s32[1]{0:T(128)} %bitcast.bead, s32[1]{0:T(128)} %bitcast.1.space, s32[3,32]{1,0:T(4,128)} %nbr.7, f32[16,2304]{1,0:T(8,128)S(1)} %get-tuple-element.24.refs_0_.refs_2_.refs_4_, f32[8,3840]{1,0:T(8,128)S(1)} %collective-permute-done.1.refs_1_.received.refs_3_.refs_5_, ...), custom_call_target="tpu_custom_call" | custom-call | flops 10000000 | bytes 100000 | tf_op jit(solution)/shard_map/pair_forces/pallas_call | solution.py:515
  33.2 0.0 collective-permute-done.refs_2_
  33.2 0.0 copy-done
  33.2 0.0 copy-done.2
  33.2 0.0 copy-done.4
  33.2 0.0 copy-done.3
  33.2 0.0 copy-done.5
  33.2 3.7 %substeps.2 = (f32[6,16,1024]{2,1,0:T(8,128)S(1)}, f32[6,16,1024]{2,1,0:T(8,128)S(1)}, f32[16,1024]{1,0:T(8,128)S(1)}) custom-call(s32[1]{0:T(128)} %bitcast.bead, f32[3,16,1024]{2,1,0:T(8,128)S(1)} %get-tuple-element.22.refs_0_, f32[3,16,1024]{2,1,0:T(8,128)S(1)} %get-tuple-element.23.refs_1_, f32[6,16,1024]{2,1,0:T(8,128)S(1)} %collective-permute-done.refs_2_, ...), custom_call_target="tpu_custom_call" | custom-call | flops 10000000 | bytes 100000 | tf_op jit(solution)/shard_map/substeps/pallas_call | solution.py:643
  36.9 4.2 %collective-permute-start.8 = (f32[6,16,1024]{2,1,0:T(8,128)S(1)}, f32[6,16,1024]{2,1,0:T(8,128)S(1)}, u32[]{:S(2)}, u32[]{:S(2)}) collective-permute-start(f32[6,16,1024]{2,1,0:T(8,128)S(1)} %get-tuple-element.34), channel_id=1, source_target_pairs={{0,1},{1,0},{2,3},{3,2},{4,5},{5,4},{6,7},{7,6},{8,9},{9,8},{10,11... | collective-permute-start | bytes 1179656 | tf_op jit(solution)/shard_map/ppermute | solution.py:926
  41.1 0.0 collective-permute-done.3.refs_2_
  41.1 3.7 %substeps.3 = (f32[6,16,1024]{2,1,0:T(8,128)S(1)}, f32[6,16,1024]{2,1,0:T(8,128)S(1)}, f32[16,1024]{1,0:T(8,128)S(1)}, f32[16,256]{1,0:T(8,128)S(1)}, f32[16,256]{1,0:T(8,128)S(1)}) custom-call(s32[1]{0:T(128)} %bitcast.bead, f32[3,16,1024]{2,1,0:T(8,128)S(1)} %get-tuple-element.28.refs_0_, f32[3,16,1024]{2,1,0:T(8,128)S(1)} %get-tuple-element.29.refs_1_, ...), custom_call_target="tpu_custom_call" | custom-call | flops 10000000 | bytes 100000 | tf_op jit(solution)/shard_map/substeps/pallas_call | solution.py:643
  44.8 0.1 collective-permute-start.9
  44.9 4.5 %pair_forces.6.inner = f32[8,2304]{1,0:T(8,128)S(1)} custom-call(s32[1]{0:T(128)} %bitcast.bead, s32[1]{0:T(128)} %bitcast.1.space, s32[3,32]{1,0:T(4,128)} %nbr.7, f32[16,1024]{1,0:T(8,128)S(1)} %get-tuple-element.27.refs_11_.refs_0_, f32[16,1024]{1,0:T(8,128)S(1)} %get-tuple-element.31.refs_1_), custom_call_target="tpu_custom_call" | custom-call | flops 10000000 | bytes 100000 | tf_op jit(solution)/shard_map/pair_forces/pallas_call | solution.py:515
  49.5 2.1 %collective-permute-start.4 = (f32[8,2304]{1,0:T(8,128)S(1)}, f32[8,2304]{1,0:T(8,128)S(1)}, u32[]{:S(2)}, u32[]{:S(2)}) collective-permute-start(f32[8,2304]{1,0:T(8,128)S(1)} %pair_forces.6.inner), channel_id=1, source_target_pairs={{0,1},{1,0},{2,3},{3,2},{4,5},{5,4},{6,7},{7,6},{8,9},{9,8},{10,11... | collective-permute-start | bytes 221192 | tf_op jit(solution)/shard_map/ppermute | solution.py:960
  51.5 0.1 collective-permute-start.5
  51.6 0.0 copy-start.1
  51.6 1.8 %collective-permute-start.6 = (f32[16,256]{1,0:T(8,128)S(1)}, f32[16,256]{1,0:T(8,128)S(1)}, u32[]{:S(2)}, u32[]{:S(2)}) collective-permute-start(f32[16,256]{1,0:T(8,128)S(1)} %get-tuple-element.33), channel_id=1, source_target_pairs={{0,31},{1,2},{2,1},{3,4},{4,3},{5,6},{6,5},{7,8},{8,7},{9,10},{10,... | collective-permute-start | bytes 49160 | tf_op jit(solution)/shard_map/ppermute | solution.py:941
  53.4 6.2 %collective-permute-done.5.refs_2_ = f32[16,256]{1,0:T(8,128)S(1)} collective-permute-done((f32[16,256]{1,0:T(8,128)S(1)}, f32[16,256]{1,0:T(8,128)S(1)}, u32[]{:S(2)}, u32[]{:S(2)}) %collective-permute-start.5) | collective-permute-done | bytes 16416 | tf_op jit(solution)/shard_map/ppermute | solution.py:940
  59.7 0.0 collective-permute-done.6.refs_3_
  59.7 2.1 %pair_forces.7.outer = f32[8,768]{1,0:T(8,128)S(1)} custom-call(s32[1]{0:T(128)} %bitcast.bead, s32[1]{0:T(128)} %bitcast.1.space, s32[3,32]{1,0:T(4,128)} %nbr.7, f32[16,1024]{1,0:T(8,128)S(1)} %get-tuple-element.27.refs_11_.refs_0_, f32[16,1024]{1,0:T(8,128)S(1)} %get-tuple-element.31.refs_1_, f32[16,256]{1,0:T(8,128)S(1)} %collective-permute-done.5.refs_2_, ...), custom_call_target="tpu_custom_call" | custom-call | flops 10000000 | bytes 100000 | tf_op jit(solution)/shard_map/pair_forces/pallas_call | solution.py:515
  61.8 0.7 collective-permute-start.7
  62.4 0.0 collective-permute-done.8.refs_2_.refs_0_
  62.4 0.0 copy-done.1
  62.4 1.1 %finish_block.2 = (f32[3,16,4096]{2,1,0:T(8,128)}, f32[3,16,4096]{2,1,0:T(8,128)}) custom-call(s32[1]{0:T(128)} %bitcast.bead, bf16[2,3,48,48]{3,2,1,0:T(8,128)(2,1)S(1)} %copy-done.1, f32[8,2304]{1,0:T(8,128)S(1)} %pair_forces.6.inner, f32[8,768]{1,0:T(8,128)S(1)} %pair_forces.7.outer, f32[6,16,1024]{2,1,0:T(8,128)S(1)} %get-tuple-element.36.refs_0_, ...), custom_call_target="tpu_custom_call" | custom-call | flops 10000000 | bytes 100000 | tf_op jit(solution)/shard_map/finish_block/pallas_call | solution.py:730
  63.5 2.1 %collective-permute-done.7.outer = f32[8,768]{1,0:T(8,128)S(1)} collective-permute-done((f32[8,768]{1,0:T(8,128)S(1)}, f32[8,768]{1,0:T(8,128)S(1)}, u32[]{:S(2)}, u32[]{:S(2)}) %collective-permute-start.7) | collective-permute-done | bytes 24608 | tf_op jit(solution)/shard_map/ppermute | solution.py:961
  65.7 0.0 collective-permute-done.4.inner
  65.7 0.0 collective-permute-done.9.refs_1_
  65.7 1.1 %finish_block.3 = (f32[3,16,4096]{2,1,0:T(8,128)}, f32[3,16,4096]{2,1,0:T(8,128)}) custom-call(s32[1]{0:T(128)} %bitcast.bead, bf16[2,3,48,48]{3,2,1,0:T(8,128)(2,1)S(1)} %copy-done.1, f32[8,2304]{1,0:T(8,128)S(1)} %collective-permute-done.4.inner, f32[8,768]{1,0:T(8,128)S(1)} %collective-permute-done.7.outer, ...), custom_call_target="tpu_custom_call", output_to_operand_aliasing={{0}: (6, {}), {1}: (7, {})} | custom-call | flops 10000000 | bytes 100000 | tf_op jit(solution)/shard_map/finish_block/pallas_call | solution.py:730
  (1 shorter events, 0.0 us)
Async XLA Ops:
  1.7 31.5 %collective-permute-start = (f32[6,16,1024]{2,1,0:T(8,128)S(1)}, f32[6,16,1024]{2,1,0:T(8,128)S(1)}, u32[]{:S(2)}, u32[]{:S(2)}) collective-permute-start(f32[6,16,1024]{2,1,0:T(8,128)S(1)} %fetch.3), channel_id=1, source_target_pairs={{0,1},{1,0},{2,3},{3,2},{4,5},{5,4},{6,7},{7,6},{8,9},{9,8},{10,11... | collective-permute-start | bytes 1179656 | tf_op jit(solution)/shard_map/ppermute | solution.py:868
  6.0 35.1 %collective-permute-start.3 = (f32[6,16,1024]{2,1,0:T(8,128)S(1)}, f32[6,16,1024]{2,1,0:T(8,128)S(1)}, u32[]{:S(2)}, u32[]{:S(2)}) collective-permute-start(f32[6,16,1024]{2,1,0:T(8,128)S(1)} %get-tuple-element.30), channel_id=1, source_target_pairs={{0,1},{1,0},{2,3},{3,2},{4,5},{5,4},{6,7},{7,6},{8,9},{9,8},{10,11... | collective-permute-start | bytes 1179656 | tf_op jit(solution)/shard_map/ppermute | solution.py:868
  7.9 17.1 %collective-permute-start.1 = (f32[8,3840]{1,0:T(8,128)S(1)}, f32[8,3840]{1,0:T(8,128)S(1)}, u32[]{:S(2)}, u32[]{:S(2)}) collective-permute-start(f32[8,3840]{1,0:T(8,128)S(1)} %get-tuple-element.25), channel_id=1, source_target_pairs={{0,1},{1,0},{2,3},{3,2},{4,5},{5,4},{6,7},{7,6},{8,9},{9,8},{10,11... | collective-permute-start | bytes 368648 | tf_op jit(solution)/shard_map/ppermute | solution.py:858
  24.9 0.8 %copy-start.6 = (s32[2,4096]{1,0:T(2,128)S(1)}, s32[2,4096]{1,0:T(2,128)}, u32[]{:S(2)}) copy-start(s32[2,4096]{1,0:T(2,128)} %bonds.1) | copy-start | bytes 98308
  24.9 0.8 %copy-start.7 = (s32[3,2048]{1,0:T(4,128)S(1)}, s32[3,2048]{1,0:T(4,128)}, u32[]{:S(2)}) copy-start(s32[3,2048]{1,0:T(4,128)} %angles.1) | copy-start | bytes 73732
  24.9 5.9 %collective-permute-start.2 = (f32[16,256]{1,0:T(8,128)S(1)}, f32[16,256]{1,0:T(8,128)S(1)}, u32[]{:S(2)}, u32[]{:S(2)}) collective-permute-start(f32[16,256]{1,0:T(8,128)S(1)} %relay.1), channel_id=1, source_target_pairs={{0,2},{1,31},{2,4},{3,1},{4,6},{5,3},{6,8},{7,5},{8,10},{9,7},{10,... | collective-permute-start | bytes 49160 | tf_op jit(solution)/shard_map/ppermute | solution.py:871
  30.8 2.4 %copy-start = (bf16[2,288,48]{2,1,0:T(8,128)(2,1)S(1)}, bf16[2,288,48]{2,1,0:T(8,128)(2,1)}, u32[]{:S(2)}) copy-start(bf16[2,288,48]{2,1,0:T(8,128)(2,1)} %constant.21.clone.refs_9_) | copy-start | bytes 165892
  30.8 2.4 %copy-start.2 = (bf16[128,256]{1,0:T(8,128)(2,1)S(1)}, bf16[128,256]{1,0:T(8,128)(2,1)}, u32[]{:S(2)}) copy-start(bf16[128,256]{1,0:T(8,128)(2,1)} %constant.22.clone.refs_8_) | copy-start | bytes 196612
  30.8 2.4 %copy-start.4 = (bf16[2,32,192]{2,1,0:T(8,128)(2,1)S(1)}, bf16[2,32,192]{2,1,0:T(8,128)(2,1)}, u32[]{:S(2)}) copy-start(bf16[2,32,192]{2,1,0:T(8,128)(2,1)} %constant.20.clone.refs_10_) | copy-start | bytes 73732
  30.9 2.3 %copy-start.3 = (f32[4096]{0:T(1024)S(1)}, f32[4096]{0:T(1024)}, u32[]{:S(2)}) copy-start(f32[4096]{0:T(1024)} %param.15) | copy-start | bytes 49156
  30.9 2.3 %copy-start.5 = (f32[4096]{0:T(1024)S(1)}, f32[4096]{0:T(1024)}, u32[]{:S(2)}) copy-start(f32[4096]{0:T(1024)} %param.14) | copy-start | bytes 49156
  36.9 25.5 %collective-permute-start.8 = (f32[6,16,1024]{2,1,0:T(8,128)S(1)}, f32[6,16,1024]{2,1,0:T(8,128)S(1)}, u32[]{:S(2)}, u32[]{:S(2)}) collective-permute-start(f32[6,16,1024]{2,1,0:T(8,128)S(1)} %get-tuple-element.34), channel_id=1, source_target_pairs={{0,1},{1,0},{2,3},{3,2},{4,5},{5,4},{6,7},{7,6},{8,9},{9,8},{10,11... | collective-permute-start | bytes 1179656 | tf_op jit(solution)/shard_map/ppermute | solution.py:926
  44.8 20.8 %collective-permute-start.9 = (f32[6,16,1024]{2,1,0:T(8,128)S(1)}, f32[6,16,1024]{2,1,0:T(8,128)S(1)}, u32[]{:S(2)}, u32[]{:S(2)}) collective-permute-start(f32[6,16,1024]{2,1,0:T(8,128)S(1)} %get-tuple-element.35), channel_id=1, source_target_pairs={{0,1},{1,0},{2,3},{3,2},{4,5},{5,4},{6,7},{7,6},{8,9},{9,8},{10,11... | collective-permute-start | bytes 1179656 | tf_op jit(solution)/shard_map/ppermute | solution.py:926
  49.5 16.2 %collective-permute-start.4 = (f32[8,2304]{1,0:T(8,128)S(1)}, f32[8,2304]{1,0:T(8,128)S(1)}, u32[]{:S(2)}, u32[]{:S(2)}) collective-permute-start(f32[8,2304]{1,0:T(8,128)S(1)} %pair_forces.6.inner), channel_id=1, source_target_pairs={{0,1},{1,0},{2,3},{3,2},{4,5},{5,4},{6,7},{7,6},{8,9},{9,8},{10,11... | collective-permute-start | bytes 221192 | tf_op jit(solution)/shard_map/ppermute | solution.py:960
  51.5 8.1 %collective-permute-start.5 = (f32[16,256]{1,0:T(8,128)S(1)}, f32[16,256]{1,0:T(8,128)S(1)}, u32[]{:S(2)}, u32[]{:S(2)}) collective-permute-start(f32[16,256]{1,0:T(8,128)S(1)} %get-tuple-element.32), channel_id=1, source_target_pairs={{0,1},{1,0},{2,3},{3,2},{4,5},{5,4},{6,7},{7,6},{8,9},{9,8},{10,11... | collective-permute-start | bytes 49160 | tf_op jit(solution)/shard_map/ppermute | solution.py:940
  51.6 10.8 %copy-start.1 = (bf16[2,3,48,48]{3,2,1,0:T(8,128)(2,1)S(1)}, bf16[2,3,48,48]{3,2,1,0:T(8,128)(2,1)}, u32[]{:S(2)}) copy-start(bf16[2,3,48,48]{3,2,1,0:T(8,128)(2,1)} %constant.19.clone.expand) | copy-start | bytes 82948
  51.6 8.0 %collective-permute-start.6 = (f32[16,256]{1,0:T(8,128)S(1)}, f32[16,256]{1,0:T(8,128)S(1)}, u32[]{:S(2)}, u32[]{:S(2)}) collective-permute-start(f32[16,256]{1,0:T(8,128)S(1)} %get-tuple-element.33), channel_id=1, source_target_pairs={{0,31},{1,2},{2,1},{3,4},{4,3},{5,6},{6,5},{7,8},{8,7},{9,10},{10,... | collective-permute-start | bytes 49160 | tf_op jit(solution)/shard_map/ppermute | solution.py:941
  61.8 3.9 %collective-permute-start.7 = (f32[8,768]{1,0:T(8,128)S(1)}, f32[8,768]{1,0:T(8,128)S(1)}, u32[]{:S(2)}, u32[]{:S(2)}) collective-permute-start(f32[8,768]{1,0:T(8,128)S(1)} %pair_forces.7.outer), channel_id=1, source_target_pairs={{0,1},{1,0},{2,3},{3,2},{4,5},{5,4},{6,7},{7,6},{8,9},{9,8},{10,11... | collective-permute-start | bytes 73736 | tf_op jit(solution)/shard_map/ppermute | solution.py:961
